TPU v7x, 512 devices: a whole 4x4x16 slice. The times are simulated.
512 devices in a mesh: pop: 8 (over z_hi, x), blk: 64 (over z_lo, y, core).
Axes of the slice: x: 4, y: 4, z: 16 (z_hi: 2, z_lo: 8; z = z_hi * 8 + z_lo), core: 2. Of those that a mesh axis runs over, the one named last changes fastest.
Arguments:
- v_init: float32 [512, 2, 16384], P('pop', None, 'blk'), may hold values from -6 to 6
- a_init: float32 [512, 2, 16384], P('pop', None, 'blk'), may hold values from 0 to 1
- z_init: bfloat16 [512, 2, 16384], P('pop', None, 'blk'), may hold values from 0 to 1
- base_weight: bfloat16 [16384, 16384], P('blk', 'pop'), may hold values from -0.046875 to 0.046875
- factor_u: bfloat16 [512, 4, 16384], P('pop', None, 'blk'), may hold values from -6 to 6
- factor_v: bfloat16 [512, 4, 16384], P('pop', None, 'blk'), may hold values from -0.046875 to 0.046875
- in_weight: bfloat16 [700, 16384], P(None, 'blk'), may hold values from -0.21875 to 0.21875
- spikes_in: int32 [2, 2, 700], replicated, may hold values 0 or 1
- step_count: int32 [512, 2], P('pop'), may hold values from 1 to 2, as said below
- member_ids: int32 [512], P('pop'), may hold values from 0 to 511, each once
- decay_mem: float32 [16384], P('blk'), may hold values from 0.3 to 0.9
- decay_adapt: float32 [16384], P('blk'), may hold values from 0.5 to 0.95
- thr_base: float32 [16384], P('blk'), may hold values from 0.2 to 1
- thr_adapt: float32 [16384], P('blk'), may hold values from 0.5 to 2
Outputs:
- v_out: float32 [512, 2, 16384], P('pop', None, 'blk')
- a_out: float32 [512, 2, 16384], P('pop', None, 'blk')
Inputs may be any that keep to these rules, and one draw needn't show every extreme that they name: `member_ids`: each member appears in exactly one slot. `step_count`: a trial's state stops changing after its last step.
All inputs are finite; a program needn't handle non-finite values.
Results may differ from a plain program's by a relative error of at most 0.00088.
Values may be sent and summed in bfloat16 or wider, within the bound.
No kernel may reach another device: no remote copies, remote signals or barrier semaphores. Data moves between devices by JAX's collectives and lax.ppermute only.
A program may use at most 64 MiB of HBM per device.

v0:
```python
import functools

import jax
import jax.numpy as jnp
import numpy as np
from jax import lax
from jax.experimental import pallas as pl
from jax.experimental.pallas import tpu as pltpu
from jax.sharding import Mesh
from jax.sharding import PartitionSpec as P

STEPS = 2
AXES = ("zh", "x", "a", "b", "y", "c")
SIZES = (2, 4, 2, 4, 4, 2)
POP = ("zh", "x")
BLK = ("a", "b", "y", "c")
EXT = 8


def permute(value, dest):
    pairs = []
    for source in np.ndindex(*SIZES):
        there = dest(*source)
        pairs.append(
            (int(np.ravel_multi_index(source, SIZES)), int(np.ravel_multi_index(there, SIZES)))
        )
    return lax.ppermute(value, AXES, pairs)


def to_owner(value):
    return permute(value, lambda zh, x, a, b, y, c: (a, x, zh, b, y, c))


def over_a(value):
    return permute(value, lambda zh, x, a, b, y, c: (zh, x, 1 - a, b, y, c))


def over_b(value, k):
    return permute(value, lambda zh, x, a, b, y, c: (zh, x, a, b ^ k, y, c))


def over_y(value, k):
    return permute(value, lambda zh, x, a, b, y, c: (zh, x, a, b, y ^ k, c))


def over_c(value):
    return permute(value, lambda zh, x, a, b, y, c: (zh, x, a, b, y, 1 - c))


def over_x(value, k):
    return permute(value, lambda zh, x, a, b, y, c: (zh, x ^ k, a, b, y, c))


def over_zh(value):
    return permute(value, lambda zh, x, a, b, y, c: (1 - zh, x, a, b, y, c))


def member_mask(rows, cols, trials, rank):
    row = lax.broadcasted_iota(jnp.int32, (rows, cols), 0) // trials
    col = lax.broadcasted_iota(jnp.int32, (rows, cols), 1) // rank
    return row == col


def pack(spike_rows, factor_rows, trials, rank):
    rows, block = spike_rows.shape
    full = lax.dot_general(
        spike_rows, factor_rows, (((1,), (1,)), ((), ())), preferred_element_type=jnp.float32
    )
    kept = jnp.where(member_mask(rows, full.shape[1], trials, rank), full, 0.0)
    part = kept.reshape(rows // trials, trials, full.shape[1]).sum(0)
    high = lax.reduce_precision(part, 8, 7)
    rest = part - high
    middle = lax.reduce_precision(rest, 8, 7)
    last = rest - middle
    terms = [t.astype(jnp.bfloat16) for t in (high, middle, last)]
    pad = jnp.zeros((EXT - 3 * trials, block), jnp.bfloat16)
    return jnp.concatenate([spike_rows, *terms, pad], axis=0)


def mix_kernel(at_ref, *refs, rows, trials, late):
    spikes, weights = refs[:4], refs[4:8]
    mine_ref, theirs_ref = refs[-2:]
    flip, shift, y = at_ref[0], at_ref[1], at_ref[2]
    tall, block = spikes[0].shape[1:]
    extra = None
    for q in range(4):
        tail = spikes[q][:2, rows:, :].astype(jnp.float32)
        tail = tail + spikes[q][2:, rows:, :].astype(jnp.float32)
        extra = tail if extra is None else extra + tail
    part = extra[:, :trials] + extra[:, trials : 2 * trials] + extra[:, 2 * trials : 3 * trials]

    def run(low):
        total = None
        for q in range(4):
            for high in range(2):
                first = ((shift >> 1) ^ high) * 2
                chunk = spikes[q][pl.ds(first, 2)]
                piece = jnp.dot(
                    chunk.reshape(2 * tall, block),
                    weights[2 * high + low][y ^ q],
                    preferred_element_type=jnp.float32,
                )
                total = piece if total is None else total + piece
        for s in range(2):
            for half, ref in enumerate((mine_ref, theirs_ref)):
                value = total[s * tall : (s + 1) * tall, half * block : (half + 1) * block]
                other = part[s]
                if late:
                    before = refs[8 + half]
                    value = value + before[s ^ flip]
                    other = other + before[s ^ flip, rows : rows + trials, :]
                ref[s ^ flip] = value
                ref[s ^ flip, rows : rows + trials, :] = other

    for low in range(2):
        pl.when(((shift & 1) ^ int(late)) == low)(functools.partial(run, low))


def mix(at, spikes, weights, rows, trials, before=()):
    blocks, tall, block = spikes[0].shape
    out = jax.ShapeDtypeStruct((2, tall, block), jnp.float32)
    whole = pl.BlockSpec(memory_space=pltpu.VMEM)
    inputs = len(spikes) * spikes[0].size + 2 * weights[0].size
    return pl.pallas_call(
        functools.partial(mix_kernel, rows=rows, trials=trials, late=len(before) > 0),
        out_shape=(out, out),
        in_specs=[pl.BlockSpec(memory_space=pltpu.SMEM)] + [whole] * (8 + len(before)),
        out_specs=(whole, whole),
        cost_estimate=pl.CostEstimate(
            flops=4 * blocks * tall * weights[0].size // 2,
            bytes_accessed=2 * inputs + 16 * tall * block,
            transcendentals=0,
        ),
        name="mix_late" if before else "mix_early",
    )(at, *spikes, *weights, *before)


def fold_kernel(mine_ref, theirs_ref, keep_ref, give_ref, *, rows, trials):
    keep_ref[...] = mine_ref[0] + theirs_ref[0]
    give = mine_ref[1] + theirs_ref[1]
    tail = give[rows : rows + trials]
    high = tail.astype(jnp.bfloat16).astype(jnp.float32)
    rest = tail - high
    middle = rest.astype(jnp.bfloat16).astype(jnp.float32)
    pad = jnp.zeros((EXT - 3 * trials, tail.shape[1]), jnp.float32)
    sent = jnp.concatenate([give[:rows], high, middle, rest - middle, pad], axis=0)
    give_ref[...] = sent.astype(jnp.bfloat16)


def fold(mine, theirs, rows, trials):
    shape = mine.shape[1:]
    whole = pl.BlockSpec(memory_space=pltpu.VMEM)
    return pl.pallas_call(
        functools.partial(fold_kernel, rows=rows, trials=trials),
        out_shape=(
            jax.ShapeDtypeStruct(shape, jnp.float32),
            jax.ShapeDtypeStruct(shape, jnp.bfloat16),
        ),
        in_specs=[whole, whole],
        out_specs=(whole, whole),
        name="fold",
    )(mine, theirs)


def spread_weights(base_weight, at):
    outs, depth = base_weight.shape
    block = depth // 8
    split = base_weight.reshape(outs, 4, 2, block)
    one = at["c"] == 1
    keep = jnp.where(one, split[:, :, 1], split[:, :, 0]).transpose(1, 2, 0)
    give = jnp.where(one, split[:, :, 0], split[:, :, 1]).transpose(1, 2, 0)
    own = jnp.concatenate([keep, over_c(give)], axis=2)
    chunks = [own]
    for k in (1, 2, 3):
        chunks.append(over_x(own, k))
    return chunks


def body(
    v_init,
    a_init,
    z_init,
    base_weight,
    factor_u,
    factor_v,
    in_weight,
    spikes_in,
    step_count,
    member_ids,
    decay_mem,
    decay_adapt,
    thr_base,
    thr_adapt,
):
    members, trials, block = v_init.shape
    rank = factor_u.shape[1]
    rows = members * trials
    at = {name: lax.axis_index(name) for name in AXES}
    sign = (1 - 2 * (member_ids % 2)).astype(jnp.float32)
    u_rows = factor_u.reshape(members * rank, block)
    v_rows = factor_v.reshape(members * rank, block)
    place = jnp.stack([at["a"] ^ at["zh"], at["b"] ^ at["x"], at["y"]])
    weights = spread_weights(base_weight, at)
    state_v, state_a, spikes = (v_init, a_init, z_init)
    for step in range(STEPS):
        spikes_f = spikes.astype(jnp.float32)
        held = pack(spikes.reshape(rows, block), v_rows, trials, rank)
        held = to_owner(held)[None]
        other = over_a(held)
        held = jnp.concatenate([held, other], axis=0)
        other = over_b(held, 2)
        early = [jnp.concatenate([held, other], axis=0)]
        late = [over_b(early[0], 1)]
        for pieces in (early, late):
            for k in (1, 2, 3):
                pieces.append(over_y(pieces[0], k))
        halves = mix(place, early, weights, rows, trials)
        mine, theirs = mix(place, late, weights, rows, trials, halves)
        theirs = over_c(theirs)
        keep, give = fold(mine, theirs, rows, trials)
        came = over_zh(give).astype(jnp.float32)
        total = keep[:rows] + came[:rows]
        proj = keep[rows : rows + trials]
        for term in range(3):
            proj = proj + came[rows + term * trials : rows + (term + 1) * trials]
        proj = proj.astype(jnp.bfloat16)
        mask = member_mask(rows, members * rank, trials, rank)
        spread = jnp.broadcast_to(proj[None], (members, trials, members * rank))
        spread = jnp.where(mask, spread.reshape(rows, members * rank), 0).astype(jnp.bfloat16)
        low = lax.dot_general(
            spread, u_rows, (((1,), (0,)), ((), ())), preferred_element_type=jnp.float32
        ).reshape(members, trials, block)
        dense = total.reshape(members, trials, block)
        current = jnp.dot(
            spikes_in[step].astype(jnp.bfloat16), in_weight, preferred_element_type=jnp.float32
        )
        drive = dense + 0.5 * sign[:, None, None] * low + current[None]
        v_new = (
            decay_mem * state_v
            + (1.0 - decay_mem) * drive
            - spikes_f * (thr_base + thr_adapt * state_a)
        )
        a_new = decay_adapt * state_a + (1.0 - decay_adapt) * spikes_f
        active = (step_count > step)[:, :, None]
        state_v = jnp.where(active, v_new, state_v)
        state_a = jnp.where(active, a_new, state_a)
        if step + 1 < STEPS:
            spikes = jax.nn.sigmoid(3.0 * (state_v - thr_base - thr_adapt * state_a)).astype(
                jnp.bfloat16
            )
    return (state_v, state_a)


def solution(mesh):
    fine = Mesh(mesh.devices.reshape(SIZES), AXES)
    in_specs = (
        P(POP, None, BLK),
        P(POP, None, BLK),
        P(POP, None, BLK),
        P(BLK, POP),
        P(POP, None, BLK),
        P(POP, None, BLK),
        P(None, BLK),
        P(),
        P(POP, None),
        P(POP),
        P(BLK),
        P(BLK),
        P(BLK),
        P(BLK),
    )
    out_specs = (P(POP, None, BLK), P(POP, None, BLK))
    return jax.shard_map(body, mesh=fine, in_specs=in_specs, out_specs=out_specs, check_vma=False)
```

profile of v0, /device:TPU:1, one launch (start us, length us, event | category | flops | bytes accessed | tf_op | source)
XLA Modules:
  0.0 235.8 jit_solution(154815252997747173)
XLA Ops:
  0.6 1.5 copy.28
  2.3 8.7 %collective-permute-start.7 = (bf16[4,256,256]{2,1,0:T(8,128)(2,1)S(1)}, bf16[4,256,256]{2,1,0:T(8,128)(2,1)S(1)}, u32[]{:S(2)}, u32[]{:S(2)}) collective-permute-start(bf16[4,256,256]{2,1,0:T(8,128)(2,1)S(1)} %get-tuple-element.33), channel_id=1, source_target_pairs={{0,1},{1,0},{2,3},{3,2},{4,5},{5,4},{6,7},{7,6},{8,9},{9,8},{10,11... | collective-permute-start | bytes 1572872 | tf_op jit(solution)/shard_map/ppermute | solution.py:27
  12.9 18.6 %collective-permute-start.1 = (bf16[1,136,256]{2,1,0:T(8,128)(2,1)S(1)}, bf16[1,136,256]{2,1,0:T(8,128)(2,1)S(1)}, u32[]{:S(2)}, u32[]{:S(2)}) collective-permute-start(bf16[1,136,256]{2,1,0:T(8,128)(2,1)S(1)} %bitcast.41), channel_id=1, source_target_pairs={{0,32},{1,33},{2,34},{3,35},{4,36},{5,37},{6,38},{7,39},{8,40},{9,... | collective-permute-start | bytes 208904 | tf_op jit(solution)/shard_map/ppermute | solution.py:27
  31.7 4.4 %collective-permute-start.10 = (bf16[4,256,512]{2,1,0:T(8,128)(2,1)S(1)}, bf16[4,256,512]{2,1,0:T(8,128)(2,1)S(1)}, u32[]{:S(2)}, u32[]{:S(2)}) collective-permute-start(bf16[4,256,512]{2,1,0:T(8,128)(2,1)S(1)} %pad_maximum_fusion.refs_4_), channel_id=1, source_target_pairs={{0,192},{1,193},{2,194},{3,195},{4,196},{5,197},{6,198},{7,199},{8... | collective-permute-start | bytes 3145736 | tf_op jit(solution)/shard_map/ppermute | solution.py:27
  36.1 0.9 collective-permute-done.1
  37.0 1.9 collective-permute-start.2
  38.9 7.8 %collective-permute-done.2 = bf16[2,136,256]{2,1,0:T(8,128)(2,1)S(1)} collective-permute-done((bf16[2,136,256]{2,1,0:T(8,128)(2,1)S(1)}, bf16[2,136,256]{2,1,0:T(8,128)(2,1)S(1)}, u32[]{:S(2)}, u32[]{:S(2)}) %collective-permute-start.2) | collective-permute-done | bytes 139296 | tf_op jit(solution)/shard_map/ppermute | solution.py:27
  47.5 3.2 %collective-permute-start.11 = (bf16[4,136,256]{2,1,0:T(8,128)(2,1)}, bf16[4,136,256]{2,1,0:T(8,128)(2,1)}, u32[]{:S(2)}, u32[]{:S(2)}) collective-permute-start(bf16[4,136,256]{2,1,0:T(8,128)(2,1)} %pad_maximum_fusion.1.refs_0_), channel_id=1, source_target_pairs={{0,2},{1,3},{2,0},{3,1},{4,6},{5,7},{6,4},{7,5},{8,10},{9,11},{10,... | collective-permute-start | bytes 835592 | tf_op jit(solution)/shard_map/ppermute | solution.py:27
  50.7 4.5 %collective-permute-start.12 = (bf16[4,136,256]{2,1,0:T(8,128)(2,1)}, bf16[4,136,256]{2,1,0:T(8,128)(2,1)}, u32[]{:S(2)}, u32[]{:S(2)}) collective-permute-start(bf16[4,136,256]{2,1,0:T(8,128)(2,1)} %pad_maximum_fusion.1.refs_0_), channel_id=1, source_target_pairs={{0,4},{1,5},{2,6},{3,7},{4,0},{5,1},{6,2},{7,3},{8,12},{9,13},{10,... | collective-permute-start | bytes 835592 | tf_op jit(solution)/shard_map/ppermute | solution.py:27
  55.2 3.0 %collective-permute-start.8 = (bf16[4,256,512]{2,1,0:T(8,128)(2,1)S(1)}, bf16[4,256,512]{2,1,0:T(8,128)(2,1)S(1)}, u32[]{:S(2)}, u32[]{:S(2)}) collective-permute-start(bf16[4,256,512]{2,1,0:T(8,128)(2,1)S(1)} %pad_maximum_fusion.refs_4_), channel_id=1, source_target_pairs={{0,64},{1,65},{2,66},{3,67},{4,68},{5,69},{6,70},{7,71},{8,72},{9,... | collective-permute-start | bytes 3145736 | tf_op jit(solution)/shard_map/ppermute | solution.py:27
  58.2 4.3 %collective-permute-start.9 = (bf16[4,256,512]{2,1,0:T(8,128)(2,1)S(1)}, bf16[4,256,512]{2,1,0:T(8,128)(2,1)}, u32[]{:S(2)}, u32[]{:S(2)}) collective-permute-start(bf16[4,256,512]{2,1,0:T(8,128)(2,1)S(1)} %pad_maximum_fusion.refs_4_), channel_id=1, source_target_pairs={{0,128},{1,129},{2,130},{3,131},{4,132},{5,133},{6,134},{7,135},{8... | collective-permute-start | bytes 3145736 | tf_op jit(solution)/shard_map/ppermute | solution.py:27
  62.6 1.9 collective-permute-start.13
  64.5 1.3 collective-permute-done.12.refs_2_
  65.8 1.9 collective-permute-start.3
  67.8 7.1 %collective-permute-done.3.refs_0_ = bf16[4,136,256]{2,1,0:T(8,128)(2,1)} collective-permute-done((bf16[4,136,256]{2,1,0:T(8,128)(2,1)}, bf16[4,136,256]{2,1,0:T(8,128)(2,1)}, u32[]{:S(2)}, u32[]{:S(2)}) %collective-permute-start.3) | collective-permute-done | bytes 278560 | tf_op jit(solution)/shard_map/ppermute | solution.py:27
  74.9 1.9 collective-permute-start.4
  76.8 3.9 %collective-permute-start.5 = (bf16[4,136,256]{2,1,0:T(8,128)(2,1)}, bf16[4,136,256]{2,1,0:T(8,128)(2,1)}, u32[]{:S(2)}, u32[]{:S(2)}) collective-permute-start(bf16[4,136,256]{2,1,0:T(8,128)(2,1)} %collective-permute-done.3.refs_0_), channel_id=1, source_target_pairs={{0,4},{1,5},{2,6},{3,7},{4,0},{5,1},{6,2},{7,3},{8,12},{9,13},{10,... | collective-permute-start | bytes 835592 | tf_op jit(solution)/shard_map/ppermute | solution.py:27
  80.8 3.7 %collective-permute-start.6 = (bf16[4,136,256]{2,1,0:T(8,128)(2,1)}, bf16[4,136,256]{2,1,0:T(8,128)(2,1)}, u32[]{:S(2)}, u32[]{:S(2)}) collective-permute-start(bf16[4,136,256]{2,1,0:T(8,128)(2,1)} %collective-permute-done.3.refs_0_), channel_id=1, source_target_pairs={{0,6},{1,7},{2,4},{3,5},{4,2},{5,3},{6,0},{7,1},{8,14},{9,15},{10,... | collective-permute-start | bytes 835592 | tf_op jit(solution)/shard_map/ppermute | solution.py:27
  85.2 20.2 %collective-permute-done.9.refs_6_ = bf16[4,256,512]{2,1,0:T(8,128)(2,1)} collective-permute-done((bf16[4,256,512]{2,1,0:T(8,128)(2,1)S(1)}, bf16[4,256,512]{2,1,0:T(8,128)(2,1)}, u32[]{:S(2)}, u32[]{:S(2)}) %collective-permute-start.9) | collective-permute-done | bytes 1048608 | tf_op jit(solution)/shard_map/ppermute | solution.py:27
  105.4 4.1 %mix_early.2 = (f32[2,136,256]{2,1,0:T(8,128)}, f32[2,136,256]{2,1,0:T(8,128)}) custom-call(s32[3]{0:T(128)} %pad_add_fusion.at_ref, bf16[4,136,256]{2,1,0:T(8,128)(2,1)} %pad_maximum_fusion.1.refs_0_, bf16[4,136,256]{2,1,0:T(8,128)(2,1)} %collective-permute-done.11.refs_1_, bf16[4,136,256]{2,1,0:T(8,128)(2,1)} %collective-permute-done.12.refs_2_, ...), custom_call_target="tpu_custom_call" | custom-call | flops 570425344 | bytes 3768320 | tf_op jit(solution)/shard_map/mix_early/pallas_call | solution.py:124
  109.5 4.3 %mix_late.2 = (f32[2,136,256]{2,1,0:T(8,128)}, f32[2,136,256]{2,1,0:T(8,128)}) custom-call(s32[3]{0:T(128)} %pad_add_fusion.at_ref, bf16[4,136,256]{2,1,0:T(8,128)(2,1)} %collective-permute-done.3.refs_0_, bf16[4,136,256]{2,1,0:T(8,128)(2,1)} %collective-permute-done.4.refs_1_, bf16[4,136,256]{2,1,0:T(8,128)(2,1)} %collective-permute-done.5.refs_2_, ...), custom_call_target="tpu_custom_call" | custom-call | flops 570425344 | bytes 3768320 | tf_op jit(solution)/shard_map/mix_late/pallas_call | solution.py:124
  113.9 3.9 %collective-permute-start.14 = (f32[2,136,256]{2,1,0:T(8,128)}, f32[2,136,256]{2,1,0:T(8,128)S(1)}, u32[]{:S(2)}, u32[]{:S(2)}) collective-permute-start(f32[2,136,256]{2,1,0:T(8,128)} %get-tuple-element.17), channel_id=1, source_target_pairs={{0,1},{1,0},{2,3},{3,2},{4,5},{5,4},{6,7},{7,6},{8,9},{9,8},{10,11... | collective-permute-start | bytes 835592 | tf_op jit(solution)/shard_map/ppermute | solution.py:27
  118.1 1.1 collective-permute-done.14.theirs_ref
  119.9 1.7 fold.2
  121.6 3.2 %collective-permute-start.15 = (bf16[136,256]{1,0:T(8,128)(2,1)}, bf16[136,256]{1,0:T(8,128)(2,1)S(1)}, u32[]{:S(2)}, u32[]{:S(2)}) collective-permute-start(bf16[136,256]{1,0:T(8,128)(2,1)} %get-tuple-element.19), channel_id=1, source_target_pairs={{0,256},{1,257},{2,258},{3,259},{4,260},{5,261},{6,262},{7,263},{8... | collective-permute-start | bytes 208904 | tf_op jit(solution)/shard_map/ppermute | solution.py:27
  124.9 13.6 %collective-permute-done.15 = bf16[136,256]{1,0:T(8,128)(2,1)S(1)} collective-permute-done((bf16[136,256]{1,0:T(8,128)(2,1)}, bf16[136,256]{1,0:T(8,128)(2,1)S(1)}, u32[]{:S(2)}, u32[]{:S(2)}) %collective-permute-start.15) | collective-permute-done | bytes 69664 | tf_op jit(solution)/shard_map/ppermute | solution.py:27
  138.5 0.9 slice_add_fusion.1
  142.2 6.6 %collective-permute-start.17 = (bf16[1,136,256]{2,1,0:T(8,128)(2,1)S(1)}, bf16[1,136,256]{2,1,0:T(8,128)(2,1)S(1)}, u32[]{:S(2)}, u32[]{:S(2)}) collective-permute-start(bf16[1,136,256]{2,1,0:T(8,128)(2,1)S(1)} %bitcast.44), channel_id=1, source_target_pairs={{0,32},{1,33},{2,34},{3,35},{4,36},{5,37},{6,38},{7,39},{8,40},{9,... | collective-permute-start | bytes 208904 | tf_op jit(solution)/shard_map/ppermute | solution.py:27
  148.9 2.3 collective-permute-done.17
  151.2 9.4 %collective-permute-start.18 = (bf16[2,136,256]{2,1,0:T(8,128)(2,1)S(1)}, bf16[2,136,256]{2,1,0:T(8,128)(2,1)S(1)}, u32[]{:S(2)}, u32[]{:S(2)}) collective-permute-start(bf16[2,136,256]{2,1,0:T(8,128)(2,1)S(1)} %pad_maximum_fusion.4), channel_id=1, source_target_pairs={{0,16},{1,17},{2,18},{3,19},{4,20},{5,21},{6,22},{7,23},{8,24},{9,... | collective-permute-start | bytes 417800 | tf_op jit(solution)/shard_map/ppermute | solution.py:27
  160.6 5.3 %collective-permute-done.18 = bf16[2,136,256]{2,1,0:T(8,128)(2,1)S(1)} collective-permute-done((bf16[2,136,256]{2,1,0:T(8,128)(2,1)S(1)}, bf16[2,136,256]{2,1,0:T(8,128)(2,1)S(1)}, u32[]{:S(2)}, u32[]{:S(2)}) %collective-permute-start.18) | collective-permute-done | bytes 139296 | tf_op jit(solution)/shard_map/ppermute | solution.py:27
  166.0 5.4 %collective-permute-start.19 = (bf16[4,136,256]{2,1,0:T(8,128)(2,1)S(1)}, bf16[4,136,256]{2,1,0:T(8,128)(2,1)S(1)}, u32[]{:S(2)}, u32[]{:S(2)}) collective-permute-start(bf16[4,136,256]{2,1,0:T(8,128)(2,1)S(1)} %pad_maximum_fusion.2.refs_0_), channel_id=1, source_target_pairs={{0,8},{1,9},{2,10},{3,11},{4,12},{5,13},{6,14},{7,15},{8,0},{9,1},... | collective-permute-start | bytes 835592 | tf_op jit(solution)/shard_map/ppermute | solution.py:27
  171.5 1.9 collective-permute-start.23
  173.4 3.0 %collective-permute-start.24 = (bf16[4,136,256]{2,1,0:T(8,128)(2,1)S(1)}, bf16[4,136,256]{2,1,0:T(8,128)(2,1)S(1)}, u32[]{:S(2)}, u32[]{:S(2)}) collective-permute-start(bf16[4,136,256]{2,1,0:T(8,128)(2,1)S(1)} %pad_maximum_fusion.2.refs_0_), channel_id=1, source_target_pairs={{0,4},{1,5},{2,6},{3,7},{4,0},{5,1},{6,2},{7,3},{8,12},{9,13},{10,... | collective-permute-start | bytes 835592 | tf_op jit(solution)/shard_map/ppermute | solution.py:27
  176.4 4.6 %collective-permute-start.25 = (bf16[4,136,256]{2,1,0:T(8,128)(2,1)S(1)}, bf16[4,136,256]{2,1,0:T(8,128)(2,1)S(1)}, u32[]{:S(2)}, u32[]{:S(2)}) collective-permute-start(bf16[4,136,256]{2,1,0:T(8,128)(2,1)S(1)} %pad_maximum_fusion.2.refs_0_), channel_id=1, source_target_pairs={{0,6},{1,7},{2,4},{3,5},{4,2},{5,3},{6,0},{7,1},{8,14},{9,15},{10,... | collective-permute-start | bytes 835592 | tf_op jit(solution)/shard_map/ppermute | solution.py:27
  181.1 1.9 collective-permute-start.20
  183.0 3.1 %collective-permute-start.21 = (bf16[4,136,256]{2,1,0:T(8,128)(2,1)S(1)}, bf16[4,136,256]{2,1,0:T(8,128)(2,1)S(1)}, u32[]{:S(2)}, u32[]{:S(2)}) collective-permute-start(bf16[4,136,256]{2,1,0:T(8,128)(2,1)S(1)} %collective-permute-done.19.refs_0_), channel_id=1, source_target_pairs={{0,4},{1,5},{2,6},{3,7},{4,0},{5,1},{6,2},{7,3},{8,12},{9,13},{10,... | collective-permute-start | bytes 835592 | tf_op jit(solution)/shard_map/ppermute | solution.py:27
  186.1 4.6 %collective-permute-start.22 = (bf16[4,136,256]{2,1,0:T(8,128)(2,1)S(1)}, bf16[4,136,256]{2,1,0:T(8,128)(2,1)S(1)}, u32[]{:S(2)}, u32[]{:S(2)}) collective-permute-start(bf16[4,136,256]{2,1,0:T(8,128)(2,1)S(1)} %collective-permute-done.19.refs_0_), channel_id=1, source_target_pairs={{0,6},{1,7},{2,4},{3,5},{4,2},{5,3},{6,0},{7,1},{8,14},{9,15},{10,... | collective-permute-start | bytes 835592 | tf_op jit(solution)/shard_map/ppermute | solution.py:27
  192.1 4.1 %mix_early.3 = (f32[2,136,256]{2,1,0:T(8,128)}, f32[2,136,256]{2,1,0:T(8,128)}) custom-call(s32[3]{0:T(128)} %pad_add_fusion.at_ref, bf16[4,136,256]{2,1,0:T(8,128)(2,1)} %copy-done.4, bf16[4,136,256]{2,1,0:T(8,128)(2,1)} %copy-done.8, bf16[4,136,256]{2,1,0:T(8,128)(2,1)} %copy-done.10, bf16[4,136,256]{2,1,0:T(8,128)(2,1)} %copy-done.11, ...), custom_call_target="tpu_custom_call" | custom-call | flops 570425344 | bytes 3768320 | tf_op jit(solution)/shard_map/mix_early/pallas_call | solution.py:124
  196.3 7.2 %collective-permute-done.22.refs_3_ = bf16[4,136,256]{2,1,0:T(8,128)(2,1)S(1)} collective-permute-done((bf16[4,136,256]{2,1,0:T(8,128)(2,1)S(1)}, bf16[4,136,256]{2,1,0:T(8,128)(2,1)S(1)}, u32[]{:S(2)}, u32[]{:S(2)}) %collective-permute-start.22) | collective-permute-done | bytes 278560 | tf_op jit(solution)/shard_map/ppermute | solution.py:27
  204.2 4.2 %mix_late.3 = (f32[2,136,256]{2,1,0:T(8,128)}, f32[2,136,256]{2,1,0:T(8,128)}) custom-call(s32[3]{0:T(128)} %pad_add_fusion.at_ref, bf16[4,136,256]{2,1,0:T(8,128)(2,1)} %copy-done.5, bf16[4,136,256]{2,1,0:T(8,128)(2,1)} %copy-done.6, bf16[4,136,256]{2,1,0:T(8,128)(2,1)} %copy-done.7, bf16[4,136,256]{2,1,0:T(8,128)(2,1)} %copy-done.9, ...), custom_call_target="tpu_custom_call" | custom-call | flops 570425344 | bytes 3768320 | tf_op jit(solution)/shard_map/mix_late/pallas_call | solution.py:124
  208.4 4.7 %collective-permute-start.26 = (f32[2,136,256]{2,1,0:T(8,128)}, f32[2,136,256]{2,1,0:T(8,128)S(1)}, u32[]{:S(2)}, u32[]{:S(2)}) collective-permute-start(f32[2,136,256]{2,1,0:T(8,128)} %get-tuple-element.23), channel_id=1, source_target_pairs={{0,1},{1,0},{2,3},{3,2},{4,5},{5,4},{6,7},{7,6},{8,9},{9,8},{10,11... | collective-permute-start | bytes 835592 | tf_op jit(solution)/shard_map/ppermute | solution.py:27
  213.1 1.4 collective-permute-done.26.theirs_ref
  215.2 1.7 fold.3
  216.9 8.6 %collective-permute-start.27 = (bf16[136,256]{1,0:T(8,128)(2,1)}, bf16[136,256]{1,0:T(8,128)(2,1)S(1)}, u32[]{:S(2)}, u32[]{:S(2)}) collective-permute-start(bf16[136,256]{1,0:T(8,128)(2,1)} %get-tuple-element.25), channel_id=1, source_target_pairs={{0,256},{1,257},{2,258},{3,259},{4,260},{5,261},{6,262},{7,263},{8... | collective-permute-start | bytes 208904 | tf_op jit(solution)/shard_map/ppermute | solution.py:27
  225.7 0.8 copy.40
  226.4 6.6 %collective-permute-done.27 = bf16[136,256]{1,0:T(8,128)(2,1)S(1)} collective-permute-done((bf16[136,256]{1,0:T(8,128)(2,1)}, bf16[136,256]{1,0:T(8,128)(2,1)S(1)}, u32[]{:S(2)}, u32[]{:S(2)}) %collective-permute-start.27) | collective-permute-done | bytes 69664 | tf_op jit(solution)/shard_map/ppermute | solution.py:27
  233.8 0.9 slice_add_fusion
  (134 shorter events, 12.0 us)
Async XLA Ops:
  0.6 117.3 %copy-start = (bf16[700,256]{1,0:T(8,128)(2,1)S(1)}, bf16[700,256]{1,0:T(8,128)(2,1)}, u32[]{:S(2)}) copy-start(bf16[700,256]{1,0:T(8,128)(2,1)} %param.20) | copy-start | bytes 1075204
  2.2 9.0 %copy-start.18 = (bf16[64,2,256]{2,1,0:T(2,128)(2,1)S(1)}, bf16[64,2,256]{2,1,0:T(2,128)(2,1)}, u32[]{:S(2)}) copy-start(bf16[64,2,256]{2,1,0:T(2,128)(2,1)} %param.16) | copy-start | bytes 196612
  2.3 29.3 %collective-permute-start.7 = (bf16[4,256,256]{2,1,0:T(8,128)(2,1)S(1)}, bf16[4,256,256]{2,1,0:T(8,128)(2,1)S(1)}, u32[]{:S(2)}, u32[]{:S(2)}) collective-permute-start(bf16[4,256,256]{2,1,0:T(8,128)(2,1)S(1)} %get-tuple-element.33), channel_id=1, source_target_pairs={{0,1},{1,0},{2,3},{3,2},{4,5},{5,4},{6,7},{7,6},{8,9},{9,8},{10,11... | collective-permute-start | bytes 1572872 | tf_op jit(solution)/shard_map/ppermute | solution.py:27
  11.1 20.6 %copy-start.31 = (pred[256]{0:T(512)(128)(4,1)}, pred[256]{0:T(512)(128)(4,1)S(1)}, u32[]{:S(2)}) copy-start(pred[256]{0:T(512)(128)(4,1)S(1)} %compare_and_fusion.1) | copy-start | bytes 772
  11.1 20.6 %copy-start.29 = (s32[128]{0:T(128)}, s32[128]{0:T(128)S(1)}, u32[]{:S(2)}) copy-start(s32[128]{0:T(128)S(1)} %get-tuple-element.46) | copy-start | bytes 1540
  11.1 20.6 %copy-start.33 = (pred[128]{0:T(512)(128)(4,1)}, pred[128]{0:T(512)(128)(4,1)S(1)}, u32[]{:S(2)}) copy-start(pred[128]{0:T(512)(128)(4,1)S(1)} %compare_and_fusion.2) | copy-start | bytes 388
  12.3 0.7 collective-permute-start
  12.9 24.1 %collective-permute-start.1 = (bf16[1,136,256]{2,1,0:T(8,128)(2,1)S(1)}, bf16[1,136,256]{2,1,0:T(8,128)(2,1)S(1)}, u32[]{:S(2)}, u32[]{:S(2)}) collective-permute-start(bf16[1,136,256]{2,1,0:T(8,128)(2,1)S(1)} %bitcast.41), channel_id=1, source_target_pairs={{0,32},{1,33},{2,34},{3,35},{4,36},{5,37},{6,38},{7,39},{8,40},{9,... | collective-permute-start | bytes 208904 | tf_op jit(solution)/shard_map/ppermute | solution.py:27
  31.6 31.0 %copy-start.28 = (s32[64]{0:T(128)S(1)}, s32[64]{0:T(128)}, u32[]{:S(2)}) copy-start(s32[64]{0:T(128)} %param.23) | copy-start | bytes 772
  31.6 31.0 %copy-start.21 = (s32[64,2]{0,1:T(2,128)S(1)}, s32[64,2]{0,1:T(2,128)}, u32[]{:S(2)}) copy-start(s32[64,2]{0,1:T(2,128)} %param.22) | copy-start | bytes 1540
  31.6 36.2 %copy-start.22 = (f32[256]{0:T(256)S(1)}, f32[256]{0:T(256)}, u32[]{:S(2)}) copy-start(f32[256]{0:T(256)} %param.25) | copy-start | bytes 3076
  31.6 53.5 %copy-start.23 = (f32[256]{0:T(256)S(1)}, f32[256]{0:T(256)}, u32[]{:S(2)}) copy-start(f32[256]{0:T(256)} %param.24) | copy-start | bytes 3076
  31.7 73.7 %copy-start.1 = (bf16[4,256,512]{2,1,0:T(8,128)(2,1)}, bf16[4,256,512]{2,1,0:T(8,128)(2,1)S(1)}, u32[]{:S(2)}) copy-start(bf16[4,256,512]{2,1,0:T(8,128)(2,1)S(1)} %pad_maximum_fusion.refs_4_) | copy-start | bytes 3145732
  31.7 49.0 %collective-permute-start.10 = (bf16[4,256,512]{2,1,0:T(8,128)(2,1)S(1)}, bf16[4,256,512]{2,1,0:T(8,128)(2,1)S(1)}, u32[]{:S(2)}, u32[]{:S(2)}) collective-permute-start(bf16[4,256,512]{2,1,0:T(8,128)(2,1)S(1)} %pad_maximum_fusion.refs_4_), channel_id=1, source_target_pairs={{0,192},{1,193},{2,194},{3,195},{4,196},{5,197},{6,198},{7,199},{8... | collective-permute-start | bytes 3145736 | tf_op jit(solution)/shard_map/ppermute | solution.py:27
  37.0 9.7 %collective-permute-start.2 = (bf16[2,136,256]{2,1,0:T(8,128)(2,1)S(1)}, bf16[2,136,256]{2,1,0:T(8,128)(2,1)S(1)}, u32[]{:S(2)}, u32[]{:S(2)}) collective-permute-start(bf16[2,136,256]{2,1,0:T(8,128)(2,1)S(1)} %pad_maximum_fusion.3), channel_id=1, source_target_pairs={{0,16},{1,17},{2,18},{3,19},{4,20},{5,21},{6,22},{7,23},{8,24},{9,... | collective-permute-start | bytes 417800 | tf_op jit(solution)/shard_map/ppermute | solution.py:27
  47.5 15.1 %collective-permute-start.11 = (bf16[4,136,256]{2,1,0:T(8,128)(2,1)}, bf16[4,136,256]{2,1,0:T(8,128)(2,1)}, u32[]{:S(2)}, u32[]{:S(2)}) collective-permute-start(bf16[4,136,256]{2,1,0:T(8,128)(2,1)} %pad_maximum_fusion.1.refs_0_), channel_id=1, source_target_pairs={{0,2},{1,3},{2,0},{3,1},{4,6},{5,7},{6,4},{7,5},{8,10},{9,11},{10,... | collective-permute-start | bytes 835592 | tf_op jit(solution)/shard_map/ppermute | solution.py:27
  50.7 15.2 %collective-permute-start.12 = (bf16[4,136,256]{2,1,0:T(8,128)(2,1)}, bf16[4,136,256]{2,1,0:T(8,128)(2,1)}, u32[]{:S(2)}, u32[]{:S(2)}) collective-permute-start(bf16[4,136,256]{2,1,0:T(8,128)(2,1)} %pad_maximum_fusion.1.refs_0_), channel_id=1, source_target_pairs={{0,4},{1,5},{2,6},{3,7},{4,0},{5,1},{6,2},{7,3},{8,12},{9,13},{10,... | collective-permute-start | bytes 835592 | tf_op jit(solution)/shard_map/ppermute | solution.py:27
  55.2 29.9 %collective-permute-start.8 = (bf16[4,256,512]{2,1,0:T(8,128)(2,1)S(1)}, bf16[4,256,512]{2,1,0:T(8,128)(2,1)S(1)}, u32[]{:S(2)}, u32[]{:S(2)}) collective-permute-start(bf16[4,256,512]{2,1,0:T(8,128)(2,1)S(1)} %pad_maximum_fusion.refs_4_), channel_id=1, source_target_pairs={{0,64},{1,65},{2,66},{3,67},{4,68},{5,69},{6,70},{7,71},{8,72},{9,... | collective-permute-start | bytes 3145736 | tf_op jit(solution)/shard_map/ppermute | solution.py:27
  58.2 47.2 %collective-permute-start.9 = (bf16[4,256,512]{2,1,0:T(8,128)(2,1)S(1)}, bf16[4,256,512]{2,1,0:T(8,128)(2,1)}, u32[]{:S(2)}, u32[]{:S(2)}) collective-permute-start(bf16[4,256,512]{2,1,0:T(8,128)(2,1)S(1)} %pad_maximum_fusion.refs_4_), channel_id=1, source_target_pairs={{0,128},{1,129},{2,130},{3,131},{4,132},{5,133},{6,134},{7,135},{8... | collective-permute-start | bytes 3145736 | tf_op jit(solution)/shard_map/ppermute | solution.py:27
  62.6 14.2 %collective-permute-start.13 = (bf16[4,136,256]{2,1,0:T(8,128)(2,1)}, bf16[4,136,256]{2,1,0:T(8,128)(2,1)}, u32[]{:S(2)}, u32[]{:S(2)}) collective-permute-start(bf16[4,136,256]{2,1,0:T(8,128)(2,1)} %pad_maximum_fusion.1.refs_0_), channel_id=1, source_target_pairs={{0,6},{1,7},{2,4},{3,5},{4,2},{5,3},{6,0},{7,1},{8,14},{9,15},{10,... | collective-permute-start | bytes 835592 | tf_op jit(solution)/shard_map/ppermute | solution.py:27
  65.8 9.1 %collective-permute-start.3 = (bf16[4,136,256]{2,1,0:T(8,128)(2,1)}, bf16[4,136,256]{2,1,0:T(8,128)(2,1)}, u32[]{:S(2)}, u32[]{:S(2)}) collective-permute-start(bf16[4,136,256]{2,1,0:T(8,128)(2,1)} %pad_maximum_fusion.1.refs_0_), channel_id=1, source_target_pairs={{0,8},{1,9},{2,10},{3,11},{4,12},{5,13},{6,14},{7,15},{8,0},{9,1},... | collective-permute-start | bytes 835592 | tf_op jit(solution)/shard_map/ppermute | solution.py:27
  74.9 34.6 %collective-permute-start.4 = (bf16[4,136,256]{2,1,0:T(8,128)(2,1)}, bf16[4,136,256]{2,1,0:T(8,128)(2,1)}, u32[]{:S(2)}, u32[]{:S(2)}) collective-permute-start(bf16[4,136,256]{2,1,0:T(8,128)(2,1)} %collective-permute-done.3.refs_0_), channel_id=1, source_target_pairs={{0,2},{1,3},{2,0},{3,1},{4,6},{5,7},{6,4},{7,5},{8,10},{9,11},{10,... | collective-permute-start | bytes 835592 | tf_op jit(solution)/shard_map/ppermute | solution.py:27
  76.8 32.7 %collective-permute-start.5 = (bf16[4,136,256]{2,1,0:T(8,128)(2,1)}, bf16[4,136,256]{2,1,0:T(8,128)(2,1)}, u32[]{:S(2)}, u32[]{:S(2)}) collective-permute-start(bf16[4,136,256]{2,1,0:T(8,128)(2,1)} %collective-permute-done.3.refs_0_), channel_id=1, source_target_pairs={{0,4},{1,5},{2,6},{3,7},{4,0},{5,1},{6,2},{7,3},{8,12},{9,13},{10,... | collective-permute-start | bytes 835592 | tf_op jit(solution)/shard_map/ppermute | solution.py:27
  80.8 24.6 %copy-start.2 = (bf16[4,256,512]{2,1,0:T(8,128)(2,1)}, bf16[4,256,512]{2,1,0:T(8,128)(2,1)S(1)}, u32[]{:S(2)}) copy-start(bf16[4,256,512]{2,1,0:T(8,128)(2,1)S(1)} %collective-permute-done.10.refs_7_) | copy-start | bytes 3145732
  80.8 28.7 %collective-permute-start.6 = (bf16[4,136,256]{2,1,0:T(8,128)(2,1)}, bf16[4,136,256]{2,1,0:T(8,128)(2,1)}, u32[]{:S(2)}, u32[]{:S(2)}) collective-permute-start(bf16[4,136,256]{2,1,0:T(8,128)(2,1)} %collective-permute-done.3.refs_0_), channel_id=1, source_target_pairs={{0,6},{1,7},{2,4},{3,5},{4,2},{5,3},{6,0},{7,1},{8,14},{9,15},{10,... | collective-permute-start | bytes 835592 | tf_op jit(solution)/shard_map/ppermute | solution.py:27
  85.1 20.3 %copy-start.3 = (bf16[4,256,512]{2,1,0:T(8,128)(2,1)}, bf16[4,256,512]{2,1,0:T(8,128)(2,1)S(1)}, u32[]{:S(2)}) copy-start(bf16[4,256,512]{2,1,0:T(8,128)(2,1)S(1)} %collective-permute-done.8.refs_5_) | copy-start | bytes 3145732
  113.8 26.4 %copy-start.19 = (bf16[64,2,256]{2,1,0:T(2,128)(2,1)S(1)}, bf16[64,2,256]{2,1,0:T(2,128)(2,1)}, u32[]{:S(2)}) copy-start(bf16[64,2,256]{2,1,0:T(2,128)(2,1)} %param.16) | copy-start | bytes 196612
  113.8 26.4 %copy-start.24 = (f32[64,2,256]{2,1,0:T(2,128)S(1)}, f32[64,2,256]{2,1,0:T(2,128)}, u32[]{:S(2)}) copy-start(f32[64,2,256]{2,1,0:T(2,128)} %param.14) | copy-start | bytes 393220
  113.8 26.4 %copy-start.25 = (f32[64,2,256]{2,1,0:T(2,128)S(1)}, f32[64,2,256]{2,1,0:T(2,128)}, u32[]{:S(2)}) copy-start(f32[64,2,256]{2,1,0:T(2,128)} %param.15) | copy-start | bytes 393220
  113.8 26.4 %copy-start.26 = (f32[256]{0:T(256)S(1)}, f32[256]{0:T(256)}, u32[]{:S(2)}) copy-start(f32[256]{0:T(256)} %param.27) | copy-start | bytes 3076
  113.9 26.4 %copy-start.27 = (f32[256]{0:T(256)S(1)}, f32[256]{0:T(256)}, u32[]{:S(2)}) copy-start(f32[256]{0:T(256)} %param.26) | copy-start | bytes 3076
  113.9 26.4 %copy-start.32 = (pred[256]{0:T(512)(128)(4,1)S(1)}, pred[256]{0:T(512)(128)(4,1)}, u32[]{:S(2)}) copy-start(pred[256]{0:T(512)(128)(4,1)} %copy-done.31) | copy-start | bytes 772
  113.9 5.3 %collective-permute-start.14 = (f32[2,136,256]{2,1,0:T(8,128)}, f32[2,136,256]{2,1,0:T(8,128)S(1)}, u32[]{:S(2)}, u32[]{:S(2)}) collective-permute-start(f32[2,136,256]{2,1,0:T(8,128)} %get-tuple-element.17), channel_id=1, source_target_pairs={{0,1},{1,0},{2,3},{3,2},{4,5},{5,4},{6,7},{7,6},{8,9},{9,8},{10,11... | collective-permute-start | bytes 835592 | tf_op jit(solution)/shard_map/ppermute | solution.py:27
  121.6 16.8 %collective-permute-start.15 = (bf16[136,256]{1,0:T(8,128)(2,1)}, bf16[136,256]{1,0:T(8,128)(2,1)S(1)}, u32[]{:S(2)}, u32[]{:S(2)}) collective-permute-start(bf16[136,256]{1,0:T(8,128)(2,1)} %get-tuple-element.19), channel_id=1, source_target_pairs={{0,256},{1,257},{2,258},{3,259},{4,260},{5,261},{6,262},{7,263},{8... | collective-permute-start | bytes 208904 | tf_op jit(solution)/shard_map/ppermute | solution.py:27
  141.6 0.7 collective-permute-start.16
  142.2 9.0 %collective-permute-start.17 = (bf16[1,136,256]{2,1,0:T(8,128)(2,1)S(1)}, bf16[1,136,256]{2,1,0:T(8,128)(2,1)S(1)}, u32[]{:S(2)}, u32[]{:S(2)}) collective-permute-start(bf16[1,136,256]{2,1,0:T(8,128)(2,1)S(1)} %bitcast.44), channel_id=1, source_target_pairs={{0,32},{1,33},{2,34},{3,35},{4,36},{5,37},{6,38},{7,39},{8,40},{9,... | collective-permute-start | bytes 208904 | tf_op jit(solution)/shard_map/ppermute | solution.py:27
  151.2 14.7 %collective-permute-start.18 = (bf16[2,136,256]{2,1,0:T(8,128)(2,1)S(1)}, bf16[2,136,256]{2,1,0:T(8,128)(2,1)S(1)}, u32[]{:S(2)}, u32[]{:S(2)}) collective-permute-start(bf16[2,136,256]{2,1,0:T(8,128)(2,1)S(1)} %pad_maximum_fusion.4), channel_id=1, source_target_pairs={{0,16},{1,17},{2,18},{3,19},{4,20},{5,21},{6,22},{7,23},{8,24},{9,... | collective-permute-start | bytes 417800 | tf_op jit(solution)/shard_map/ppermute | solution.py:27
  166.0 24.7 %copy-start.4 = (bf16[4,136,256]{2,1,0:T(8,128)(2,1)}, bf16[4,136,256]{2,1,0:T(8,128)(2,1)S(1)}, u32[]{:S(2)}) copy-start(bf16[4,136,256]{2,1,0:T(8,128)(2,1)S(1)} %pad_maximum_fusion.2.refs_0_) | copy-start | bytes 835588
  166.0 15.1 %collective-permute-start.19 = (bf16[4,136,256]{2,1,0:T(8,128)(2,1)S(1)}, bf16[4,136,256]{2,1,0:T(8,128)(2,1)S(1)}, u32[]{:S(2)}, u32[]{:S(2)}) collective-permute-start(bf16[4,136,256]{2,1,0:T(8,128)(2,1)S(1)} %pad_maximum_fusion.2.refs_0_), channel_id=1, source_target_pairs={{0,8},{1,9},{2,10},{3,11},{4,12},{5,13},{6,14},{7,15},{8,0},{9,1},... | collective-permute-start | bytes 835592 | tf_op jit(solution)/shard_map/ppermute | solution.py:27
  171.5 14.7 %collective-permute-start.23 = (bf16[4,136,256]{2,1,0:T(8,128)(2,1)S(1)}, bf16[4,136,256]{2,1,0:T(8,128)(2,1)S(1)}, u32[]{:S(2)}, u32[]{:S(2)}) collective-permute-start(bf16[4,136,256]{2,1,0:T(8,128)(2,1)S(1)} %pad_maximum_fusion.2.refs_0_), channel_id=1, source_target_pairs={{0,2},{1,3},{2,0},{3,1},{4,6},{5,7},{6,4},{7,5},{8,10},{9,11},{10,... | collective-permute-start | bytes 835592 | tf_op jit(solution)/shard_map/ppermute | solution.py:27
  173.4 17.3 %collective-permute-start.24 = (bf16[4,136,256]{2,1,0:T(8,128)(2,1)S(1)}, bf16[4,136,256]{2,1,0:T(8,128)(2,1)S(1)}, u32[]{:S(2)}, u32[]{:S(2)}) collective-permute-start(bf16[4,136,256]{2,1,0:T(8,128)(2,1)S(1)} %pad_maximum_fusion.2.refs_0_), channel_id=1, source_target_pairs={{0,4},{1,5},{2,6},{3,7},{4,0},{5,1},{6,2},{7,3},{8,12},{9,13},{10,... | collective-permute-start | bytes 835592 | tf_op jit(solution)/shard_map/ppermute | solution.py:27
  176.4 14.3 %collective-permute-start.25 = (bf16[4,136,256]{2,1,0:T(8,128)(2,1)S(1)}, bf16[4,136,256]{2,1,0:T(8,128)(2,1)S(1)}, u32[]{:S(2)}, u32[]{:S(2)}) collective-permute-start(bf16[4,136,256]{2,1,0:T(8,128)(2,1)S(1)} %pad_maximum_fusion.2.refs_0_), channel_id=1, source_target_pairs={{0,6},{1,7},{2,4},{3,5},{4,2},{5,3},{6,0},{7,1},{8,14},{9,15},{10,... | collective-permute-start | bytes 835592 | tf_op jit(solution)/shard_map/ppermute | solution.py:27
  181.1 15.1 %copy-start.5 = (bf16[4,136,256]{2,1,0:T(8,128)(2,1)}, bf16[4,136,256]{2,1,0:T(8,128)(2,1)S(1)}, u32[]{:S(2)}) copy-start(bf16[4,136,256]{2,1,0:T(8,128)(2,1)S(1)} %collective-permute-done.19.refs_0_) | copy-start | bytes 835588
  181.1 15.1 %collective-permute-start.20 = (bf16[4,136,256]{2,1,0:T(8,128)(2,1)S(1)}, bf16[4,136,256]{2,1,0:T(8,128)(2,1)S(1)}, u32[]{:S(2)}, u32[]{:S(2)}) collective-permute-start(bf16[4,136,256]{2,1,0:T(8,128)(2,1)S(1)} %collective-permute-done.19.refs_0_), channel_id=1, source_target_pairs={{0,2},{1,3},{2,0},{3,1},{4,6},{5,7},{6,4},{7,5},{8,10},{9,11},{10,... | collective-permute-start | bytes 835592 | tf_op jit(solution)/shard_map/ppermute | solution.py:27
  183.0 13.3 %collective-permute-start.21 = (bf16[4,136,256]{2,1,0:T(8,128)(2,1)S(1)}, bf16[4,136,256]{2,1,0:T(8,128)(2,1)S(1)}, u32[]{:S(2)}, u32[]{:S(2)}) collective-permute-start(bf16[4,136,256]{2,1,0:T(8,128)(2,1)S(1)} %collective-permute-done.19.refs_0_), channel_id=1, source_target_pairs={{0,4},{1,5},{2,6},{3,7},{4,0},{5,1},{6,2},{7,3},{8,12},{9,13},{10,... | collective-permute-start | bytes 835592 | tf_op jit(solution)/shard_map/ppermute | solution.py:27
  186.1 17.3 %collective-permute-start.22 = (bf16[4,136,256]{2,1,0:T(8,128)(2,1)S(1)}, bf16[4,136,256]{2,1,0:T(8,128)(2,1)S(1)}, u32[]{:S(2)}, u32[]{:S(2)}) collective-permute-start(bf16[4,136,256]{2,1,0:T(8,128)(2,1)S(1)} %collective-permute-done.19.refs_0_), channel_id=1, source_target_pairs={{0,6},{1,7},{2,4},{3,5},{4,2},{5,3},{6,0},{7,1},{8,14},{9,15},{10,... | collective-permute-start | bytes 835592 | tf_op jit(solution)/shard_map/ppermute | solution.py:27
  208.4 6.0 %collective-permute-start.26 = (f32[2,136,256]{2,1,0:T(8,128)}, f32[2,136,256]{2,1,0:T(8,128)S(1)}, u32[]{:S(2)}, u32[]{:S(2)}) collective-permute-start(f32[2,136,256]{2,1,0:T(8,128)} %get-tuple-element.23), channel_id=1, source_target_pairs={{0,1},{1,0},{2,3},{3,2},{4,5},{5,4},{6,7},{7,6},{8,9},{9,8},{10,11... | collective-permute-start | bytes 835592 | tf_op jit(solution)/shard_map/ppermute | solution.py:27
  216.9 16.2 %collective-permute-start.27 = (bf16[136,256]{1,0:T(8,128)(2,1)}, bf16[136,256]{1,0:T(8,128)(2,1)S(1)}, u32[]{:S(2)}, u32[]{:S(2)}) collective-permute-start(bf16[136,256]{1,0:T(8,128)(2,1)} %get-tuple-element.25), channel_id=1, source_target_pairs={{0,256},{1,257},{2,258},{3,259},{4,260},{5,261},{6,262},{7,263},{8... | collective-permute-start | bytes 208904 | tf_op jit(solution)/shard_map/ppermute | solution.py:27
  (15 other events, 51.5 us)
where the time goes:
time: 237 us; the launch traced here: 236 us
  starting transfers between devices  125 us (53%)
  waiting for transfers between devices  74.9 us (32%)
  Pallas kernels  20.1 us (8%)
  local copies, waits for them, and re-layouts  8.36 us (4%)
  other arithmetic  5.11 us (2%)
    ppermute x28, starting transfers between devices, permute(): return lax.ppermute(value, AXES, pairs)  125 us
    ppermute x28, waiting for transfers between devices, permute(): return lax.ppermute(value, AXES, pairs)  74.9 us
    pallas_call x4, Pallas kernels, mix(): pl.pallas_call(functools.partial(mix_kernel, rows=rows, trials=trials, la...  16.7 us
    unnamed x73, local copies, waits for them, and re-layouts  7.79 us
  transfers between devices with their start and end apart: 28, of which 13 were waited for; matrix products, arithmetic and copies ran while one was open for 1% of the time, Pallas kernels for 3%

commit v1 on v0

--- a/solution.py
+++ b/solution.py
@@ -61,20 +61,100 @@
     return row == col
 
 
-def pack(spike_rows, factor_rows, trials, rank):
-    rows, block = spike_rows.shape
+def by_trial(values, rows):
+    trials, block = values.shape
+    trial = lax.broadcasted_iota(jnp.int32, (rows, block), 0) % trials
+    out = jnp.broadcast_to(values[:1], (rows, block))
+    for j in range(1, trials):
+        out = jnp.where(trial == j, jnp.broadcast_to(values[j : j + 1], (rows, block)), out)
+    return out
+
+
+def three_terms(value):
+    high = value.astype(jnp.bfloat16).astype(jnp.float32)
+    rest = value - high
+    middle = rest.astype(jnp.bfloat16).astype(jnp.float32)
+    return [high, middle, rest - middle]
+
+
+def store_packed(out_ref, spikes, factors, trials, rank):
+    rows, block = spikes.shape
     full = lax.dot_general(
-        spike_rows, factor_rows, (((1,), (1,)), ((), ())), preferred_element_type=jnp.float32
+        spikes, factors, (((1,), (1,)), ((), ())), preferred_element_type=jnp.float32
     )
     kept = jnp.where(member_mask(rows, full.shape[1], trials, rank), full, 0.0)
-    part = kept.reshape(rows // trials, trials, full.shape[1]).sum(0)
-    high = lax.reduce_precision(part, 8, 7)
-    rest = part - high
-    middle = lax.reduce_precision(rest, 8, 7)
-    last = rest - middle
-    terms = [t.astype(jnp.bfloat16) for t in (high, middle, last)]
-    pad = jnp.zeros((EXT - 3 * trials, block), jnp.bfloat16)
-    return jnp.concatenate([spike_rows, *terms, pad], axis=0)
+    trial = lax.broadcasted_iota(jnp.int32, kept.shape, 0) % trials
+    parts = [
+        jnp.sum(jnp.where(trial == j, kept, 0.0), axis=0, keepdims=True) for j in range(trials)
+    ]
+    terms = three_terms(jnp.concatenate(parts, axis=0))
+    pad = jnp.zeros((EXT - 3 * trials, block), jnp.float32)
+    out_ref[:rows] = spikes
+    out_ref[rows:] = jnp.concatenate([*terms, pad], axis=0).astype(jnp.bfloat16)
+
+
+def pack_kernel(spikes_ref, factors_ref, out_ref, *, trials, rank):
+    store_packed(out_ref, spikes_ref[...], factors_ref[...], trials, rank)
+
+
+def pack(spikes, factors, trials, rank):
+    rows, block = spikes.shape
+    whole = pl.BlockSpec(memory_space=pltpu.VMEM)
+    return pl.pallas_call(
+        functools.partial(pack_kernel, trials=trials, rank=rank),
+        out_shape=jax.ShapeDtypeStruct((rows + EXT, block), jnp.bfloat16),
+        in_specs=[whole] * 2,
+        out_specs=whole,
+        compiler_params=pltpu.CompilerParams(vmem_limit_bytes=4 << 20),
+        name="pack",
+    )(spikes, factors)
+
+
+def update_kernel(
+    keep_ref, came_ref, packed_ref, v_ref, a_ref, lanes_ref, cols_ref, u_ref, f_ref, *outs, **sizes
+):
+    step, trials, rank = sizes["step"], sizes["trials"], sizes["rank"]
+    rows, _ = v_ref.shape
+    total = keep_ref[:rows] + came_ref[:rows].astype(jnp.float32)
+    tail = came_ref[rows:].astype(jnp.float32)
+    proj = keep_ref[rows : rows + trials]
+    for term in range(3):
+        proj = proj + tail[term * trials : (term + 1) * trials]
+    mask = member_mask(rows, u_ref.shape[0], trials, rank)
+    spread = jnp.where(mask, by_trial(proj, rows), 0.0).astype(jnp.bfloat16)
+    low = jnp.dot(spread, u_ref[...], preferred_element_type=jnp.float32)
+    current = by_trial(lanes_ref[4 + step * trials : 4 + (step + 1) * trials], rows)
+    drive = total + cols_ref[:, :1] * low + current
+    decay_mem, decay_adapt = lanes_ref[0:1], lanes_ref[1:2]
+    base, adapt = lanes_ref[2:3], lanes_ref[3:4]
+    spikes = packed_ref[:rows].astype(jnp.float32)
+    v, a = v_ref[...], a_ref[...]
+    v_new = decay_mem * v + (1.0 - decay_mem) * drive - spikes * (base + adapt * a)
+    a_new = decay_adapt * a + (1.0 - decay_adapt) * spikes
+    active = cols_ref[:, 1:2] > float(step)
+    v = jnp.where(active, v_new, v)
+    a = jnp.where(active, a_new, a)
+    outs[0][...] = v
+    outs[1][...] = a
+    if len(outs) > 2:
+        fresh = jax.nn.sigmoid(3.0 * (v - base - adapt * a)).astype(jnp.bfloat16)
+        store_packed(outs[2], fresh, f_ref[...], trials, rank)
+
+
+def update(keep, came, packed, v, a, lanes, cols, u_rows, f_rows, step, trials, rank):
+    state = jax.ShapeDtypeStruct(v.shape, jnp.float32)
+    outs = [state, state]
+    if step + 1 < STEPS:
+        outs.append(jax.ShapeDtypeStruct(packed.shape, packed.dtype))
+    whole = pl.BlockSpec(memory_space=pltpu.VMEM)
+    return pl.pallas_call(
+        functools.partial(update_kernel, step=step, trials=trials, rank=rank),
+        out_shape=tuple(outs),
+        in_specs=[whole] * 9,
+        out_specs=(whole,) * len(outs),
+        compiler_params=pltpu.CompilerParams(vmem_limit_bytes=6 << 20),
+        name="update",
+    )(keep, came, packed, v, a, lanes, cols, u_rows, f_rows)
 
 
 def mix_kernel(at_ref, *refs, rows, trials, late):
@@ -131,6 +211,7 @@
             bytes_accessed=2 * inputs + 16 * tall * block,
             transcendentals=0,
         ),
+        compiler_params=pltpu.CompilerParams(vmem_limit_bytes=12 << 20),
         name="mix_late" if before else "mix_early",
     )(at, *spikes, *weights, *before)
 
@@ -138,13 +219,9 @@
 def fold_kernel(mine_ref, theirs_ref, keep_ref, give_ref, *, rows, trials):
     keep_ref[...] = mine_ref[0] + theirs_ref[0]
     give = mine_ref[1] + theirs_ref[1]
-    tail = give[rows : rows + trials]
-    high = tail.astype(jnp.bfloat16).astype(jnp.float32)
-    rest = tail - high
-    middle = rest.astype(jnp.bfloat16).astype(jnp.float32)
-    pad = jnp.zeros((EXT - 3 * trials, tail.shape[1]), jnp.float32)
-    sent = jnp.concatenate([give[:rows], high, middle, rest - middle, pad], axis=0)
-    give_ref[...] = sent.astype(jnp.bfloat16)
+    terms = three_terms(give[rows : rows + trials])
+    pad = jnp.zeros((EXT - 3 * trials, give.shape[1]), jnp.float32)
+    give_ref[...] = jnp.concatenate([give[:rows], *terms, pad], axis=0).astype(jnp.bfloat16)
 
 
 def fold(mine, theirs, rows, trials):
@@ -158,6 +235,7 @@
         ),
         in_specs=[whole, whole],
         out_specs=(whole, whole),
+        compiler_params=pltpu.CompilerParams(vmem_limit_bytes=4 << 20),
         name="fold",
     )(mine, theirs)
 
@@ -169,7 +247,8 @@
     one = at["c"] == 1
     keep = jnp.where(one, split[:, :, 1], split[:, :, 0]).transpose(1, 2, 0)
     give = jnp.where(one, split[:, :, 0], split[:, :, 1]).transpose(1, 2, 0)
-    own = jnp.concatenate([keep, over_c(give)], axis=2)
+    got = over_c(give)
+    own = jnp.concatenate([keep, got], axis=2)
     chunks = [own]
     for k in (1, 2, 3):
         chunks.append(over_x(own, k))
@@ -196,20 +275,33 @@
     rank = factor_u.shape[1]
     rows = members * trials
     at = {name: lax.axis_index(name) for name in AXES}
-    sign = (1 - 2 * (member_ids % 2)).astype(jnp.float32)
     u_rows = factor_u.reshape(members * rank, block)
-    v_rows = factor_v.reshape(members * rank, block)
+    f_rows = factor_v.reshape(members * rank, block)
+    half_sign = 0.5 * (1 - 2 * (member_ids % 2)).astype(jnp.float32)
+    cols = jnp.stack(
+        [jnp.repeat(half_sign, trials), step_count.reshape(rows).astype(jnp.float32)], axis=1
+    )
+    current = jnp.dot(
+        spikes_in.reshape(STEPS * trials, -1).astype(jnp.bfloat16),
+        in_weight,
+        preferred_element_type=jnp.float32,
+    )
+    lanes = jnp.stack([decay_mem, decay_adapt, thr_base, thr_adapt])
+    lanes = jnp.concatenate([lanes, current], axis=0)
     place = jnp.stack([at["a"] ^ at["zh"], at["b"] ^ at["x"], at["y"]])
+    v, a = v_init.reshape(rows, block), a_init.reshape(rows, block)
+    packed = pack(z_init.reshape(rows, block), f_rows, trials, rank)
     weights = spread_weights(base_weight, at)
-    state_v, state_a, spikes = (v_init, a_init, z_init)
     for step in range(STEPS):
-        spikes_f = spikes.astype(jnp.float32)
-        held = pack(spikes.reshape(rows, block), v_rows, trials, rank)
-        held = to_owner(held)[None]
+        held = to_owner(packed)[None]
         other = over_a(held)
         held = jnp.concatenate([held, other], axis=0)
         other = over_b(held, 2)
-        early = [jnp.concatenate([held, other], axis=0)]
+        held = jnp.concatenate([held, other], axis=0)
+        if step == 0:
+            ready = (held, place, lanes, cols, u_rows, v, a)
+            held, place, lanes, cols, u_rows, v, a = lax.optimization_barrier(ready)
+        early = [held]
         late = [over_b(early[0], 1)]
         for pieces in (early, late):
             for k in (1, 2, 3):
@@ -218,37 +310,12 @@
         mine, theirs = mix(place, late, weights, rows, trials, halves)
         theirs = over_c(theirs)
         keep, give = fold(mine, theirs, rows, trials)
-        came = over_zh(give).astype(jnp.float32)
-        total = keep[:rows] + came[:rows]
-        proj = keep[rows : rows + trials]
-        for term in range(3):
-            proj = proj + came[rows + term * trials : rows + (term + 1) * trials]
-        proj = proj.astype(jnp.bfloat16)
-        mask = member_mask(rows, members * rank, trials, rank)
-        spread = jnp.broadcast_to(proj[None], (members, trials, members * rank))
-        spread = jnp.where(mask, spread.reshape(rows, members * rank), 0).astype(jnp.bfloat16)
-        low = lax.dot_general(
-            spread, u_rows, (((1,), (0,)), ((), ())), preferred_element_type=jnp.float32
-        ).reshape(members, trials, block)
-        dense = total.reshape(members, trials, block)
-        current = jnp.dot(
-            spikes_in[step].astype(jnp.bfloat16), in_weight, preferred_element_type=jnp.float32
+        came = over_zh(give)
+        v, a, *rest = update(
+            keep, came, packed, v, a, lanes, cols, u_rows, f_rows, step, trials, rank
         )
-        drive = dense + 0.5 * sign[:, None, None] * low + current[None]
-        v_new = (
-            decay_mem * state_v
-            + (1.0 - decay_mem) * drive
-            - spikes_f * (thr_base + thr_adapt * state_a)
-        )
-        a_new = decay_adapt * state_a + (1.0 - decay_adapt) * spikes_f
-        active = (step_count > step)[:, :, None]
-        state_v = jnp.where(active, v_new, state_v)
-        state_a = jnp.where(active, a_new, state_a)
-        if step + 1 < STEPS:
-            spikes = jax.nn.sigmoid(3.0 * (state_v - thr_base - thr_adapt * state_a)).astype(
-                jnp.bfloat16
-            )
-    return (state_v, state_a)
+        packed = rest[0] if rest else None
+    return (v.reshape(v_init.shape), a.reshape(a_init.shape))
 
 
 def solution(mesh):

time: 237 us -> 224 us (0.945)
  the two profiles are of different devices: /device:TPU:1 before, /device:TPU:35 now
where the time goes in v1:
time: 224 us; the launch traced here: 223 us
  starting transfers between devices  137 us (61%)
  waiting for transfers between devices  52.5 us (23%)
  local copies, waits for them, and re-layouts  18.5 us (8%)
  Pallas kernels  10.3 us (5%)
  other arithmetic  3.18 us (1%)
    ppermute x28, starting transfers between devices, permute(): return lax.ppermute(value, AXES, pairs)  137 us
    ppermute x28, waiting for transfers between devices, permute(): return lax.ppermute(value, AXES, pairs)  52.5 us
    unnamed x43, local copies, waits for them, and re-layouts  8.48 us
    pallas_call x4, Pallas kernels, mix(): pl.pallas_call(functools.partial(mix_kernel, rows=rows, trials=trials, la...  7.98 us
  transfers between devices with their start and end apart: 28, of which 15 were waited for; matrix products, arithmetic and copies ran while one was open for 5% of the time, Pallas kernels for 2%

profile of v1, /device:TPU:35, one launch (start us, length us, event | category | flops | bytes accessed | tf_op | source)
XLA Modules:
  0.0 223.0 jit_solution(4924264292548659975)
XLA Ops:
  0.6 1.5 copy.26
  2.3 2.6 %collective-permute-start.7 = (bf16[4,256,256]{2,1,0:T(8,128)(2,1)S(1)}, bf16[4,256,256]{2,1,0:T(8,128)(2,1)S(1)}, u32[]{:S(2)}, u32[]{:S(2)}) collective-permute-start(bf16[4,256,256]{2,1,0:T(8,128)(2,1)S(1)} %get-tuple-element.51), channel_id=1, source_target_pairs={{0,1},{1,0},{2,3},{3,2},{4,5},{5,4},{6,7},{7,6},{8,9},{9,8},{10,11... | collective-permute-start | bytes 1572872 | tf_op jit(solution)/shard_map/ppermute | solution.py:27
  6.1 21.4 %collective-permute-start.1 = (bf16[1,136,256]{2,1,0:T(8,128)(2,1)S(1)}, bf16[1,136,256]{2,1,0:T(8,128)(2,1)S(1)}, u32[]{:S(2)}, u32[]{:S(2)}) collective-permute-start(bf16[1,136,256]{2,1,0:T(8,128)(2,1)S(1)} %bitcast.33), channel_id=1, source_target_pairs={{0,32},{1,33},{2,34},{3,35},{4,36},{5,37},{6,38},{7,39},{8,40},{9,... | collective-permute-start | bytes 208904 | tf_op jit(solution)/shard_map/ppermute | solution.py:27
  27.6 3.1 %collective-permute-start.10 = (bf16[4,256,512]{2,1,0:T(8,128)(2,1)S(1)}, bf16[4,256,512]{2,1,0:T(8,128)(2,1)S(1)}, u32[]{:S(2)}, u32[]{:S(2)}) collective-permute-start(bf16[4,256,512]{2,1,0:T(8,128)(2,1)S(1)} %pad_maximum_fusion.refs_4_), channel_id=1, source_target_pairs={{0,192},{1,193},{2,194},{3,195},{4,196},{5,197},{6,198},{7,199},{8... | collective-permute-start | bytes 3145736 | tf_op jit(solution)/shard_map/ppermute | solution.py:27
  32.9 2.6 %collective-permute-start.2 = (bf16[2,136,256]{2,1,0:T(8,128)(2,1)}, bf16[2,136,256]{2,1,0:T(8,128)(2,1)}, u32[]{:S(2)}, u32[]{:S(2)}) collective-permute-start(bf16[2,136,256]{2,1,0:T(8,128)(2,1)} %pad_maximum_fusion.3), channel_id=1, source_target_pairs={{0,16},{1,17},{2,18},{3,19},{4,20},{5,21},{6,22},{7,23},{8,24},{9,... | collective-permute-start | bytes 417800 | tf_op jit(solution)/shard_map/ppermute | solution.py:27
  35.5 3.4 %collective-permute-start.8 = (bf16[4,256,512]{2,1,0:T(8,128)(2,1)S(1)}, bf16[4,256,512]{2,1,0:T(8,128)(2,1)S(1)}, u32[]{:S(2)}, u32[]{:S(2)}) collective-permute-start(bf16[4,256,512]{2,1,0:T(8,128)(2,1)S(1)} %pad_maximum_fusion.refs_4_), channel_id=1, source_target_pairs={{0,64},{1,65},{2,66},{3,67},{4,68},{5,69},{6,70},{7,71},{8,72},{9,... | collective-permute-start | bytes 3145736 | tf_op jit(solution)/shard_map/ppermute | solution.py:27
  38.9 2.1 collective-permute-start.9
  41.1 1.6 reshape.48.u_ref
  42.7 1.6 reshape.49.v_ref
  44.3 1.6 reshape.50.a_ref
  49.5 1.0 pad_maximum_fusion.1.refs_0_
  50.5 3.2 %collective-permute-start.11 = (bf16[4,136,256]{2,1,0:T(8,128)(2,1)S(1)}, bf16[4,136,256]{2,1,0:T(8,128)(2,1)S(1)}, u32[]{:S(2)}, u32[]{:S(2)}) collective-permute-start(bf16[4,136,256]{2,1,0:T(8,128)(2,1)S(1)} %pad_maximum_fusion.1.refs_0_), channel_id=1, source_target_pairs={{0,2},{1,3},{2,0},{3,1},{4,6},{5,7},{6,4},{7,5},{8,10},{9,11},{10,... | collective-permute-start | bytes 835592 | tf_op jit(solution)/shard_map/ppermute | solution.py:27
  53.7 4.5 %collective-permute-start.12 = (bf16[4,136,256]{2,1,0:T(8,128)(2,1)S(1)}, bf16[4,136,256]{2,1,0:T(8,128)(2,1)S(1)}, u32[]{:S(2)}, u32[]{:S(2)}) collective-permute-start(bf16[4,136,256]{2,1,0:T(8,128)(2,1)S(1)} %pad_maximum_fusion.1.refs_0_), channel_id=1, source_target_pairs={{0,4},{1,5},{2,6},{3,7},{4,0},{5,1},{6,2},{7,3},{8,12},{9,13},{10,... | collective-permute-start | bytes 835592 | tf_op jit(solution)/shard_map/ppermute | solution.py:27
  58.3 6.2 %collective-permute-start.3 = (bf16[4,136,256]{2,1,0:T(8,128)(2,1)S(1)}, bf16[4,136,256]{2,1,0:T(8,128)(2,1)S(1)}, u32[]{:S(2)}, u32[]{:S(2)}) collective-permute-start(bf16[4,136,256]{2,1,0:T(8,128)(2,1)S(1)} %pad_maximum_fusion.1.refs_0_), channel_id=1, source_target_pairs={{0,8},{1,9},{2,10},{3,11},{4,12},{5,13},{6,14},{7,15},{8,0},{9,1},... | collective-permute-start | bytes 835592 | tf_op jit(solution)/shard_map/ppermute | solution.py:27
  64.9 4.3 %collective-permute-start.13 = (bf16[4,136,256]{2,1,0:T(8,128)(2,1)S(1)}, bf16[4,136,256]{2,1,0:T(8,128)(2,1)S(1)}, u32[]{:S(2)}, u32[]{:S(2)}) collective-permute-start(bf16[4,136,256]{2,1,0:T(8,128)(2,1)S(1)} %pad_maximum_fusion.1.refs_0_), channel_id=1, source_target_pairs={{0,6},{1,7},{2,4},{3,5},{4,2},{5,3},{6,0},{7,1},{8,14},{9,15},{10,... | collective-permute-start | bytes 835592 | tf_op jit(solution)/shard_map/ppermute | solution.py:27
  69.3 2.8 %collective-permute-start.4 = (bf16[4,136,256]{2,1,0:T(8,128)(2,1)S(1)}, bf16[4,136,256]{2,1,0:T(8,128)(2,1)S(1)}, u32[]{:S(2)}, u32[]{:S(2)}) collective-permute-start(bf16[4,136,256]{2,1,0:T(8,128)(2,1)S(1)} %collective-permute-done.3.refs_0_), channel_id=1, source_target_pairs={{0,2},{1,3},{2,0},{3,1},{4,6},{5,7},{6,4},{7,5},{8,10},{9,11},{10,... | collective-permute-start | bytes 835592 | tf_op jit(solution)/shard_map/ppermute | solution.py:27
  72.0 1.6 collective-permute-done.13.refs_3_
  73.7 4.3 %collective-permute-start.5 = (bf16[4,136,256]{2,1,0:T(8,128)(2,1)S(1)}, bf16[4,136,256]{2,1,0:T(8,128)(2,1)S(1)}, u32[]{:S(2)}, u32[]{:S(2)}) collective-permute-start(bf16[4,136,256]{2,1,0:T(8,128)(2,1)S(1)} %collective-permute-done.3.refs_0_), channel_id=1, source_target_pairs={{0,4},{1,5},{2,6},{3,7},{4,0},{5,1},{6,2},{7,3},{8,12},{9,13},{10,... | collective-permute-start | bytes 835592 | tf_op jit(solution)/shard_map/ppermute | solution.py:27
  78.0 2.5 %collective-permute-start.6 = (bf16[4,136,256]{2,1,0:T(8,128)(2,1)S(1)}, bf16[4,136,256]{2,1,0:T(8,128)(2,1)S(1)}, u32[]{:S(2)}, u32[]{:S(2)}) collective-permute-start(bf16[4,136,256]{2,1,0:T(8,128)(2,1)S(1)} %collective-permute-done.3.refs_0_), channel_id=1, source_target_pairs={{0,6},{1,7},{2,4},{3,5},{4,2},{5,3},{6,0},{7,1},{8,14},{9,15},{10,... | collective-permute-start | bytes 835592 | tf_op jit(solution)/shard_map/ppermute | solution.py:27
  80.6 1.4 collective-permute-done.9.refs_6_
  82.0 2.0 mix_early.2
  84.8 6.9 %collective-permute-done.6.refs_3_ = bf16[4,136,256]{2,1,0:T(8,128)(2,1)S(1)} collective-permute-done((bf16[4,136,256]{2,1,0:T(8,128)(2,1)S(1)}, bf16[4,136,256]{2,1,0:T(8,128)(2,1)S(1)}, u32[]{:S(2)}, u32[]{:S(2)}) %collective-permute-start.6) | collective-permute-done | bytes 278560 | tf_op jit(solution)/shard_map/ppermute | solution.py:27
  91.7 2.0 mix_late.2
  93.7 4.0 %collective-permute-start.14 = (f32[2,136,256]{2,1,0:T(8,128)S(1)}, f32[2,136,256]{2,1,0:T(8,128)S(1)}, u32[]{:S(2)}, u32[]{:S(2)}) collective-permute-start(f32[2,136,256]{2,1,0:T(8,128)S(1)} %get-tuple-element.31), channel_id=1, source_target_pairs={{0,1},{1,0},{2,3},{3,2},{4,5},{5,4},{6,7},{7,6},{8,9},{9,8},{10,11... | collective-permute-start | bytes 835592 | tf_op jit(solution)/shard_map/ppermute | solution.py:27
  97.7 1.2 collective-permute-done.14.theirs_ref
  100.2 12.8 %collective-permute-start.15 = (bf16[136,256]{1,0:T(8,128)(2,1)}, bf16[136,256]{1,0:T(8,128)(2,1)}, u32[]{:S(2)}, u32[]{:S(2)}) collective-permute-start(bf16[136,256]{1,0:T(8,128)(2,1)} %get-tuple-element.33), channel_id=1, source_target_pairs={{0,256},{1,257},{2,258},{3,259},{4,260},{5,261},{6,262},{7,263},{8... | collective-permute-start | bytes 208904 | tf_op jit(solution)/shard_map/ppermute | solution.py:27
  113.7 1.8 collective-permute-done.15.came_ref
  121.7 1.2 update.2
  123.7 23.4 %collective-permute-start.17 = (bf16[1,136,256]{2,1,0:T(8,128)(2,1)S(1)}, bf16[1,136,256]{2,1,0:T(8,128)(2,1)S(1)}, u32[]{:S(2)}, u32[]{:S(2)}) collective-permute-start(bf16[1,136,256]{2,1,0:T(8,128)(2,1)S(1)} %bitcast.36), channel_id=1, source_target_pairs={{0,32},{1,33},{2,34},{3,35},{4,36},{5,37},{6,38},{7,39},{8,40},{9,... | collective-permute-start | bytes 208904 | tf_op jit(solution)/shard_map/ppermute | solution.py:27
  147.0 1.7 collective-permute-done.17
  148.7 1.9 collective-permute-start.18
  150.7 4.8 %collective-permute-done.18 = bf16[2,136,256]{2,1,0:T(8,128)(2,1)S(1)} collective-permute-done((bf16[2,136,256]{2,1,0:T(8,128)(2,1)S(1)}, bf16[2,136,256]{2,1,0:T(8,128)(2,1)S(1)}, u32[]{:S(2)}, u32[]{:S(2)}) %collective-permute-start.18) | collective-permute-done | bytes 139296 | tf_op jit(solution)/shard_map/ppermute | solution.py:27
  155.5 1.9 collective-permute-start.19
  157.4 2.3 %collective-permute-start.23 = (bf16[4,136,256]{2,1,0:T(8,128)(2,1)S(1)}, bf16[4,136,256]{2,1,0:T(8,128)(2,1)S(1)}, u32[]{:S(2)}, u32[]{:S(2)}) collective-permute-start(bf16[4,136,256]{2,1,0:T(8,128)(2,1)S(1)} %pad_maximum_fusion.2.refs_0_), channel_id=1, source_target_pairs={{0,2},{1,3},{2,0},{3,1},{4,6},{5,7},{6,4},{7,5},{8,10},{9,11},{10,... | collective-permute-start | bytes 835592 | tf_op jit(solution)/shard_map/ppermute | solution.py:27
  159.7 9.2 %collective-permute-start.24 = (bf16[4,136,256]{2,1,0:T(8,128)(2,1)S(1)}, bf16[4,136,256]{2,1,0:T(8,128)(2,1)S(1)}, u32[]{:S(2)}, u32[]{:S(2)}) collective-permute-start(bf16[4,136,256]{2,1,0:T(8,128)(2,1)S(1)} %pad_maximum_fusion.2.refs_0_), channel_id=1, source_target_pairs={{0,4},{1,5},{2,6},{3,7},{4,0},{5,1},{6,2},{7,3},{8,12},{9,13},{10,... | collective-permute-start | bytes 835592 | tf_op jit(solution)/shard_map/ppermute | solution.py:27
  168.9 1.9 collective-permute-start.25
  170.8 1.9 collective-permute-start.20
  172.7 5.7 %collective-permute-start.21 = (bf16[4,136,256]{2,1,0:T(8,128)(2,1)S(1)}, bf16[4,136,256]{2,1,0:T(8,128)(2,1)S(1)}, u32[]{:S(2)}, u32[]{:S(2)}) collective-permute-start(bf16[4,136,256]{2,1,0:T(8,128)(2,1)S(1)} %collective-permute-done.19.refs_0_), channel_id=1, source_target_pairs={{0,4},{1,5},{2,6},{3,7},{4,0},{5,1},{6,2},{7,3},{8,12},{9,13},{10,... | collective-permute-start | bytes 835592 | tf_op jit(solution)/shard_map/ppermute | solution.py:27
  178.5 1.9 collective-permute-start.22
  180.4 5.2 %collective-permute-done.25.refs_3_ = bf16[4,136,256]{2,1,0:T(8,128)(2,1)S(1)} collective-permute-done((bf16[4,136,256]{2,1,0:T(8,128)(2,1)S(1)}, bf16[4,136,256]{2,1,0:T(8,128)(2,1)S(1)}, u32[]{:S(2)}, u32[]{:S(2)}) %collective-permute-start.25) | collective-permute-done | bytes 278560 | tf_op jit(solution)/shard_map/ppermute | solution.py:27
  185.7 2.0 mix_early.3
  187.7 3.2 %collective-permute-done.21.refs_2_ = bf16[4,136,256]{2,1,0:T(8,128)(2,1)S(1)} collective-permute-done((bf16[4,136,256]{2,1,0:T(8,128)(2,1)S(1)}, bf16[4,136,256]{2,1,0:T(8,128)(2,1)S(1)}, u32[]{:S(2)}, u32[]{:S(2)}) %collective-permute-start.21) | collective-permute-done | bytes 278560 | tf_op jit(solution)/shard_map/ppermute | solution.py:27
  190.9 6.3 %collective-permute-done.22.refs_3_ = bf16[4,136,256]{2,1,0:T(8,128)(2,1)S(1)} collective-permute-done((bf16[4,136,256]{2,1,0:T(8,128)(2,1)S(1)}, bf16[4,136,256]{2,1,0:T(8,128)(2,1)S(1)}, u32[]{:S(2)}, u32[]{:S(2)}) %collective-permute-start.22) | collective-permute-done | bytes 278560 | tf_op jit(solution)/shard_map/ppermute | solution.py:27
  197.2 2.0 mix_late.3
  199.3 2.8 %collective-permute-start.26 = (f32[2,136,256]{2,1,0:T(8,128)S(1)}, f32[2,136,256]{2,1,0:T(8,128)S(1)}, u32[]{:S(2)}, u32[]{:S(2)}) collective-permute-start(f32[2,136,256]{2,1,0:T(8,128)S(1)} %get-tuple-element.43), channel_id=1, source_target_pairs={{0,1},{1,0},{2,3},{3,2},{4,5},{5,4},{6,7},{7,6},{8,9},{9,8},{10,11... | collective-permute-start | bytes 835592 | tf_op jit(solution)/shard_map/ppermute | solution.py:27
  202.0 1.2 collective-permute-done.26.theirs_ref
  203.2 3.0 %collective-permute-start.27 = (bf16[136,256]{1,0:T(8,128)(2,1)S(1)}, bf16[136,256]{1,0:T(8,128)(2,1)S(1)}, u32[]{:S(2)}, u32[]{:S(2)}) collective-permute-start(bf16[136,256]{1,0:T(8,128)(2,1)S(1)} %get-tuple-element.45), channel_id=1, source_target_pairs={{0,256},{1,257},{2,258},{3,259},{4,260},{5,261},{6,262},{7,263},{8... | collective-permute-start | bytes 208904 | tf_op jit(solution)/shard_map/ppermute | solution.py:27
  206.3 15.1 %collective-permute-done.27.came_ref = bf16[136,256]{1,0:T(8,128)(2,1)S(1)} collective-permute-done((bf16[136,256]{1,0:T(8,128)(2,1)S(1)}, bf16[136,256]{1,0:T(8,128)(2,1)S(1)}, u32[]{:S(2)}, u32[]{:S(2)}) %collective-permute-start.27) | collective-permute-done | bytes 69664 | tf_op jit(solution)/shard_map/ppermute | solution.py:27
  (86 shorter events, 19.0 us)
Async XLA Ops:
  0.6 5.3 %copy-start = (bf16[700,256]{1,0:T(8,128)(2,1)S(1)}, bf16[700,256]{1,0:T(8,128)(2,1)}, u32[]{:S(2)}) copy-start(bf16[700,256]{1,0:T(8,128)(2,1)} %param.20) | copy-start | bytes 1075204
  2.2 2.7 %copy-start.16 = (bf16[64,4,256]{2,1,0:T(4,128)(2,1)S(1)}, bf16[64,4,256]{2,1,0:T(4,128)(2,1)}, u32[]{:S(2)}) copy-start(bf16[64,4,256]{2,1,0:T(4,128)(2,1)} %param.19) | copy-start | bytes 393220
  2.2 2.8 %copy-start.17 = (bf16[64,2,256]{2,1,0:T(2,128)(2,1)S(1)}, bf16[64,2,256]{2,1,0:T(2,128)(2,1)}, u32[]{:S(2)}) copy-start(bf16[64,2,256]{2,1,0:T(2,128)(2,1)} %param.16) | copy-start | bytes 196612
  2.2 3.7 %copy-start.18 = (s32[2,2,700]{2,1,0:T(2,128)S(1)}, s32[2,2,700]{2,1,0:T(2,128)}, u32[]{:S(2)}) copy-start(s32[2,2,700]{2,1,0:T(2,128)} %param.21) | copy-start | bytes 33604
  2.3 25.2 %collective-permute-start.7 = (bf16[4,256,256]{2,1,0:T(8,128)(2,1)S(1)}, bf16[4,256,256]{2,1,0:T(8,128)(2,1)S(1)}, u32[]{:S(2)}, u32[]{:S(2)}) collective-permute-start(bf16[4,256,256]{2,1,0:T(8,128)(2,1)S(1)} %get-tuple-element.51), channel_id=1, source_target_pairs={{0,1},{1,0},{2,3},{3,2},{4,5},{5,4},{6,7},{7,6},{8,9},{9,8},{10,11... | collective-permute-start | bytes 1572872 | tf_op jit(solution)/shard_map/ppermute | solution.py:27
  5.0 22.6 %copy-start.1 = (bf16[256,256]{1,0:T(8,128)(2,1)}, bf16[256,256]{1,0:T(8,128)(2,1)S(1)}, u32[]{:S(2)}) copy-start(bf16[256,256]{1,0:T(8,128)(2,1)S(1)} %reshape.47.factors_ref.f_ref) | copy-start | bytes 393220
  5.2 22.3 %copy-start.10 = (bf16[136,256]{1,0:T(8,128)(2,1)}, bf16[136,256]{1,0:T(8,128)(2,1)S(1)}, u32[]{:S(2)}) copy-start(bf16[136,256]{1,0:T(8,128)(2,1)S(1)} %pack.1.packed_ref) | copy-start | bytes 208900
  5.2 0.9 collective-permute-start
  6.1 26.8 %copy-start.14 = (bf16[136,256]{1,0:T(8,128)(2,1)}, bf16[136,256]{1,0:T(8,128)(2,1)S(1)}, u32[]{:S(2)}) copy-start(bf16[136,256]{1,0:T(8,128)(2,1)S(1)} %collective-permute-done) | copy-start | bytes 208900
  6.1 26.1 %collective-permute-start.1 = (bf16[1,136,256]{2,1,0:T(8,128)(2,1)S(1)}, bf16[1,136,256]{2,1,0:T(8,128)(2,1)S(1)}, u32[]{:S(2)}, u32[]{:S(2)}) collective-permute-start(bf16[1,136,256]{2,1,0:T(8,128)(2,1)S(1)} %bitcast.33), channel_id=1, source_target_pairs={{0,32},{1,33},{2,34},{3,35},{4,36},{5,37},{6,38},{7,39},{8,40},{9,... | collective-permute-start | bytes 208904 | tf_op jit(solution)/shard_map/ppermute | solution.py:27
  27.5 3.2 %copy-start.20 = (s32[64]{0:T(128)S(1)}, s32[64]{0:T(128)}, u32[]{:S(2)}) copy-start(s32[64]{0:T(128)} %param.23) | copy-start | bytes 772
  27.6 18.3 %copy-start.19 = (s32[64,2]{0,1:T(2,128)S(1)}, s32[64,2]{0,1:T(2,128)}, u32[]{:S(2)}) copy-start(s32[64,2]{0,1:T(2,128)} %param.22) | copy-start | bytes 1540
  27.6 50.4 %collective-permute-start.10 = (bf16[4,256,512]{2,1,0:T(8,128)(2,1)S(1)}, bf16[4,256,512]{2,1,0:T(8,128)(2,1)S(1)}, u32[]{:S(2)}, u32[]{:S(2)}) collective-permute-start(bf16[4,256,512]{2,1,0:T(8,128)(2,1)S(1)} %pad_maximum_fusion.refs_4_), channel_id=1, source_target_pairs={{0,192},{1,193},{2,194},{3,195},{4,196},{5,197},{6,198},{7,199},{8... | collective-permute-start | bytes 3145736 | tf_op jit(solution)/shard_map/ppermute | solution.py:27
  32.2 0.7 copy-start.15
  32.9 16.6 %collective-permute-start.2 = (bf16[2,136,256]{2,1,0:T(8,128)(2,1)}, bf16[2,136,256]{2,1,0:T(8,128)(2,1)}, u32[]{:S(2)}, u32[]{:S(2)}) collective-permute-start(bf16[2,136,256]{2,1,0:T(8,128)(2,1)} %pad_maximum_fusion.3), channel_id=1, source_target_pairs={{0,16},{1,17},{2,18},{3,19},{4,20},{5,21},{6,22},{7,23},{8,24},{9,... | collective-permute-start | bytes 417800 | tf_op jit(solution)/shard_map/ppermute | solution.py:27
  35.5 45.1 %collective-permute-start.8 = (bf16[4,256,512]{2,1,0:T(8,128)(2,1)S(1)}, bf16[4,256,512]{2,1,0:T(8,128)(2,1)S(1)}, u32[]{:S(2)}, u32[]{:S(2)}) collective-permute-start(bf16[4,256,512]{2,1,0:T(8,128)(2,1)S(1)} %pad_maximum_fusion.refs_4_), channel_id=1, source_target_pairs={{0,64},{1,65},{2,66},{3,67},{4,68},{5,69},{6,70},{7,71},{8,72},{9,... | collective-permute-start | bytes 3145736 | tf_op jit(solution)/shard_map/ppermute | solution.py:27
  38.9 43.1 %collective-permute-start.9 = (bf16[4,256,512]{2,1,0:T(8,128)(2,1)S(1)}, bf16[4,256,512]{2,1,0:T(8,128)(2,1)}, u32[]{:S(2)}, u32[]{:S(2)}) collective-permute-start(bf16[4,256,512]{2,1,0:T(8,128)(2,1)S(1)} %pad_maximum_fusion.refs_4_), channel_id=1, source_target_pairs={{0,128},{1,129},{2,130},{3,131},{4,132},{5,133},{6,134},{7,135},{8... | collective-permute-start | bytes 3145736 | tf_op jit(solution)/shard_map/ppermute | solution.py:27
  50.5 7.8 %collective-permute-start.11 = (bf16[4,136,256]{2,1,0:T(8,128)(2,1)S(1)}, bf16[4,136,256]{2,1,0:T(8,128)(2,1)S(1)}, u32[]{:S(2)}, u32[]{:S(2)}) collective-permute-start(bf16[4,136,256]{2,1,0:T(8,128)(2,1)S(1)} %pad_maximum_fusion.1.refs_0_), channel_id=1, source_target_pairs={{0,2},{1,3},{2,0},{3,1},{4,6},{5,7},{6,4},{7,5},{8,10},{9,11},{10,... | collective-permute-start | bytes 835592 | tf_op jit(solution)/shard_map/ppermute | solution.py:27
  53.7 11.2 %collective-permute-start.12 = (bf16[4,136,256]{2,1,0:T(8,128)(2,1)S(1)}, bf16[4,136,256]{2,1,0:T(8,128)(2,1)S(1)}, u32[]{:S(2)}, u32[]{:S(2)}) collective-permute-start(bf16[4,136,256]{2,1,0:T(8,128)(2,1)S(1)} %pad_maximum_fusion.1.refs_0_), channel_id=1, source_target_pairs={{0,4},{1,5},{2,6},{3,7},{4,0},{5,1},{6,2},{7,3},{8,12},{9,13},{10,... | collective-permute-start | bytes 835592 | tf_op jit(solution)/shard_map/ppermute | solution.py:27
  58.3 11.0 %collective-permute-start.3 = (bf16[4,136,256]{2,1,0:T(8,128)(2,1)S(1)}, bf16[4,136,256]{2,1,0:T(8,128)(2,1)S(1)}, u32[]{:S(2)}, u32[]{:S(2)}) collective-permute-start(bf16[4,136,256]{2,1,0:T(8,128)(2,1)S(1)} %pad_maximum_fusion.1.refs_0_), channel_id=1, source_target_pairs={{0,8},{1,9},{2,10},{3,11},{4,12},{5,13},{6,14},{7,15},{8,0},{9,1},... | collective-permute-start | bytes 835592 | tf_op jit(solution)/shard_map/ppermute | solution.py:27
  64.9 8.7 %collective-permute-start.13 = (bf16[4,136,256]{2,1,0:T(8,128)(2,1)S(1)}, bf16[4,136,256]{2,1,0:T(8,128)(2,1)S(1)}, u32[]{:S(2)}, u32[]{:S(2)}) collective-permute-start(bf16[4,136,256]{2,1,0:T(8,128)(2,1)S(1)} %pad_maximum_fusion.1.refs_0_), channel_id=1, source_target_pairs={{0,6},{1,7},{2,4},{3,5},{4,2},{5,3},{6,0},{7,1},{8,14},{9,15},{10,... | collective-permute-start | bytes 835592 | tf_op jit(solution)/shard_map/ppermute | solution.py:27
  69.3 14.7 %collective-permute-start.4 = (bf16[4,136,256]{2,1,0:T(8,128)(2,1)S(1)}, bf16[4,136,256]{2,1,0:T(8,128)(2,1)S(1)}, u32[]{:S(2)}, u32[]{:S(2)}) collective-permute-start(bf16[4,136,256]{2,1,0:T(8,128)(2,1)S(1)} %collective-permute-done.3.refs_0_), channel_id=1, source_target_pairs={{0,2},{1,3},{2,0},{3,1},{4,6},{5,7},{6,4},{7,5},{8,10},{9,11},{10,... | collective-permute-start | bytes 835592 | tf_op jit(solution)/shard_map/ppermute | solution.py:27
  73.7 11.1 %collective-permute-start.5 = (bf16[4,136,256]{2,1,0:T(8,128)(2,1)S(1)}, bf16[4,136,256]{2,1,0:T(8,128)(2,1)S(1)}, u32[]{:S(2)}, u32[]{:S(2)}) collective-permute-start(bf16[4,136,256]{2,1,0:T(8,128)(2,1)S(1)} %collective-permute-done.3.refs_0_), channel_id=1, source_target_pairs={{0,4},{1,5},{2,6},{3,7},{4,0},{5,1},{6,2},{7,3},{8,12},{9,13},{10,... | collective-permute-start | bytes 835592 | tf_op jit(solution)/shard_map/ppermute | solution.py:27
  78.0 13.7 %collective-permute-start.6 = (bf16[4,136,256]{2,1,0:T(8,128)(2,1)S(1)}, bf16[4,136,256]{2,1,0:T(8,128)(2,1)S(1)}, u32[]{:S(2)}, u32[]{:S(2)}) collective-permute-start(bf16[4,136,256]{2,1,0:T(8,128)(2,1)S(1)} %collective-permute-done.3.refs_0_), channel_id=1, source_target_pairs={{0,6},{1,7},{2,4},{3,5},{4,2},{5,3},{6,0},{7,1},{8,14},{9,15},{10,... | collective-permute-start | bytes 835592 | tf_op jit(solution)/shard_map/ppermute | solution.py:27
  93.7 5.2 %collective-permute-start.14 = (f32[2,136,256]{2,1,0:T(8,128)S(1)}, f32[2,136,256]{2,1,0:T(8,128)S(1)}, u32[]{:S(2)}, u32[]{:S(2)}) collective-permute-start(f32[2,136,256]{2,1,0:T(8,128)S(1)} %get-tuple-element.31), channel_id=1, source_target_pairs={{0,1},{1,0},{2,3},{3,2},{4,5},{5,4},{6,7},{7,6},{8,9},{9,8},{10,11... | collective-permute-start | bytes 835592 | tf_op jit(solution)/shard_map/ppermute | solution.py:27
  100.2 15.3 %collective-permute-start.15 = (bf16[136,256]{1,0:T(8,128)(2,1)}, bf16[136,256]{1,0:T(8,128)(2,1)}, u32[]{:S(2)}, u32[]{:S(2)}) collective-permute-start(bf16[136,256]{1,0:T(8,128)(2,1)} %get-tuple-element.33), channel_id=1, source_target_pairs={{0,256},{1,257},{2,258},{3,259},{4,260},{5,261},{6,262},{7,263},{8... | collective-permute-start | bytes 208904 | tf_op jit(solution)/shard_map/ppermute | solution.py:27
  115.5 0.9 copy-start.2
  116.4 0.9 copy-start.4
  117.3 0.8 copy-start.6
  118.1 0.9 copy-start.8
  119.0 0.9 copy-start.9
  119.9 0.9 copy-start.11
  120.8 0.9 copy-start.13
  123.0 0.7 collective-permute-start.16
  123.7 25.1 %collective-permute-start.17 = (bf16[1,136,256]{2,1,0:T(8,128)(2,1)S(1)}, bf16[1,136,256]{2,1,0:T(8,128)(2,1)S(1)}, u32[]{:S(2)}, u32[]{:S(2)}) collective-permute-start(bf16[1,136,256]{2,1,0:T(8,128)(2,1)S(1)} %bitcast.36), channel_id=1, source_target_pairs={{0,32},{1,33},{2,34},{3,35},{4,36},{5,37},{6,38},{7,39},{8,40},{9,... | collective-permute-start | bytes 208904 | tf_op jit(solution)/shard_map/ppermute | solution.py:27
  148.7 6.7 %collective-permute-start.18 = (bf16[2,136,256]{2,1,0:T(8,128)(2,1)S(1)}, bf16[2,136,256]{2,1,0:T(8,128)(2,1)S(1)}, u32[]{:S(2)}, u32[]{:S(2)}) collective-permute-start(bf16[2,136,256]{2,1,0:T(8,128)(2,1)S(1)} %pad_maximum_fusion.4), channel_id=1, source_target_pairs={{0,16},{1,17},{2,18},{3,19},{4,20},{5,21},{6,22},{7,23},{8,24},{9,... | collective-permute-start | bytes 417800 | tf_op jit(solution)/shard_map/ppermute | solution.py:27
  155.5 15.4 %collective-permute-start.19 = (bf16[4,136,256]{2,1,0:T(8,128)(2,1)S(1)}, bf16[4,136,256]{2,1,0:T(8,128)(2,1)S(1)}, u32[]{:S(2)}, u32[]{:S(2)}) collective-permute-start(bf16[4,136,256]{2,1,0:T(8,128)(2,1)S(1)} %pad_maximum_fusion.2.refs_0_), channel_id=1, source_target_pairs={{0,8},{1,9},{2,10},{3,11},{4,12},{5,13},{6,14},{7,15},{8,0},{9,1},... | collective-permute-start | bytes 835592 | tf_op jit(solution)/shard_map/ppermute | solution.py:27
  157.4 21.1 %collective-permute-start.23 = (bf16[4,136,256]{2,1,0:T(8,128)(2,1)S(1)}, bf16[4,136,256]{2,1,0:T(8,128)(2,1)S(1)}, u32[]{:S(2)}, u32[]{:S(2)}) collective-permute-start(bf16[4,136,256]{2,1,0:T(8,128)(2,1)S(1)} %pad_maximum_fusion.2.refs_0_), channel_id=1, source_target_pairs={{0,2},{1,3},{2,0},{3,1},{4,6},{5,7},{6,4},{7,5},{8,10},{9,11},{10,... | collective-permute-start | bytes 835592 | tf_op jit(solution)/shard_map/ppermute | solution.py:27
  159.7 20.8 %collective-permute-start.24 = (bf16[4,136,256]{2,1,0:T(8,128)(2,1)S(1)}, bf16[4,136,256]{2,1,0:T(8,128)(2,1)S(1)}, u32[]{:S(2)}, u32[]{:S(2)}) collective-permute-start(bf16[4,136,256]{2,1,0:T(8,128)(2,1)S(1)} %pad_maximum_fusion.2.refs_0_), channel_id=1, source_target_pairs={{0,4},{1,5},{2,6},{3,7},{4,0},{5,1},{6,2},{7,3},{8,12},{9,13},{10,... | collective-permute-start | bytes 835592 | tf_op jit(solution)/shard_map/ppermute | solution.py:27
  168.9 16.8 %collective-permute-start.25 = (bf16[4,136,256]{2,1,0:T(8,128)(2,1)S(1)}, bf16[4,136,256]{2,1,0:T(8,128)(2,1)S(1)}, u32[]{:S(2)}, u32[]{:S(2)}) collective-permute-start(bf16[4,136,256]{2,1,0:T(8,128)(2,1)S(1)} %pad_maximum_fusion.2.refs_0_), channel_id=1, source_target_pairs={{0,6},{1,7},{2,4},{3,5},{4,2},{5,3},{6,0},{7,1},{8,14},{9,15},{10,... | collective-permute-start | bytes 835592 | tf_op jit(solution)/shard_map/ppermute | solution.py:27
  170.8 16.9 %collective-permute-start.20 = (bf16[4,136,256]{2,1,0:T(8,128)(2,1)S(1)}, bf16[4,136,256]{2,1,0:T(8,128)(2,1)S(1)}, u32[]{:S(2)}, u32[]{:S(2)}) collective-permute-start(bf16[4,136,256]{2,1,0:T(8,128)(2,1)S(1)} %collective-permute-done.19.refs_0_), channel_id=1, source_target_pairs={{0,2},{1,3},{2,0},{3,1},{4,6},{5,7},{6,4},{7,5},{8,10},{9,11},{10,... | collective-permute-start | bytes 835592 | tf_op jit(solution)/shard_map/ppermute | solution.py:27
  172.7 18.2 %collective-permute-start.21 = (bf16[4,136,256]{2,1,0:T(8,128)(2,1)S(1)}, bf16[4,136,256]{2,1,0:T(8,128)(2,1)S(1)}, u32[]{:S(2)}, u32[]{:S(2)}) collective-permute-start(bf16[4,136,256]{2,1,0:T(8,128)(2,1)S(1)} %collective-permute-done.19.refs_0_), channel_id=1, source_target_pairs={{0,4},{1,5},{2,6},{3,7},{4,0},{5,1},{6,2},{7,3},{8,12},{9,13},{10,... | collective-permute-start | bytes 835592 | tf_op jit(solution)/shard_map/ppermute | solution.py:27
  178.5 18.7 %collective-permute-start.22 = (bf16[4,136,256]{2,1,0:T(8,128)(2,1)S(1)}, bf16[4,136,256]{2,1,0:T(8,128)(2,1)S(1)}, u32[]{:S(2)}, u32[]{:S(2)}) collective-permute-start(bf16[4,136,256]{2,1,0:T(8,128)(2,1)S(1)} %collective-permute-done.19.refs_0_), channel_id=1, source_target_pairs={{0,6},{1,7},{2,4},{3,5},{4,2},{5,3},{6,0},{7,1},{8,14},{9,15},{10,... | collective-permute-start | bytes 835592 | tf_op jit(solution)/shard_map/ppermute | solution.py:27
  197.2 24.1 %copy-start.3 = (bf16[256,256]{1,0:T(8,128)(2,1)S(1)}, bf16[256,256]{1,0:T(8,128)(2,1)}, u32[]{:S(2)}) copy-start(bf16[256,256]{1,0:T(8,128)(2,1)} %copy-done.1) | copy-start | bytes 393220
  197.2 24.1 %copy-start.5 = (bf16[256,256]{1,0:T(8,128)(2,1)S(1)}, bf16[256,256]{1,0:T(8,128)(2,1)}, u32[]{:S(2)}) copy-start(bf16[256,256]{1,0:T(8,128)(2,1)} %reshape.48.u_ref) | copy-start | bytes 393220
  197.2 24.1 %copy-start.7 = (f32[128,2]{1,0:T(8,128)S(1)}, f32[128,2]{1,0:T(8,128)}, u32[]{:S(2)}) copy-start(f32[128,2]{1,0:T(8,128)} %copy.29.cols_ref) | copy-start | bytes 3076
  199.3 3.9 %collective-permute-start.26 = (f32[2,136,256]{2,1,0:T(8,128)S(1)}, f32[2,136,256]{2,1,0:T(8,128)S(1)}, u32[]{:S(2)}, u32[]{:S(2)}) collective-permute-start(f32[2,136,256]{2,1,0:T(8,128)S(1)} %get-tuple-element.43), channel_id=1, source_target_pairs={{0,1},{1,0},{2,3},{3,2},{4,5},{5,4},{6,7},{7,6},{8,9},{9,8},{10,11... | collective-permute-start | bytes 835592 | tf_op jit(solution)/shard_map/ppermute | solution.py:27
  203.2 18.1 %collective-permute-start.27 = (bf16[136,256]{1,0:T(8,128)(2,1)S(1)}, bf16[136,256]{1,0:T(8,128)(2,1)S(1)}, u32[]{:S(2)}, u32[]{:S(2)}) collective-permute-start(bf16[136,256]{1,0:T(8,128)(2,1)S(1)} %get-tuple-element.45), channel_id=1, source_target_pairs={{0,256},{1,257},{2,258},{3,259},{4,260},{5,261},{6,262},{7,263},{8... | collective-permute-start | bytes 208904 | tf_op jit(solution)/shard_map/ppermute | solution.py:27
  (1 other events, 0.6 us)

commit v2 on v1

--- a/solution.py
+++ b/solution.py
@@ -110,10 +110,20 @@
     )(spikes, factors)
 
 
-def update_kernel(
-    keep_ref, came_ref, packed_ref, v_ref, a_ref, lanes_ref, cols_ref, u_ref, f_ref, *outs, **sizes
-):
-    step, trials, rank = sizes["step"], sizes["trials"], sizes["rank"]
+def to_column(value, rows, trials):
+    shape = (rows, value.shape[1])
+    row = lax.broadcasted_iota(jnp.int32, shape, 0)
+    kept = row // trials == lax.broadcasted_iota(jnp.int32, shape, 1)
+    if value.shape[0] == 1:
+        spread = jnp.broadcast_to(value, shape)
+    else:
+        spread = by_trial(value, rows)
+    return jnp.sum(jnp.where(kept, spread, 0.0), axis=1, keepdims=True)
+
+
+def update_kernel(*refs, step, trials, rank):
+    keep_ref, came_ref, packed_ref, v_ref, a_ref, lanes_ref, ids_ref, count_ref = refs[:8]
+    u_ref, f_ref, outs = refs[8], refs[9], refs[10:]
     rows, _ = v_ref.shape
     total = keep_ref[:rows] + came_ref[:rows].astype(jnp.float32)
     tail = came_ref[rows:].astype(jnp.float32)
@@ -124,37 +134,39 @@
     spread = jnp.where(mask, by_trial(proj, rows), 0.0).astype(jnp.bfloat16)
     low = jnp.dot(spread, u_ref[...], preferred_element_type=jnp.float32)
     current = by_trial(lanes_ref[4 + step * trials : 4 + (step + 1) * trials], rows)
-    drive = total + cols_ref[:, :1] * low + current
+    half_sign = to_column(0.5 - (ids_ref[...] & 1).astype(jnp.float32), rows, trials)
+    count = to_column(count_ref[...].astype(jnp.float32), rows, trials)
+    drive = total + half_sign * low + current
     decay_mem, decay_adapt = lanes_ref[0:1], lanes_ref[1:2]
     base, adapt = lanes_ref[2:3], lanes_ref[3:4]
     spikes = packed_ref[:rows].astype(jnp.float32)
     v, a = v_ref[...], a_ref[...]
     v_new = decay_mem * v + (1.0 - decay_mem) * drive - spikes * (base + adapt * a)
-    a_new = decay_adapt * a + (1.0 - decay_adapt) * spikes
-    active = cols_ref[:, 1:2] > float(step)
+    active = count > float(step)
     v = jnp.where(active, v_new, v)
-    a = jnp.where(active, a_new, a)
     outs[0][...] = v
-    outs[1][...] = a
-    if len(outs) > 2:
+    if len(outs) > 1:
+        a_new = decay_adapt * a + (1.0 - decay_adapt) * spikes
+        a = jnp.where(active, a_new, a)
+        outs[1][...] = a
         fresh = jax.nn.sigmoid(3.0 * (v - base - adapt * a)).astype(jnp.bfloat16)
         store_packed(outs[2], fresh, f_ref[...], trials, rank)
 
 
-def update(keep, came, packed, v, a, lanes, cols, u_rows, f_rows, step, trials, rank):
+def update(keep, came, packed, v, a, lanes, ids, count, u_rows, f_rows, step, trials, rank):
     state = jax.ShapeDtypeStruct(v.shape, jnp.float32)
-    outs = [state, state]
+    outs = [state]
     if step + 1 < STEPS:
-        outs.append(jax.ShapeDtypeStruct(packed.shape, packed.dtype))
+        outs += [state, jax.ShapeDtypeStruct(packed.shape, packed.dtype)]
     whole = pl.BlockSpec(memory_space=pltpu.VMEM)
     return pl.pallas_call(
         functools.partial(update_kernel, step=step, trials=trials, rank=rank),
         out_shape=tuple(outs),
-        in_specs=[whole] * 9,
+        in_specs=[whole] * 10,
         out_specs=(whole,) * len(outs),
         compiler_params=pltpu.CompilerParams(vmem_limit_bytes=6 << 20),
         name="update",
-    )(keep, came, packed, v, a, lanes, cols, u_rows, f_rows)
+    )(keep, came, packed, v, a, lanes, ids, count, u_rows, f_rows)
 
 
 def mix_kernel(at_ref, *refs, rows, trials, late):
@@ -277,10 +289,8 @@
     at = {name: lax.axis_index(name) for name in AXES}
     u_rows = factor_u.reshape(members * rank, block)
     f_rows = factor_v.reshape(members * rank, block)
-    half_sign = 0.5 * (1 - 2 * (member_ids % 2)).astype(jnp.float32)
-    cols = jnp.stack(
-        [jnp.repeat(half_sign, trials), step_count.reshape(rows).astype(jnp.float32)], axis=1
-    )
+    ids = member_ids.reshape(1, members)
+    count = step_count.T
     current = jnp.dot(
         spikes_in.reshape(STEPS * trials, -1).astype(jnp.bfloat16),
         in_weight,
@@ -299,8 +309,15 @@
         other = over_b(held, 2)
         held = jnp.concatenate([held, other], axis=0)
         if step == 0:
-            ready = (held, place, lanes, cols, u_rows, v, a)
-            held, place, lanes, cols, u_rows, v, a = lax.optimization_barrier(ready)
+            ready = (held, place, lanes, u_rows, v, a)
+            held, place, lanes, u_rows, v, a = lax.optimization_barrier(ready)
+        if step + 1 == STEPS:
+            spikes_f = packed[:rows].astype(jnp.float32)
+            a_new = decay_adapt * a + (1.0 - decay_adapt) * spikes_f
+            a_new = a_new.reshape(a_init.shape)
+            active = (step_count > step)[:, :, None]
+            a_out = jnp.where(active, a_new, a.reshape(a_init.shape))
+            held, a_out = lax.optimization_barrier((held, a_out))
         early = [held]
         late = [over_b(early[0], 1)]
         for pieces in (early, late):
@@ -311,11 +328,12 @@
         theirs = over_c(theirs)
         keep, give = fold(mine, theirs, rows, trials)
         came = over_zh(give)
-        v, a, *rest = update(
-            keep, came, packed, v, a, lanes, cols, u_rows, f_rows, step, trials, rank
+        v, *rest = update(
+            keep, came, packed, v, a, lanes, ids, count, u_rows, f_rows, step, trials, rank
         )
-        packed = rest[0] if rest else None
-    return (v.reshape(v_init.shape), a.reshape(a_init.shape))
+        if rest:
+            a, packed = rest
+    return (v.reshape(v_init.shape), a_out)
 
 
 def solution(mesh):

time: 224 us -> 217 us (0.969)
  the two profiles are of different devices: /device:TPU:35 before, /device:TPU:65 now
where the time goes in v2:
time: 217 us; the launch traced here: 215 us
  starting transfers between devices  115 us (53%)
  waiting for transfers between devices  68.3 us (31%)
  local copies, waits for them, and re-layouts  12.7 us (6%)
  Pallas kernels  10.4 us (5%)
  other arithmetic  7.17 us (3%)
    ppermute x28, starting transfers between devices, permute(): return lax.ppermute(value, AXES, pairs)  115 us
    ppermute x28, waiting for transfers between devices, permute(): return lax.ppermute(value, AXES, pairs)  68.3 us
    pallas_call x4, Pallas kernels, mix(): pl.pallas_call(functools.partial(mix_kernel, rows=rows, trials=trials, la...  8.07 us
  transfers between devices with their start and end apart: 28, of which 13 were waited for; matrix products, arithmetic and copies ran while one was open for 6% of the time, Pallas kernels for 2%

profile of v2, /device:TPU:65, one launch (start us, length us, event | category | flops | bytes accessed | tf_op | source)
XLA Modules:
  0.0 215.3 jit_solution(14932058329117722248)
XLA Ops:
  2.3 2.6 %collective-permute-start.7 = (bf16[4,256,256]{2,1,0:T(8,128)(2,1)S(1)}, bf16[4,256,256]{2,1,0:T(8,128)(2,1)S(1)}, u32[]{:S(2)}, u32[]{:S(2)}) collective-permute-start(bf16[4,256,256]{2,1,0:T(8,128)(2,1)S(1)} %get-tuple-element.49), channel_id=1, source_target_pairs={{0,1},{1,0},{2,3},{3,2},{4,5},{5,4},{6,7},{7,6},{8,9},{9,8},{10,11... | collective-permute-start | bytes 1572872 | tf_op jit(solution)/shard_map/ppermute | solution.py:27
  6.6 18.9 %collective-permute-start.1 = (bf16[1,136,256]{2,1,0:T(8,128)(2,1)S(1)}, bf16[1,136,256]{2,1,0:T(8,128)(2,1)S(1)}, u32[]{:S(2)}, u32[]{:S(2)}) collective-permute-start(bf16[1,136,256]{2,1,0:T(8,128)(2,1)S(1)} %bitcast.39), channel_id=1, source_target_pairs={{0,32},{1,33},{2,34},{3,35},{4,36},{5,37},{6,38},{7,39},{8,40},{9,... | collective-permute-start | bytes 208904 | tf_op jit(solution)/shard_map/ppermute | solution.py:27
  25.6 4.5 %collective-permute-start.10 = (bf16[4,256,512]{2,1,0:T(8,128)(2,1)S(1)}, bf16[4,256,512]{2,1,0:T(8,128)(2,1)S(1)}, u32[]{:S(2)}, u32[]{:S(2)}) collective-permute-start(bf16[4,256,512]{2,1,0:T(8,128)(2,1)S(1)} %pad_maximum_fusion.refs_4_), channel_id=1, source_target_pairs={{0,192},{1,193},{2,194},{3,195},{4,196},{5,197},{6,198},{7,199},{8... | collective-permute-start | bytes 3145736 | tf_op jit(solution)/shard_map/ppermute | solution.py:27
  30.9 6.4 %collective-permute-start.2 = (bf16[2,136,256]{2,1,0:T(8,128)(2,1)}, bf16[2,136,256]{2,1,0:T(8,128)(2,1)}, u32[]{:S(2)}, u32[]{:S(2)}) collective-permute-start(bf16[2,136,256]{2,1,0:T(8,128)(2,1)} %pad_maximum_fusion.3), channel_id=1, source_target_pairs={{0,16},{1,17},{2,18},{3,19},{4,20},{5,21},{6,22},{7,23},{8,24},{9,... | collective-permute-start | bytes 417800 | tf_op jit(solution)/shard_map/ppermute | solution.py:27
  37.3 3.1 %collective-permute-start.8 = (bf16[4,256,512]{2,1,0:T(8,128)(2,1)S(1)}, bf16[4,256,512]{2,1,0:T(8,128)(2,1)S(1)}, u32[]{:S(2)}, u32[]{:S(2)}) collective-permute-start(bf16[4,256,512]{2,1,0:T(8,128)(2,1)S(1)} %pad_maximum_fusion.refs_4_), channel_id=1, source_target_pairs={{0,64},{1,65},{2,66},{3,67},{4,68},{5,69},{6,70},{7,71},{8,72},{9,... | collective-permute-start | bytes 3145736 | tf_op jit(solution)/shard_map/ppermute | solution.py:27
  40.4 4.3 %collective-permute-start.9 = (bf16[4,256,512]{2,1,0:T(8,128)(2,1)S(1)}, bf16[4,256,512]{2,1,0:T(8,128)(2,1)}, u32[]{:S(2)}, u32[]{:S(2)}) collective-permute-start(bf16[4,256,512]{2,1,0:T(8,128)(2,1)S(1)} %pad_maximum_fusion.refs_4_), channel_id=1, source_target_pairs={{0,128},{1,129},{2,130},{3,131},{4,132},{5,133},{6,134},{7,135},{8... | collective-permute-start | bytes 3145736 | tf_op jit(solution)/shard_map/ppermute | solution.py:27
  44.9 1.6 reshape.45.refs_8_
  46.5 1.6 reshape.46.refs_3_
  48.2 1.6 reshape.47.refs_4_
  51.0 3.2 %collective-permute-start.11 = (bf16[4,136,256]{2,1,0:T(8,128)(2,1)S(1)}, bf16[4,136,256]{2,1,0:T(8,128)(2,1)S(1)}, u32[]{:S(2)}, u32[]{:S(2)}) collective-permute-start(bf16[4,136,256]{2,1,0:T(8,128)(2,1)S(1)} %pad_maximum_fusion.1.refs_0_), channel_id=1, source_target_pairs={{0,2},{1,3},{2,0},{3,1},{4,6},{5,7},{6,4},{7,5},{8,10},{9,11},{10,... | collective-permute-start | bytes 835592 | tf_op jit(solution)/shard_map/ppermute | solution.py:27
  54.2 4.5 %collective-permute-start.12 = (bf16[4,136,256]{2,1,0:T(8,128)(2,1)S(1)}, bf16[4,136,256]{2,1,0:T(8,128)(2,1)S(1)}, u32[]{:S(2)}, u32[]{:S(2)}) collective-permute-start(bf16[4,136,256]{2,1,0:T(8,128)(2,1)S(1)} %pad_maximum_fusion.1.refs_0_), channel_id=1, source_target_pairs={{0,4},{1,5},{2,6},{3,7},{4,0},{5,1},{6,2},{7,3},{8,12},{9,13},{10,... | collective-permute-start | bytes 835592 | tf_op jit(solution)/shard_map/ppermute | solution.py:27
  59.8 1.9 collective-permute-start.3
  61.7 6.6 %collective-permute-done.12.refs_2_ = bf16[4,136,256]{2,1,0:T(8,128)(2,1)S(1)} collective-permute-done((bf16[4,136,256]{2,1,0:T(8,128)(2,1)S(1)}, bf16[4,136,256]{2,1,0:T(8,128)(2,1)S(1)}, u32[]{:S(2)}, u32[]{:S(2)}) %collective-permute-start.12) | collective-permute-done | bytes 278560 | tf_op jit(solution)/shard_map/ppermute | solution.py:27
  68.3 1.9 collective-permute-start.13
  70.3 2.2 collective-permute-start.4
  72.4 5.3 %collective-permute-done.13.refs_3_ = bf16[4,136,256]{2,1,0:T(8,128)(2,1)S(1)} collective-permute-done((bf16[4,136,256]{2,1,0:T(8,128)(2,1)S(1)}, bf16[4,136,256]{2,1,0:T(8,128)(2,1)S(1)}, u32[]{:S(2)}, u32[]{:S(2)}) %collective-permute-start.13) | collective-permute-done | bytes 278560 | tf_op jit(solution)/shard_map/ppermute | solution.py:27
  77.7 1.9 collective-permute-start.5
  79.6 2.7 %collective-permute-start.6 = (bf16[4,136,256]{2,1,0:T(8,128)(2,1)S(1)}, bf16[4,136,256]{2,1,0:T(8,128)(2,1)S(1)}, u32[]{:S(2)}, u32[]{:S(2)}) collective-permute-start(bf16[4,136,256]{2,1,0:T(8,128)(2,1)S(1)} %collective-permute-done.3.refs_0_), channel_id=1, source_target_pairs={{0,6},{1,7},{2,4},{3,5},{4,2},{5,3},{6,0},{7,1},{8,14},{9,15},{10,... | collective-permute-start | bytes 835592 | tf_op jit(solution)/shard_map/ppermute | solution.py:27
  82.4 5.6 %collective-permute-done.9.refs_6_ = bf16[4,256,512]{2,1,0:T(8,128)(2,1)} collective-permute-done((bf16[4,256,512]{2,1,0:T(8,128)(2,1)S(1)}, bf16[4,256,512]{2,1,0:T(8,128)(2,1)}, u32[]{:S(2)}, u32[]{:S(2)}) %collective-permute-start.9) | collective-permute-done | bytes 1048608 | tf_op jit(solution)/shard_map/ppermute | solution.py:27
  87.9 2.0 mix_early.2
  89.9 5.5 %collective-permute-done.6.refs_3_ = bf16[4,136,256]{2,1,0:T(8,128)(2,1)S(1)} collective-permute-done((bf16[4,136,256]{2,1,0:T(8,128)(2,1)S(1)}, bf16[4,136,256]{2,1,0:T(8,128)(2,1)S(1)}, u32[]{:S(2)}, u32[]{:S(2)}) %collective-permute-start.6) | collective-permute-done | bytes 278560 | tf_op jit(solution)/shard_map/ppermute | solution.py:27
  95.5 2.1 mix_late.2
  97.5 2.6 %collective-permute-start.14 = (f32[2,136,256]{2,1,0:T(8,128)S(1)}, f32[2,136,256]{2,1,0:T(8,128)S(1)}, u32[]{:S(2)}, u32[]{:S(2)}) collective-permute-start(f32[2,136,256]{2,1,0:T(8,128)S(1)} %get-tuple-element.30), channel_id=1, source_target_pairs={{0,1},{1,0},{2,3},{3,2},{4,5},{5,4},{6,7},{7,6},{8,9},{9,8},{10,11... | collective-permute-start | bytes 835592 | tf_op jit(solution)/shard_map/ppermute | solution.py:27
  101.4 4.5 %collective-permute-start.15 = (bf16[136,256]{1,0:T(8,128)(2,1)S(1)}, bf16[136,256]{1,0:T(8,128)(2,1)S(1)}, u32[]{:S(2)}, u32[]{:S(2)}) collective-permute-start(bf16[136,256]{1,0:T(8,128)(2,1)S(1)} %get-tuple-element.32), channel_id=1, source_target_pairs={{0,256},{1,257},{2,258},{3,259},{4,260},{5,261},{6,262},{7,263},{8... | collective-permute-start | bytes 208904 | tf_op jit(solution)/shard_map/ppermute | solution.py:27
  105.9 12.1 %collective-permute-done.15.refs_1_ = bf16[136,256]{1,0:T(8,128)(2,1)S(1)} collective-permute-done((bf16[136,256]{1,0:T(8,128)(2,1)S(1)}, bf16[136,256]{1,0:T(8,128)(2,1)S(1)}, u32[]{:S(2)}, u32[]{:S(2)}) %collective-permute-start.15) | collective-permute-done | bytes 69664 | tf_op jit(solution)/shard_map/ppermute | solution.py:27
  120.4 2.1 collective-permute-start.16
  122.6 8.4 %collective-permute-start.17 = (bf16[1,136,256]{2,1,0:T(8,128)(2,1)}, bf16[1,136,256]{2,1,0:T(8,128)(2,1)}, u32[]{:S(2)}, u32[]{:S(2)}) collective-permute-start(bf16[1,136,256]{2,1,0:T(8,128)(2,1)} %bitcast.15), channel_id=1, source_target_pairs={{0,32},{1,33},{2,34},{3,35},{4,36},{5,37},{6,38},{7,39},{8,40},{9,... | collective-permute-start | bytes 208904 | tf_op jit(solution)/shard_map/ppermute | solution.py:27
  131.1 1.6 multiply_add_fusion
  132.6 1.6 reshape.51
  134.3 1.6 reshape.50
  136.8 2.7 %collective-permute-start.18 = (bf16[2,136,256]{2,1,0:T(8,128)(2,1)S(1)}, bf16[2,136,256]{2,1,0:T(8,128)(2,1)S(1)}, u32[]{:S(2)}, u32[]{:S(2)}) collective-permute-start(bf16[2,136,256]{2,1,0:T(8,128)(2,1)S(1)} %pad_maximum_fusion.4), channel_id=1, source_target_pairs={{0,16},{1,17},{2,18},{3,19},{4,20},{5,21},{6,22},{7,23},{8,24},{9,... | collective-permute-start | bytes 417800 | tf_op jit(solution)/shard_map/ppermute | solution.py:27
  139.5 1.8 broadcast_select_fusion
  141.3 2.3 %collective-permute-done.18 = bf16[2,136,256]{2,1,0:T(8,128)(2,1)S(1)} collective-permute-done((bf16[2,136,256]{2,1,0:T(8,128)(2,1)S(1)}, bf16[2,136,256]{2,1,0:T(8,128)(2,1)S(1)}, u32[]{:S(2)}, u32[]{:S(2)}) %collective-permute-start.18) | collective-permute-done | bytes 139296 | tf_op jit(solution)/shard_map/ppermute | solution.py:27
  144.6 8.5 %collective-permute-start.19 = (bf16[4,136,256]{2,1,0:T(8,128)(2,1)S(1)}, bf16[4,136,256]{2,1,0:T(8,128)(2,1)S(1)}, u32[]{:S(2)}, u32[]{:S(2)}) collective-permute-start(bf16[4,136,256]{2,1,0:T(8,128)(2,1)S(1)} %pad_maximum_fusion.2.refs_0_), channel_id=1, source_target_pairs={{0,8},{1,9},{2,10},{3,11},{4,12},{5,13},{6,14},{7,15},{8,0},{9,1},... | collective-permute-start | bytes 835592 | tf_op jit(solution)/shard_map/ppermute | solution.py:27
  153.1 2.2 %collective-permute-start.23 = (bf16[4,136,256]{2,1,0:T(8,128)(2,1)S(1)}, bf16[4,136,256]{2,1,0:T(8,128)(2,1)S(1)}, u32[]{:S(2)}, u32[]{:S(2)}) collective-permute-start(bf16[4,136,256]{2,1,0:T(8,128)(2,1)S(1)} %pad_maximum_fusion.2.refs_0_), channel_id=1, source_target_pairs={{0,2},{1,3},{2,0},{3,1},{4,6},{5,7},{6,4},{7,5},{8,10},{9,11},{10,... | collective-permute-start | bytes 835592 | tf_op jit(solution)/shard_map/ppermute | solution.py:27
  155.2 6.5 %collective-permute-start.24 = (bf16[4,136,256]{2,1,0:T(8,128)(2,1)S(1)}, bf16[4,136,256]{2,1,0:T(8,128)(2,1)S(1)}, u32[]{:S(2)}, u32[]{:S(2)}) collective-permute-start(bf16[4,136,256]{2,1,0:T(8,128)(2,1)S(1)} %pad_maximum_fusion.2.refs_0_), channel_id=1, source_target_pairs={{0,4},{1,5},{2,6},{3,7},{4,0},{5,1},{6,2},{7,3},{8,12},{9,13},{10,... | collective-permute-start | bytes 835592 | tf_op jit(solution)/shard_map/ppermute | solution.py:27
  161.7 1.9 collective-permute-start.25
  163.7 1.9 collective-permute-start.20
  165.6 5.7 %collective-permute-start.21 = (bf16[4,136,256]{2,1,0:T(8,128)(2,1)S(1)}, bf16[4,136,256]{2,1,0:T(8,128)(2,1)S(1)}, u32[]{:S(2)}, u32[]{:S(2)}) collective-permute-start(bf16[4,136,256]{2,1,0:T(8,128)(2,1)S(1)} %collective-permute-done.19.refs_0_), channel_id=1, source_target_pairs={{0,4},{1,5},{2,6},{3,7},{4,0},{5,1},{6,2},{7,3},{8,12},{9,13},{10,... | collective-permute-start | bytes 835592 | tf_op jit(solution)/shard_map/ppermute | solution.py:27
  171.4 1.9 collective-permute-start.22
  173.3 5.2 %collective-permute-done.25.refs_3_ = bf16[4,136,256]{2,1,0:T(8,128)(2,1)S(1)} collective-permute-done((bf16[4,136,256]{2,1,0:T(8,128)(2,1)S(1)}, bf16[4,136,256]{2,1,0:T(8,128)(2,1)S(1)}, u32[]{:S(2)}, u32[]{:S(2)}) %collective-permute-start.25) | collective-permute-done | bytes 278560 | tf_op jit(solution)/shard_map/ppermute | solution.py:27
  178.5 2.0 mix_early.3
  180.5 3.2 %collective-permute-done.21.refs_2_ = bf16[4,136,256]{2,1,0:T(8,128)(2,1)S(1)} collective-permute-done((bf16[4,136,256]{2,1,0:T(8,128)(2,1)S(1)}, bf16[4,136,256]{2,1,0:T(8,128)(2,1)S(1)}, u32[]{:S(2)}, u32[]{:S(2)}) %collective-permute-start.21) | collective-permute-done | bytes 278560 | tf_op jit(solution)/shard_map/ppermute | solution.py:27
  183.7 6.3 %collective-permute-done.22.refs_3_ = bf16[4,136,256]{2,1,0:T(8,128)(2,1)S(1)} collective-permute-done((bf16[4,136,256]{2,1,0:T(8,128)(2,1)S(1)}, bf16[4,136,256]{2,1,0:T(8,128)(2,1)S(1)}, u32[]{:S(2)}, u32[]{:S(2)}) %collective-permute-start.22) | collective-permute-done | bytes 278560 | tf_op jit(solution)/shard_map/ppermute | solution.py:27
  190.0 2.0 mix_late.3
  192.1 2.8 %collective-permute-start.26 = (f32[2,136,256]{2,1,0:T(8,128)S(1)}, f32[2,136,256]{2,1,0:T(8,128)S(1)}, u32[]{:S(2)}, u32[]{:S(2)}) collective-permute-start(f32[2,136,256]{2,1,0:T(8,128)S(1)} %get-tuple-element.43), channel_id=1, source_target_pairs={{0,1},{1,0},{2,3},{3,2},{4,5},{5,4},{6,7},{7,6},{8,9},{9,8},{10,11... | collective-permute-start | bytes 835592 | tf_op jit(solution)/shard_map/ppermute | solution.py:27
  196.1 4.6 %collective-permute-start.27 = (bf16[136,256]{1,0:T(8,128)(2,1)S(1)}, bf16[136,256]{1,0:T(8,128)(2,1)S(1)}, u32[]{:S(2)}, u32[]{:S(2)}) collective-permute-start(bf16[136,256]{1,0:T(8,128)(2,1)S(1)} %get-tuple-element.45), channel_id=1, source_target_pairs={{0,256},{1,257},{2,258},{3,259},{4,260},{5,261},{6,262},{7,263},{8... | collective-permute-start | bytes 208904 | tf_op jit(solution)/shard_map/ppermute | solution.py:27
  200.7 12.7 %collective-permute-done.27.refs_1_ = bf16[136,256]{1,0:T(8,128)(2,1)S(1)} collective-permute-done((bf16[136,256]{1,0:T(8,128)(2,1)S(1)}, bf16[136,256]{1,0:T(8,128)(2,1)S(1)}, u32[]{:S(2)}, u32[]{:S(2)}) %collective-permute-start.27) | collective-permute-done | bytes 69664 | tf_op jit(solution)/shard_map/ppermute | solution.py:27
  (92 shorter events, 14.9 us)
Async XLA Ops:
  0.6 44.1 %copy-start = (bf16[700,256]{1,0:T(8,128)(2,1)S(1)}, bf16[700,256]{1,0:T(8,128)(2,1)}, u32[]{:S(2)}) copy-start(bf16[700,256]{1,0:T(8,128)(2,1)} %param.20) | copy-start | bytes 1075204
  2.2 2.8 %copy-start.19 = (bf16[64,2,256]{2,1,0:T(2,128)(2,1)S(1)}, bf16[64,2,256]{2,1,0:T(2,128)(2,1)}, u32[]{:S(2)}) copy-start(bf16[64,2,256]{2,1,0:T(2,128)(2,1)} %param.16) | copy-start | bytes 196612
  2.2 4.3 %copy-start.20 = (s32[2,2,700]{2,1,0:T(2,128)S(1)}, s32[2,2,700]{2,1,0:T(2,128)}, u32[]{:S(2)}) copy-start(s32[2,2,700]{2,1,0:T(2,128)} %param.21) | copy-start | bytes 33604
  2.3 23.2 %collective-permute-start.7 = (bf16[4,256,256]{2,1,0:T(8,128)(2,1)S(1)}, bf16[4,256,256]{2,1,0:T(8,128)(2,1)S(1)}, u32[]{:S(2)}, u32[]{:S(2)}) collective-permute-start(bf16[4,256,256]{2,1,0:T(8,128)(2,1)S(1)} %get-tuple-element.49), channel_id=1, source_target_pairs={{0,1},{1,0},{2,3},{3,2},{4,5},{5,4},{6,7},{7,6},{8,9},{9,8},{10,11... | collective-permute-start | bytes 1572872 | tf_op jit(solution)/shard_map/ppermute | solution.py:27
  5.0 20.5 %copy-start.1 = (bf16[256,256]{1,0:T(8,128)(2,1)}, bf16[256,256]{1,0:T(8,128)(2,1)S(1)}, u32[]{:S(2)}) copy-start(bf16[256,256]{1,0:T(8,128)(2,1)S(1)} %reshape.44.factors_ref.refs_9_) | copy-start | bytes 393220
  5.2 1.3 collective-permute-start
  6.6 23.6 %copy-start.16 = (bf16[136,256]{1,0:T(8,128)(2,1)}, bf16[136,256]{1,0:T(8,128)(2,1)S(1)}, u32[]{:S(2)}) copy-start(bf16[136,256]{1,0:T(8,128)(2,1)S(1)} %collective-permute-done) | copy-start | bytes 208900
  6.6 23.6 %collective-permute-start.1 = (bf16[1,136,256]{2,1,0:T(8,128)(2,1)S(1)}, bf16[1,136,256]{2,1,0:T(8,128)(2,1)S(1)}, u32[]{:S(2)}, u32[]{:S(2)}) collective-permute-start(bf16[1,136,256]{2,1,0:T(8,128)(2,1)S(1)} %bitcast.39), channel_id=1, source_target_pairs={{0,32},{1,33},{2,34},{3,35},{4,36},{5,37},{6,38},{7,39},{8,40},{9,... | collective-permute-start | bytes 208904 | tf_op jit(solution)/shard_map/ppermute | solution.py:27
  25.6 24.3 %copy-start.21 = (f32[256]{0:T(256)S(1)}, f32[256]{0:T(256)}, u32[]{:S(2)}) copy-start(f32[256]{0:T(256)} %param.25) | copy-start | bytes 3076
  25.6 24.2 %copy-start.22 = (f32[256]{0:T(256)S(1)}, f32[256]{0:T(256)}, u32[]{:S(2)}) copy-start(f32[256]{0:T(256)} %param.24) | copy-start | bytes 3076
  25.6 24.2 %copy-start.23 = (f32[256]{0:T(256)S(1)}, f32[256]{0:T(256)}, u32[]{:S(2)}) copy-start(f32[256]{0:T(256)} %param.26) | copy-start | bytes 3076
  25.6 24.2 %copy-start.24 = (f32[256]{0:T(256)S(1)}, f32[256]{0:T(256)}, u32[]{:S(2)}) copy-start(f32[256]{0:T(256)} %param.27) | copy-start | bytes 3076
  25.6 54.0 %collective-permute-start.10 = (bf16[4,256,512]{2,1,0:T(8,128)(2,1)S(1)}, bf16[4,256,512]{2,1,0:T(8,128)(2,1)S(1)}, u32[]{:S(2)}, u32[]{:S(2)}) collective-permute-start(bf16[4,256,512]{2,1,0:T(8,128)(2,1)S(1)} %pad_maximum_fusion.refs_4_), channel_id=1, source_target_pairs={{0,192},{1,193},{2,194},{3,195},{4,196},{5,197},{6,198},{7,199},{8... | collective-permute-start | bytes 3145736 | tf_op jit(solution)/shard_map/ppermute | solution.py:27
  30.9 19.1 %collective-permute-start.2 = (bf16[2,136,256]{2,1,0:T(8,128)(2,1)}, bf16[2,136,256]{2,1,0:T(8,128)(2,1)}, u32[]{:S(2)}, u32[]{:S(2)}) collective-permute-start(bf16[2,136,256]{2,1,0:T(8,128)(2,1)} %pad_maximum_fusion.3), channel_id=1, source_target_pairs={{0,16},{1,17},{2,18},{3,19},{4,20},{5,21},{6,22},{7,23},{8,24},{9,... | collective-permute-start | bytes 417800 | tf_op jit(solution)/shard_map/ppermute | solution.py:27
  37.3 45.1 %collective-permute-start.8 = (bf16[4,256,512]{2,1,0:T(8,128)(2,1)S(1)}, bf16[4,256,512]{2,1,0:T(8,128)(2,1)S(1)}, u32[]{:S(2)}, u32[]{:S(2)}) collective-permute-start(bf16[4,256,512]{2,1,0:T(8,128)(2,1)S(1)} %pad_maximum_fusion.refs_4_), channel_id=1, source_target_pairs={{0,64},{1,65},{2,66},{3,67},{4,68},{5,69},{6,70},{7,71},{8,72},{9,... | collective-permute-start | bytes 3145736 | tf_op jit(solution)/shard_map/ppermute | solution.py:27
  40.4 47.5 %collective-permute-start.9 = (bf16[4,256,512]{2,1,0:T(8,128)(2,1)S(1)}, bf16[4,256,512]{2,1,0:T(8,128)(2,1)}, u32[]{:S(2)}, u32[]{:S(2)}) collective-permute-start(bf16[4,256,512]{2,1,0:T(8,128)(2,1)S(1)} %pad_maximum_fusion.refs_4_), channel_id=1, source_target_pairs={{0,128},{1,129},{2,130},{3,131},{4,132},{5,133},{6,134},{7,135},{8... | collective-permute-start | bytes 3145736 | tf_op jit(solution)/shard_map/ppermute | solution.py:27
  51.0 8.8 %collective-permute-start.11 = (bf16[4,136,256]{2,1,0:T(8,128)(2,1)S(1)}, bf16[4,136,256]{2,1,0:T(8,128)(2,1)S(1)}, u32[]{:S(2)}, u32[]{:S(2)}) collective-permute-start(bf16[4,136,256]{2,1,0:T(8,128)(2,1)S(1)} %pad_maximum_fusion.1.refs_0_), channel_id=1, source_target_pairs={{0,2},{1,3},{2,0},{3,1},{4,6},{5,7},{6,4},{7,5},{8,10},{9,11},{10,... | collective-permute-start | bytes 835592 | tf_op jit(solution)/shard_map/ppermute | solution.py:27
  54.2 14.1 %collective-permute-start.12 = (bf16[4,136,256]{2,1,0:T(8,128)(2,1)S(1)}, bf16[4,136,256]{2,1,0:T(8,128)(2,1)S(1)}, u32[]{:S(2)}, u32[]{:S(2)}) collective-permute-start(bf16[4,136,256]{2,1,0:T(8,128)(2,1)S(1)} %pad_maximum_fusion.1.refs_0_), channel_id=1, source_target_pairs={{0,4},{1,5},{2,6},{3,7},{4,0},{5,1},{6,2},{7,3},{8,12},{9,13},{10,... | collective-permute-start | bytes 835592 | tf_op jit(solution)/shard_map/ppermute | solution.py:27
  59.8 10.5 %collective-permute-start.3 = (bf16[4,136,256]{2,1,0:T(8,128)(2,1)S(1)}, bf16[4,136,256]{2,1,0:T(8,128)(2,1)S(1)}, u32[]{:S(2)}, u32[]{:S(2)}) collective-permute-start(bf16[4,136,256]{2,1,0:T(8,128)(2,1)S(1)} %pad_maximum_fusion.1.refs_0_), channel_id=1, source_target_pairs={{0,8},{1,9},{2,10},{3,11},{4,12},{5,13},{6,14},{7,15},{8,0},{9,1},... | collective-permute-start | bytes 835592 | tf_op jit(solution)/shard_map/ppermute | solution.py:27
  68.3 9.4 %collective-permute-start.13 = (bf16[4,136,256]{2,1,0:T(8,128)(2,1)S(1)}, bf16[4,136,256]{2,1,0:T(8,128)(2,1)S(1)}, u32[]{:S(2)}, u32[]{:S(2)}) collective-permute-start(bf16[4,136,256]{2,1,0:T(8,128)(2,1)S(1)} %pad_maximum_fusion.1.refs_0_), channel_id=1, source_target_pairs={{0,6},{1,7},{2,4},{3,5},{4,2},{5,3},{6,0},{7,1},{8,14},{9,15},{10,... | collective-permute-start | bytes 835592 | tf_op jit(solution)/shard_map/ppermute | solution.py:27
  70.3 19.6 %collective-permute-start.4 = (bf16[4,136,256]{2,1,0:T(8,128)(2,1)S(1)}, bf16[4,136,256]{2,1,0:T(8,128)(2,1)S(1)}, u32[]{:S(2)}, u32[]{:S(2)}) collective-permute-start(bf16[4,136,256]{2,1,0:T(8,128)(2,1)S(1)} %collective-permute-done.3.refs_0_), channel_id=1, source_target_pairs={{0,2},{1,3},{2,0},{3,1},{4,6},{5,7},{6,4},{7,5},{8,10},{9,11},{10,... | collective-permute-start | bytes 835592 | tf_op jit(solution)/shard_map/ppermute | solution.py:27
  77.7 12.2 %collective-permute-start.5 = (bf16[4,136,256]{2,1,0:T(8,128)(2,1)S(1)}, bf16[4,136,256]{2,1,0:T(8,128)(2,1)S(1)}, u32[]{:S(2)}, u32[]{:S(2)}) collective-permute-start(bf16[4,136,256]{2,1,0:T(8,128)(2,1)S(1)} %collective-permute-done.3.refs_0_), channel_id=1, source_target_pairs={{0,4},{1,5},{2,6},{3,7},{4,0},{5,1},{6,2},{7,3},{8,12},{9,13},{10,... | collective-permute-start | bytes 835592 | tf_op jit(solution)/shard_map/ppermute | solution.py:27
  79.6 15.8 %collective-permute-start.6 = (bf16[4,136,256]{2,1,0:T(8,128)(2,1)S(1)}, bf16[4,136,256]{2,1,0:T(8,128)(2,1)S(1)}, u32[]{:S(2)}, u32[]{:S(2)}) collective-permute-start(bf16[4,136,256]{2,1,0:T(8,128)(2,1)S(1)} %collective-permute-done.3.refs_0_), channel_id=1, source_target_pairs={{0,6},{1,7},{2,4},{3,5},{4,2},{5,3},{6,0},{7,1},{8,14},{9,15},{10,... | collective-permute-start | bytes 835592 | tf_op jit(solution)/shard_map/ppermute | solution.py:27
  95.4 22.6 %copy-start.2 = (bf16[256,256]{1,0:T(8,128)(2,1)S(1)}, bf16[256,256]{1,0:T(8,128)(2,1)}, u32[]{:S(2)}) copy-start(bf16[256,256]{1,0:T(8,128)(2,1)} %copy-done.1) | copy-start | bytes 393220
  95.4 22.6 %copy-start.6 = (bf16[256,256]{1,0:T(8,128)(2,1)S(1)}, bf16[256,256]{1,0:T(8,128)(2,1)}, u32[]{:S(2)}) copy-start(bf16[256,256]{1,0:T(8,128)(2,1)} %reshape.45.refs_8_) | copy-start | bytes 393220
  95.4 22.6 %copy-start.8 = (f32[128,256]{1,0:T(8,128)S(1)}, f32[128,256]{1,0:T(8,128)}, u32[]{:S(2)}) copy-start(f32[128,256]{1,0:T(8,128)} %reshape.46.refs_3_) | copy-start | bytes 393220
  95.4 22.6 %copy-start.9 = (f32[128,256]{1,0:T(8,128)S(1)}, f32[128,256]{1,0:T(8,128)}, u32[]{:S(2)}) copy-start(f32[128,256]{1,0:T(8,128)} %reshape.47.refs_4_) | copy-start | bytes 393220
  95.4 22.6 %copy-start.11 = (bf16[136,256]{1,0:T(8,128)(2,1)S(1)}, bf16[136,256]{1,0:T(8,128)(2,1)}, u32[]{:S(2)}) copy-start(bf16[136,256]{1,0:T(8,128)(2,1)} %copy-done.10) | copy-start | bytes 208900
  95.5 22.6 %copy-start.14 = (s32[64,2]{0,1:T(2,128)S(1)}, s32[64,2]{0,1:T(2,128)}, u32[]{:S(2)}) copy-start(s32[64,2]{0,1:T(2,128)} %param.22) | copy-start | bytes 1540
  95.5 22.6 %copy-start.15 = (s32[64]{0:T(128)S(1)}, s32[64]{0:T(128)}, u32[]{:S(2)}) copy-start(s32[64]{0:T(128)} %param.23) | copy-start | bytes 772
  97.5 3.8 %collective-permute-start.14 = (f32[2,136,256]{2,1,0:T(8,128)S(1)}, f32[2,136,256]{2,1,0:T(8,128)S(1)}, u32[]{:S(2)}, u32[]{:S(2)}) collective-permute-start(f32[2,136,256]{2,1,0:T(8,128)S(1)} %get-tuple-element.30), channel_id=1, source_target_pairs={{0,1},{1,0},{2,3},{3,2},{4,5},{5,4},{6,7},{7,6},{8,9},{9,8},{10,11... | collective-permute-start | bytes 835592 | tf_op jit(solution)/shard_map/ppermute | solution.py:27
  101.4 16.6 %collective-permute-start.15 = (bf16[136,256]{1,0:T(8,128)(2,1)S(1)}, bf16[136,256]{1,0:T(8,128)(2,1)S(1)}, u32[]{:S(2)}, u32[]{:S(2)}) collective-permute-start(bf16[136,256]{1,0:T(8,128)(2,1)S(1)} %get-tuple-element.32), channel_id=1, source_target_pairs={{0,256},{1,257},{2,258},{3,259},{4,260},{5,261},{6,262},{7,263},{8... | collective-permute-start | bytes 208904 | tf_op jit(solution)/shard_map/ppermute | solution.py:27
  120.4 2.2 %collective-permute-start.16 = (bf16[136,256]{1,0:T(8,128)(2,1)}, bf16[136,256]{1,0:T(8,128)(2,1)}, u32[]{:S(2)}, u32[]{:S(2)}) collective-permute-start(bf16[136,256]{1,0:T(8,128)(2,1)} %get-tuple-element.37.refs_2_), channel_id=1, source_target_pairs={{0,0},{1,1},{2,2},{3,3},{4,4},{5,5},{6,6},{7,7},{8,8},{9,9},{10,10... | collective-permute-start | bytes 208904 | tf_op jit(solution)/shard_map/ppermute | solution.py:27
  122.6 13.3 %collective-permute-start.17 = (bf16[1,136,256]{2,1,0:T(8,128)(2,1)}, bf16[1,136,256]{2,1,0:T(8,128)(2,1)}, u32[]{:S(2)}, u32[]{:S(2)}) collective-permute-start(bf16[1,136,256]{2,1,0:T(8,128)(2,1)} %bitcast.15), channel_id=1, source_target_pairs={{0,32},{1,33},{2,34},{3,35},{4,36},{5,37},{6,38},{7,39},{8,40},{9,... | collective-permute-start | bytes 208904 | tf_op jit(solution)/shard_map/ppermute | solution.py:27
  136.8 6.8 %collective-permute-start.18 = (bf16[2,136,256]{2,1,0:T(8,128)(2,1)S(1)}, bf16[2,136,256]{2,1,0:T(8,128)(2,1)S(1)}, u32[]{:S(2)}, u32[]{:S(2)}) collective-permute-start(bf16[2,136,256]{2,1,0:T(8,128)(2,1)S(1)} %pad_maximum_fusion.4), channel_id=1, source_target_pairs={{0,16},{1,17},{2,18},{3,19},{4,20},{5,21},{6,22},{7,23},{8,24},{9,... | collective-permute-start | bytes 417800 | tf_op jit(solution)/shard_map/ppermute | solution.py:27
  144.6 19.1 %collective-permute-start.19 = (bf16[4,136,256]{2,1,0:T(8,128)(2,1)S(1)}, bf16[4,136,256]{2,1,0:T(8,128)(2,1)S(1)}, u32[]{:S(2)}, u32[]{:S(2)}) collective-permute-start(bf16[4,136,256]{2,1,0:T(8,128)(2,1)S(1)} %pad_maximum_fusion.2.refs_0_), channel_id=1, source_target_pairs={{0,8},{1,9},{2,10},{3,11},{4,12},{5,13},{6,14},{7,15},{8,0},{9,1},... | collective-permute-start | bytes 835592 | tf_op jit(solution)/shard_map/ppermute | solution.py:27
  153.1 18.3 %collective-permute-start.23 = (bf16[4,136,256]{2,1,0:T(8,128)(2,1)S(1)}, bf16[4,136,256]{2,1,0:T(8,128)(2,1)S(1)}, u32[]{:S(2)}, u32[]{:S(2)}) collective-permute-start(bf16[4,136,256]{2,1,0:T(8,128)(2,1)S(1)} %pad_maximum_fusion.2.refs_0_), channel_id=1, source_target_pairs={{0,2},{1,3},{2,0},{3,1},{4,6},{5,7},{6,4},{7,5},{8,10},{9,11},{10,... | collective-permute-start | bytes 835592 | tf_op jit(solution)/shard_map/ppermute | solution.py:27
  155.2 18.1 %collective-permute-start.24 = (bf16[4,136,256]{2,1,0:T(8,128)(2,1)S(1)}, bf16[4,136,256]{2,1,0:T(8,128)(2,1)S(1)}, u32[]{:S(2)}, u32[]{:S(2)}) collective-permute-start(bf16[4,136,256]{2,1,0:T(8,128)(2,1)S(1)} %pad_maximum_fusion.2.refs_0_), channel_id=1, source_target_pairs={{0,4},{1,5},{2,6},{3,7},{4,0},{5,1},{6,2},{7,3},{8,12},{9,13},{10,... | collective-permute-start | bytes 835592 | tf_op jit(solution)/shard_map/ppermute | solution.py:27
  161.7 16.7 %collective-permute-start.25 = (bf16[4,136,256]{2,1,0:T(8,128)(2,1)S(1)}, bf16[4,136,256]{2,1,0:T(8,128)(2,1)S(1)}, u32[]{:S(2)}, u32[]{:S(2)}) collective-permute-start(bf16[4,136,256]{2,1,0:T(8,128)(2,1)S(1)} %pad_maximum_fusion.2.refs_0_), channel_id=1, source_target_pairs={{0,6},{1,7},{2,4},{3,5},{4,2},{5,3},{6,0},{7,1},{8,14},{9,15},{10,... | collective-permute-start | bytes 835592 | tf_op jit(solution)/shard_map/ppermute | solution.py:27
  163.7 16.8 %collective-permute-start.20 = (bf16[4,136,256]{2,1,0:T(8,128)(2,1)S(1)}, bf16[4,136,256]{2,1,0:T(8,128)(2,1)S(1)}, u32[]{:S(2)}, u32[]{:S(2)}) collective-permute-start(bf16[4,136,256]{2,1,0:T(8,128)(2,1)S(1)} %collective-permute-done.19.refs_0_), channel_id=1, source_target_pairs={{0,2},{1,3},{2,0},{3,1},{4,6},{5,7},{6,4},{7,5},{8,10},{9,11},{10,... | collective-permute-start | bytes 835592 | tf_op jit(solution)/shard_map/ppermute | solution.py:27
  165.6 18.1 %collective-permute-start.21 = (bf16[4,136,256]{2,1,0:T(8,128)(2,1)S(1)}, bf16[4,136,256]{2,1,0:T(8,128)(2,1)S(1)}, u32[]{:S(2)}, u32[]{:S(2)}) collective-permute-start(bf16[4,136,256]{2,1,0:T(8,128)(2,1)S(1)} %collective-permute-done.19.refs_0_), channel_id=1, source_target_pairs={{0,4},{1,5},{2,6},{3,7},{4,0},{5,1},{6,2},{7,3},{8,12},{9,13},{10,... | collective-permute-start | bytes 835592 | tf_op jit(solution)/shard_map/ppermute | solution.py:27
  171.4 18.7 %collective-permute-start.22 = (bf16[4,136,256]{2,1,0:T(8,128)(2,1)S(1)}, bf16[4,136,256]{2,1,0:T(8,128)(2,1)S(1)}, u32[]{:S(2)}, u32[]{:S(2)}) collective-permute-start(bf16[4,136,256]{2,1,0:T(8,128)(2,1)S(1)} %collective-permute-done.19.refs_0_), channel_id=1, source_target_pairs={{0,6},{1,7},{2,4},{3,5},{4,2},{5,3},{6,0},{7,1},{8,14},{9,15},{10,... | collective-permute-start | bytes 835592 | tf_op jit(solution)/shard_map/ppermute | solution.py:27
  190.0 23.4 %copy-start.3 = (bf16[256,256]{1,0:T(8,128)(2,1)S(1)}, bf16[256,256]{1,0:T(8,128)(2,1)}, u32[]{:S(2)}) copy-start(bf16[256,256]{1,0:T(8,128)(2,1)} %copy-done.1) | copy-start | bytes 393220
  190.0 23.4 %copy-start.5 = (f32[128,256]{1,0:T(8,128)S(1)}, f32[128,256]{1,0:T(8,128)}, u32[]{:S(2)}) copy-start(f32[128,256]{1,0:T(8,128)} %copy-done.4) | copy-start | bytes 393220
  190.0 23.4 %copy-start.7 = (bf16[256,256]{1,0:T(8,128)(2,1)S(1)}, bf16[256,256]{1,0:T(8,128)(2,1)}, u32[]{:S(2)}) copy-start(bf16[256,256]{1,0:T(8,128)(2,1)} %reshape.45.refs_8_) | copy-start | bytes 393220
  190.0 23.4 %copy-start.13 = (f32[128,256]{1,0:T(8,128)S(1)}, f32[128,256]{1,0:T(8,128)}, u32[]{:S(2)}) copy-start(f32[128,256]{1,0:T(8,128)} %copy-done.12) | copy-start | bytes 393220
  192.1 4.0 %collective-permute-start.26 = (f32[2,136,256]{2,1,0:T(8,128)S(1)}, f32[2,136,256]{2,1,0:T(8,128)S(1)}, u32[]{:S(2)}, u32[]{:S(2)}) collective-permute-start(f32[2,136,256]{2,1,0:T(8,128)S(1)} %get-tuple-element.43), channel_id=1, source_target_pairs={{0,1},{1,0},{2,3},{3,2},{4,5},{5,4},{6,7},{7,6},{8,9},{9,8},{10,11... | collective-permute-start | bytes 835592 | tf_op jit(solution)/shard_map/ppermute | solution.py:27
  196.1 17.4 %collective-permute-start.27 = (bf16[136,256]{1,0:T(8,128)(2,1)S(1)}, bf16[136,256]{1,0:T(8,128)(2,1)S(1)}, u32[]{:S(2)}, u32[]{:S(2)}) collective-permute-start(bf16[136,256]{1,0:T(8,128)(2,1)S(1)} %get-tuple-element.45), channel_id=1, source_target_pairs={{0,256},{1,257},{2,258},{3,259},{4,260},{5,261},{6,262},{7,263},{8... | collective-permute-start | bytes 208904 | tf_op jit(solution)/shard_map/ppermute | solution.py:27
  (5 other events, 5.3 us)

commit v3 on v2

--- a/solution.py
+++ b/solution.py
@@ -94,11 +94,14 @@
 
 
 def pack_kernel(spikes_ref, factors_ref, out_ref, *, trials, rank):
-    store_packed(out_ref, spikes_ref[...], factors_ref[...], trials, rank)
-
-
-def pack(spikes, factors, trials, rank):
-    rows, block = spikes.shape
+    members, _, block = spikes_ref.shape
+    spikes = spikes_ref[...].reshape(members * trials, block)
+    store_packed(out_ref, spikes, factors_ref[...].reshape(members * rank, block), trials, rank)
+
+
+def pack(spikes, factors):
+    members, trials, block = spikes.shape
+    rows, rank = members * trials, factors.shape[1]
     whole = pl.BlockSpec(memory_space=pltpu.VMEM)
     return pl.pallas_call(
         functools.partial(pack_kernel, trials=trials, rank=rank),
@@ -124,15 +127,17 @@
 def update_kernel(*refs, step, trials, rank):
     keep_ref, came_ref, packed_ref, v_ref, a_ref, lanes_ref, ids_ref, count_ref = refs[:8]
     u_ref, f_ref, outs = refs[8], refs[9], refs[10:]
-    rows, _ = v_ref.shape
+    members, _, block = u_ref.shape
+    rows = members * trials
     total = keep_ref[:rows] + came_ref[:rows].astype(jnp.float32)
     tail = came_ref[rows:].astype(jnp.float32)
     proj = keep_ref[rows : rows + trials]
     for term in range(3):
         proj = proj + tail[term * trials : (term + 1) * trials]
-    mask = member_mask(rows, u_ref.shape[0], trials, rank)
+    mask = member_mask(rows, members * rank, trials, rank)
     spread = jnp.where(mask, by_trial(proj, rows), 0.0).astype(jnp.bfloat16)
-    low = jnp.dot(spread, u_ref[...], preferred_element_type=jnp.float32)
+    u_rows = u_ref[...].reshape(members * rank, block)
+    low = jnp.dot(spread, u_rows, preferred_element_type=jnp.float32)
     current = by_trial(lanes_ref[4 + step * trials : 4 + (step + 1) * trials], rows)
     half_sign = to_column(0.5 - (ids_ref[...] & 1).astype(jnp.float32), rows, trials)
     count = to_column(count_ref[...].astype(jnp.float32), rows, trials)
@@ -140,24 +145,33 @@
     decay_mem, decay_adapt = lanes_ref[0:1], lanes_ref[1:2]
     base, adapt = lanes_ref[2:3], lanes_ref[3:4]
     spikes = packed_ref[:rows].astype(jnp.float32)
-    v, a = v_ref[...], a_ref[...]
+    v, a = v_ref[...].reshape(rows, block), a_ref[...].reshape(rows, block)
     v_new = decay_mem * v + (1.0 - decay_mem) * drive - spikes * (base + adapt * a)
-    active = count > float(step)
-    v = jnp.where(active, v_new, v)
-    outs[0][...] = v
-    if len(outs) > 1:
+    v = jnp.where(count > float(step), v_new, v)
+    outs[0][...] = v.reshape(outs[0].shape)
+    if step + 1 < STEPS:
         a_new = decay_adapt * a + (1.0 - decay_adapt) * spikes
-        a = jnp.where(active, a_new, a)
-        outs[1][...] = a
+        a = jnp.where(count > float(step), a_new, a)
         fresh = jax.nn.sigmoid(3.0 * (v - base - adapt * a)).astype(jnp.bfloat16)
-        store_packed(outs[2], fresh, f_ref[...], trials, rank)
-
-
-def update(keep, came, packed, v, a, lanes, ids, count, u_rows, f_rows, step, trials, rank):
-    state = jax.ShapeDtypeStruct(v.shape, jnp.float32)
-    outs = [state]
+        f_rows = f_ref[...].reshape(members * rank, block)
+        store_packed(outs[1], fresh, f_rows, trials, rank)
+        outs[2][...] = a
+        if step + 2 == STEPS:
+            a_new = decay_adapt * a + (1.0 - decay_adapt) * fresh.astype(jnp.float32)
+            a = jnp.where(count > float(step + 1), a_new, a)
+            outs[3][...] = a.reshape(outs[3].shape)
+
+
+def update(keep, came, packed, v, a, lanes, ids, count, factor_u, factor_v, step):
+    members, rank, block = factor_u.shape
+    trials = count.shape[0]
+    rows = jax.ShapeDtypeStruct((members * trials, block), jnp.float32)
+    final = jax.ShapeDtypeStruct((members, trials, block), jnp.float32)
     if step + 1 < STEPS:
-        outs += [state, jax.ShapeDtypeStruct(packed.shape, packed.dtype)]
+        outs = [rows, jax.ShapeDtypeStruct(packed.shape, packed.dtype), rows]
+        outs += [final] if step + 2 == STEPS else []
+    else:
+        outs = [final]
     whole = pl.BlockSpec(memory_space=pltpu.VMEM)
     return pl.pallas_call(
         functools.partial(update_kernel, step=step, trials=trials, rank=rank),
@@ -166,30 +180,32 @@
         out_specs=(whole,) * len(outs),
         compiler_params=pltpu.CompilerParams(vmem_limit_bytes=6 << 20),
         name="update",
-    )(keep, came, packed, v, a, lanes, ids, count, u_rows, f_rows)
-
-
-def mix_kernel(at_ref, *refs, rows, trials, late):
-    spikes, weights = refs[:4], refs[4:8]
+    )(keep, came, packed, v, a, lanes, ids, count, factor_u, factor_v)
+
+
+def mix_kernel(at_ref, *refs, pieces, rows, trials, late):
+    spikes, weights = refs[: 4 * pieces], refs[4 * pieces : 4 * pieces + 4]
     mine_ref, theirs_ref = refs[-2:]
+    before = refs[-4:-2]
     flip, shift, y = at_ref[0], at_ref[1], at_ref[2]
     tall, block = spikes[0].shape[1:]
+    depth = spikes[0].shape[0] // 2
     extra = None
-    for q in range(4):
-        tail = spikes[q][:2, rows:, :].astype(jnp.float32)
-        tail = tail + spikes[q][2:, rows:, :].astype(jnp.float32)
-        extra = tail if extra is None else extra + tail
+    for ref in spikes:
+        for pair in range(depth):
+            tail = ref[2 * pair : 2 * pair + 2, rows:, :].astype(jnp.float32)
+            extra = tail if extra is None else extra + tail
     part = extra[:, :trials] + extra[:, trials : 2 * trials] + extra[:, 2 * trials : 3 * trials]
 
-    def run(low):
+    def run(there):
         total = None
         for q in range(4):
             for high in range(2):
-                first = ((shift >> 1) ^ high) * 2
-                chunk = spikes[q][pl.ds(first, 2)]
+                ref = spikes[q + 4 * high] if pieces == 2 else spikes[q]
+                chunk = ref[...] if pieces == 2 else ref[2 * high : 2 * high + 2]
                 piece = jnp.dot(
                     chunk.reshape(2 * tall, block),
-                    weights[2 * high + low][y ^ q],
+                    weights[there ^ (2 * high + int(late))][y ^ q],
                     preferred_element_type=jnp.float32,
                 )
                 total = piece if total is None else total + piece
@@ -198,28 +214,30 @@
                 value = total[s * tall : (s + 1) * tall, half * block : (half + 1) * block]
                 other = part[s]
                 if late:
-                    before = refs[8 + half]
-                    value = value + before[s ^ flip]
-                    other = other + before[s ^ flip, rows : rows + trials, :]
+                    value = value + before[half][s ^ flip]
+                    other = other + before[half][s ^ flip, rows : rows + trials, :]
                 ref[s ^ flip] = value
                 ref[s ^ flip, rows : rows + trials, :] = other
 
-    for low in range(2):
-        pl.when(((shift & 1) ^ int(late)) == low)(functools.partial(run, low))
+    for there in range(4):
+        pl.when(shift == there)(functools.partial(run, there))
 
 
 def mix(at, spikes, weights, rows, trials, before=()):
-    blocks, tall, block = spikes[0].shape
+    _, tall, block = spikes[0].shape
     out = jax.ShapeDtypeStruct((2, tall, block), jnp.float32)
     whole = pl.BlockSpec(memory_space=pltpu.VMEM)
     inputs = len(spikes) * spikes[0].size + 2 * weights[0].size
     return pl.pallas_call(
-        functools.partial(mix_kernel, rows=rows, trials=trials, late=len(before) > 0),
+        functools.partial(
+            mix_kernel, pieces=len(spikes) // 4, rows=rows, trials=trials, late=len(before) > 0
+        ),
         out_shape=(out, out),
-        in_specs=[pl.BlockSpec(memory_space=pltpu.SMEM)] + [whole] * (8 + len(before)),
+        in_specs=[pl.BlockSpec(memory_space=pltpu.SMEM)]
+        + [whole] * (len(spikes) + 4 + len(before)),
         out_specs=(whole, whole),
         cost_estimate=pl.CostEstimate(
-            flops=4 * blocks * tall * weights[0].size // 2,
+            flops=16 * tall * weights[0].size // 2,
             bytes_accessed=2 * inputs + 16 * tall * block,
             transcendentals=0,
         ),
@@ -283,12 +301,9 @@
     thr_base,
     thr_adapt,
 ):
-    members, trials, block = v_init.shape
-    rank = factor_u.shape[1]
+    members, trials, _ = v_init.shape
     rows = members * trials
     at = {name: lax.axis_index(name) for name in AXES}
-    u_rows = factor_u.reshape(members * rank, block)
-    f_rows = factor_v.reshape(members * rank, block)
     ids = member_ids.reshape(1, members)
     count = step_count.T
     current = jnp.dot(
@@ -299,41 +314,33 @@
     lanes = jnp.stack([decay_mem, decay_adapt, thr_base, thr_adapt])
     lanes = jnp.concatenate([lanes, current], axis=0)
     place = jnp.stack([at["a"] ^ at["zh"], at["b"] ^ at["x"], at["y"]])
-    v, a = v_init.reshape(rows, block), a_init.reshape(rows, block)
-    packed = pack(z_init.reshape(rows, block), f_rows, trials, rank)
+    v, a = v_init, a_init
+    packed = pack(z_init, factor_v)
     weights = spread_weights(base_weight, at)
     for step in range(STEPS):
         held = to_owner(packed)[None]
         other = over_a(held)
-        held = jnp.concatenate([held, other], axis=0)
-        other = over_b(held, 2)
-        held = jnp.concatenate([held, other], axis=0)
+        first = [jnp.concatenate([held, other], axis=0)]
+        second = [over_b(first[0], 2)]
+        held = jnp.concatenate([first[0], second[0]], axis=0)
         if step == 0:
-            ready = (held, place, lanes, u_rows, v, a)
-            held, place, lanes, u_rows, v, a = lax.optimization_barrier(ready)
-        if step + 1 == STEPS:
-            spikes_f = packed[:rows].astype(jnp.float32)
-            a_new = decay_adapt * a + (1.0 - decay_adapt) * spikes_f
-            a_new = a_new.reshape(a_init.shape)
-            active = (step_count > step)[:, :, None]
-            a_out = jnp.where(active, a_new, a.reshape(a_init.shape))
-            held, a_out = lax.optimization_barrier((held, a_out))
-        early = [held]
-        late = [over_b(early[0], 1)]
-        for pieces in (early, late):
+            held, place, lanes = lax.optimization_barrier((held, place, lanes))
+        last = [over_b(held, 1)]
+        for pieces in (first, second, last):
             for k in (1, 2, 3):
                 pieces.append(over_y(pieces[0], k))
-        halves = mix(place, early, weights, rows, trials)
-        mine, theirs = mix(place, late, weights, rows, trials, halves)
+        halves = mix(place, first + second, weights, rows, trials)
+        mine, theirs = mix(place, last, weights, rows, trials, halves)
         theirs = over_c(theirs)
         keep, give = fold(mine, theirs, rows, trials)
         came = over_zh(give)
         v, *rest = update(
-            keep, came, packed, v, a, lanes, ids, count, u_rows, f_rows, step, trials, rank
+            keep, came, packed, v, a, lanes, ids, count, factor_u, factor_v, step
         )
         if rest:
-            a, packed = rest
-    return (v.reshape(v_init.shape), a_out)
+            packed, a, *ends = rest
+            a_out = ends[0] if ends else None
+    return (v, a_out)
 
 
 def solution(mesh):

time: 217 us -> 226 us (1.041)
  the two profiles are of different devices: /device:TPU:65 before, /device:TPU:35 now
where the time goes in v3:
time: 226 us; the launch traced here: 224 us
  starting transfers between devices  155 us (69%)
  waiting for transfers between devices  50.2 us (22%)
  Pallas kernels  10.4 us (5%)
  local copies, waits for them, and re-layouts  5.42 us (2%)
    ppermute x34, starting transfers between devices, permute(): return lax.ppermute(value, AXES, pairs)  155 us
    ppermute x34, waiting for transfers between devices, permute(): return lax.ppermute(value, AXES, pairs)  50.2 us
    pallas_call x4, Pallas kernels, mix(): pl.pallas_call(functools.partial(mix_kernel, pieces=len(spikes) // 4, row...  8.33 us
    unnamed x45, local copies, waits for them, and re-layouts  5.38 us
  transfers between devices with their start and end apart: 34, of which 13 were waited for; matrix products, arithmetic and copies ran while one was open for 1% of the time, Pallas kernels for 2%

profile of v3, /device:TPU:35, one launch (start us, length us, event | category | flops | bytes accessed | tf_op | source)
XLA Modules:
  0.0 224.3 jit_solution(2968596885832464177)
XLA Ops:
  0.6 1.5 copy.16
  2.3 2.6 %collective-permute-start.7 = (bf16[4,256,256]{2,1,0:T(8,128)(2,1)S(1)}, bf16[4,256,256]{2,1,0:T(8,128)(2,1)S(1)}, u32[]{:S(2)}, u32[]{:S(2)}) collective-permute-start(bf16[4,256,256]{2,1,0:T(8,128)(2,1)S(1)} %get-tuple-element.41), channel_id=1, source_target_pairs={{0,1},{1,0},{2,3},{3,2},{4,5},{5,4},{6,7},{7,6},{8,9},{9,8},{10,11... | collective-permute-start | bytes 1572872 | tf_op jit(solution)/shard_map/ppermute | solution.py:27
  6.4 21.0 %collective-permute-start.1 = (bf16[1,136,256]{2,1,0:T(8,128)(2,1)S(1)}, bf16[1,136,256]{2,1,0:T(8,128)(2,1)S(1)}, u32[]{:S(2)}, u32[]{:S(2)}) collective-permute-start(bf16[1,136,256]{2,1,0:T(8,128)(2,1)S(1)} %bitcast.39), channel_id=1, source_target_pairs={{0,32},{1,33},{2,34},{3,35},{4,36},{5,37},{6,38},{7,39},{8,40},{9,... | collective-permute-start | bytes 208904 | tf_op jit(solution)/shard_map/ppermute | solution.py:27
  27.6 3.1 %collective-permute-start.10 = (bf16[4,256,512]{2,1,0:T(8,128)(2,1)S(1)}, bf16[4,256,512]{2,1,0:T(8,128)(2,1)S(1)}, u32[]{:S(2)}, u32[]{:S(2)}) collective-permute-start(bf16[4,256,512]{2,1,0:T(8,128)(2,1)S(1)} %pad_maximum_fusion.refs_8_.refs_4_), channel_id=1, source_target_pairs={{0,192},{1,193},{2,194},{3,195},{4,196},{5,197},{6,198},{7,199},{8... | collective-permute-start | bytes 3145736 | tf_op jit(solution)/shard_map/ppermute | solution.py:27
  30.7 1.4 collective-permute-done.1
  32.7 2.1 collective-permute-start.2
  34.8 3.4 %collective-permute-start.8 = (bf16[4,256,512]{2,1,0:T(8,128)(2,1)S(1)}, bf16[4,256,512]{2,1,0:T(8,128)(2,1)S(1)}, u32[]{:S(2)}, u32[]{:S(2)}) collective-permute-start(bf16[4,256,512]{2,1,0:T(8,128)(2,1)S(1)} %pad_maximum_fusion.refs_8_.refs_4_), channel_id=1, source_target_pairs={{0,64},{1,65},{2,66},{3,67},{4,68},{5,69},{6,70},{7,71},{8,72},{9,... | collective-permute-start | bytes 3145736 | tf_op jit(solution)/shard_map/ppermute | solution.py:27
  38.3 2.6 %collective-permute-start.9 = (bf16[4,256,512]{2,1,0:T(8,128)(2,1)S(1)}, bf16[4,256,512]{2,1,0:T(8,128)(2,1)}, u32[]{:S(2)}, u32[]{:S(2)}) collective-permute-start(bf16[4,256,512]{2,1,0:T(8,128)(2,1)S(1)} %pad_maximum_fusion.refs_8_.refs_4_), channel_id=1, source_target_pairs={{0,128},{1,129},{2,130},{3,131},{4,132},{5,133},{6,134},{7,135},{8... | collective-permute-start | bytes 3145736 | tf_op jit(solution)/shard_map/ppermute | solution.py:27
  40.9 3.2 %collective-permute-start.11 = (bf16[2,136,256]{2,1,0:T(8,128)(2,1)}, bf16[2,136,256]{2,1,0:T(8,128)(2,1)S(1)}, u32[]{:S(2)}, u32[]{:S(2)}) collective-permute-start(bf16[2,136,256]{2,1,0:T(8,128)(2,1)} %pad_maximum_fusion.3.refs_0_), channel_id=1, source_target_pairs={{0,2},{1,3},{2,0},{3,1},{4,6},{5,7},{6,4},{7,5},{8,10},{9,11},{10,... | collective-permute-start | bytes 417800 | tf_op jit(solution)/shard_map/ppermute | solution.py:27
  44.2 4.5 %collective-permute-start.12 = (bf16[2,136,256]{2,1,0:T(8,128)(2,1)}, bf16[2,136,256]{2,1,0:T(8,128)(2,1)S(1)}, u32[]{:S(2)}, u32[]{:S(2)}) collective-permute-start(bf16[2,136,256]{2,1,0:T(8,128)(2,1)} %pad_maximum_fusion.3.refs_0_), channel_id=1, source_target_pairs={{0,4},{1,5},{2,6},{3,7},{4,0},{5,1},{6,2},{7,3},{8,12},{9,13},{10,... | collective-permute-start | bytes 417800 | tf_op jit(solution)/shard_map/ppermute | solution.py:27
  49.6 3.0 %collective-permute-start.13 = (bf16[2,136,256]{2,1,0:T(8,128)(2,1)}, bf16[2,136,256]{2,1,0:T(8,128)(2,1)}, u32[]{:S(2)}, u32[]{:S(2)}) collective-permute-start(bf16[2,136,256]{2,1,0:T(8,128)(2,1)} %pad_maximum_fusion.3.refs_0_), channel_id=1, source_target_pairs={{0,6},{1,7},{2,4},{3,5},{4,2},{5,3},{6,0},{7,1},{8,14},{9,15},{10,... | collective-permute-start | bytes 417800 | tf_op jit(solution)/shard_map/ppermute | solution.py:27
  53.2 1.9 collective-permute-start.14
  56.3 1.6 collective-permute-done.13.refs_3_
  57.9 3.9 %collective-permute-start.3 = (bf16[4,136,256]{2,1,0:T(8,128)(2,1)S(1)}, bf16[4,136,256]{2,1,0:T(8,128)(2,1)S(1)}, u32[]{:S(2)}, u32[]{:S(2)}) collective-permute-start(bf16[4,136,256]{2,1,0:T(8,128)(2,1)S(1)} %pad_maximum_fusion.1), channel_id=1, source_target_pairs={{0,8},{1,9},{2,10},{3,11},{4,12},{5,13},{6,14},{7,15},{8,0},{9,1},... | collective-permute-start | bytes 835592 | tf_op jit(solution)/shard_map/ppermute | solution.py:27
  61.8 4.1 %collective-permute-start.15 = (bf16[2,136,256]{2,1,0:T(8,128)(2,1)}, bf16[2,136,256]{2,1,0:T(8,128)(2,1)S(1)}, u32[]{:S(2)}, u32[]{:S(2)}) collective-permute-start(bf16[2,136,256]{2,1,0:T(8,128)(2,1)} %collective-permute-done.2.refs_4_), channel_id=1, source_target_pairs={{0,4},{1,5},{2,6},{3,7},{4,0},{5,1},{6,2},{7,3},{8,12},{9,13},{10,... | collective-permute-start | bytes 417800 | tf_op jit(solution)/shard_map/ppermute | solution.py:27
  65.9 3.4 %collective-permute-done.15.refs_6_ = bf16[2,136,256]{2,1,0:T(8,128)(2,1)S(1)} collective-permute-done((bf16[2,136,256]{2,1,0:T(8,128)(2,1)}, bf16[2,136,256]{2,1,0:T(8,128)(2,1)S(1)}, u32[]{:S(2)}, u32[]{:S(2)}) %collective-permute-start.15) | collective-permute-done | bytes 139296 | tf_op jit(solution)/shard_map/ppermute | solution.py:27
  69.3 3.3 %collective-permute-start.16 = (bf16[2,136,256]{2,1,0:T(8,128)(2,1)}, bf16[2,136,256]{2,1,0:T(8,128)(2,1)S(1)}, u32[]{:S(2)}, u32[]{:S(2)}) collective-permute-start(bf16[2,136,256]{2,1,0:T(8,128)(2,1)} %collective-permute-done.2.refs_4_), channel_id=1, source_target_pairs={{0,6},{1,7},{2,4},{3,5},{4,2},{5,3},{6,0},{7,1},{8,14},{9,15},{10,... | collective-permute-start | bytes 417800 | tf_op jit(solution)/shard_map/ppermute | solution.py:27
  72.6 2.7 %collective-permute-start.4 = (bf16[4,136,256]{2,1,0:T(8,128)(2,1)S(1)}, bf16[4,136,256]{2,1,0:T(8,128)(2,1)S(1)}, u32[]{:S(2)}, u32[]{:S(2)}) collective-permute-start(bf16[4,136,256]{2,1,0:T(8,128)(2,1)S(1)} %collective-permute-done.3.refs_0_), channel_id=1, source_target_pairs={{0,2},{1,3},{2,0},{3,1},{4,6},{5,7},{6,4},{7,5},{8,10},{9,11},{10,... | collective-permute-start | bytes 835592 | tf_op jit(solution)/shard_map/ppermute | solution.py:27
  75.4 1.4 collective-permute-done.16.refs_7_
  76.8 3.4 %collective-permute-start.5 = (bf16[4,136,256]{2,1,0:T(8,128)(2,1)S(1)}, bf16[4,136,256]{2,1,0:T(8,128)(2,1)S(1)}, u32[]{:S(2)}, u32[]{:S(2)}) collective-permute-start(bf16[4,136,256]{2,1,0:T(8,128)(2,1)S(1)} %collective-permute-done.3.refs_0_), channel_id=1, source_target_pairs={{0,4},{1,5},{2,6},{3,7},{4,0},{5,1},{6,2},{7,3},{8,12},{9,13},{10,... | collective-permute-start | bytes 835592 | tf_op jit(solution)/shard_map/ppermute | solution.py:27
  80.2 3.6 %collective-permute-start.6 = (bf16[4,136,256]{2,1,0:T(8,128)(2,1)S(1)}, bf16[4,136,256]{2,1,0:T(8,128)(2,1)S(1)}, u32[]{:S(2)}, u32[]{:S(2)}) collective-permute-start(bf16[4,136,256]{2,1,0:T(8,128)(2,1)S(1)} %collective-permute-done.3.refs_0_), channel_id=1, source_target_pairs={{0,6},{1,7},{2,4},{3,5},{4,2},{5,3},{6,0},{7,1},{8,14},{9,15},{10,... | collective-permute-start | bytes 835592 | tf_op jit(solution)/shard_map/ppermute | solution.py:27
  85.6 2.3 %mix_early.2 = (f32[2,136,256]{2,1,0:T(8,128)S(1)}, f32[2,136,256]{2,1,0:T(8,128)S(1)}) custom-call(s32[3]{0:T(128)S(1)} %pad_add_fusion.at_ref, bf16[2,136,256]{2,1,0:T(8,128)(2,1)} %pad_maximum_fusion.3.refs_0_, bf16[2,136,256]{2,1,0:T(8,128)(2,1)S(1)} %copy-done.7, bf16[2,136,256]{2,1,0:T(8,128)(2,1)S(1)} %copy-done.9, ...), custom_call_target="tpu_custom_call" | custom-call | flops 570425344 | bytes 3768320 | tf_op jit(solution)/shard_map/mix_early/pallas_call | solution.py:231
  87.9 5.9 %collective-permute-done.6.refs_3_ = bf16[4,136,256]{2,1,0:T(8,128)(2,1)S(1)} collective-permute-done((bf16[4,136,256]{2,1,0:T(8,128)(2,1)S(1)}, bf16[4,136,256]{2,1,0:T(8,128)(2,1)S(1)}, u32[]{:S(2)}, u32[]{:S(2)}) %collective-permute-start.6) | collective-permute-done | bytes 278560 | tf_op jit(solution)/shard_map/ppermute | solution.py:27
  93.8 2.1 mix_late.2
  95.9 4.4 %collective-permute-start.17 = (f32[2,136,256]{2,1,0:T(8,128)S(1)}, f32[2,136,256]{2,1,0:T(8,128)S(1)}, u32[]{:S(2)}, u32[]{:S(2)}) collective-permute-start(f32[2,136,256]{2,1,0:T(8,128)S(1)} %get-tuple-element.26), channel_id=1, source_target_pairs={{0,1},{1,0},{2,3},{3,2},{4,5},{5,4},{6,7},{7,6},{8,9},{9,8},{10,11... | collective-permute-start | bytes 835592 | tf_op jit(solution)/shard_map/ppermute | solution.py:27
  101.6 13.7 %collective-permute-start.18 = (bf16[136,256]{1,0:T(8,128)(2,1)S(1)}, bf16[136,256]{1,0:T(8,128)(2,1)S(1)}, u32[]{:S(2)}, u32[]{:S(2)}) collective-permute-start(bf16[136,256]{1,0:T(8,128)(2,1)S(1)} %get-tuple-element.28), channel_id=1, source_target_pairs={{0,256},{1,257},{2,258},{3,259},{4,260},{5,261},{6,262},{7,263},{8... | collective-permute-start | bytes 208904 | tf_op jit(solution)/shard_map/ppermute | solution.py:27
  115.3 3.7 %collective-permute-done.18.refs_1_ = bf16[136,256]{1,0:T(8,128)(2,1)S(1)} collective-permute-done((bf16[136,256]{1,0:T(8,128)(2,1)S(1)}, bf16[136,256]{1,0:T(8,128)(2,1)S(1)}, u32[]{:S(2)}, u32[]{:S(2)}) %collective-permute-start.18) | collective-permute-done | bytes 69664 | tf_op jit(solution)/shard_map/ppermute | solution.py:27
  120.6 16.4 %collective-permute-start.20 = (bf16[1,136,256]{2,1,0:T(8,128)(2,1)S(1)}, bf16[1,136,256]{2,1,0:T(8,128)(2,1)S(1)}, u32[]{:S(2)}, u32[]{:S(2)}) collective-permute-start(bf16[1,136,256]{2,1,0:T(8,128)(2,1)S(1)} %bitcast.42), channel_id=1, source_target_pairs={{0,32},{1,33},{2,34},{3,35},{4,36},{5,37},{6,38},{7,39},{8,40},{9,... | collective-permute-start | bytes 208904 | tf_op jit(solution)/shard_map/ppermute | solution.py:27
  137.1 1.7 collective-permute-done.20
  138.8 3.2 %collective-permute-start.21 = (bf16[2,136,256]{2,1,0:T(8,128)(2,1)S(1)}, bf16[2,136,256]{2,1,0:T(8,128)(2,1)S(1)}, u32[]{:S(2)}, u32[]{:S(2)}) collective-permute-start(bf16[2,136,256]{2,1,0:T(8,128)(2,1)S(1)} %pad_maximum_fusion.4.refs_0_), channel_id=1, source_target_pairs={{0,16},{1,17},{2,18},{3,19},{4,20},{5,21},{6,22},{7,23},{8,24},{9,... | collective-permute-start | bytes 417800 | tf_op jit(solution)/shard_map/ppermute | solution.py:27
  142.0 3.5 %collective-permute-done.21.refs_4_ = bf16[2,136,256]{2,1,0:T(8,128)(2,1)S(1)} collective-permute-done((bf16[2,136,256]{2,1,0:T(8,128)(2,1)S(1)}, bf16[2,136,256]{2,1,0:T(8,128)(2,1)S(1)}, u32[]{:S(2)}, u32[]{:S(2)}) %collective-permute-start.21) | collective-permute-done | bytes 139296 | tf_op jit(solution)/shard_map/ppermute | solution.py:27
  145.5 10.8 %collective-permute-start.22 = (bf16[4,136,256]{2,1,0:T(8,128)(2,1)S(1)}, bf16[4,136,256]{2,1,0:T(8,128)(2,1)S(1)}, u32[]{:S(2)}, u32[]{:S(2)}) collective-permute-start(bf16[4,136,256]{2,1,0:T(8,128)(2,1)S(1)} %pad_maximum_fusion.2), channel_id=1, source_target_pairs={{0,8},{1,9},{2,10},{3,11},{4,12},{5,13},{6,14},{7,15},{8,0},{9,1},... | collective-permute-start | bytes 835592 | tf_op jit(solution)/shard_map/ppermute | solution.py:27
  156.3 2.6 %collective-permute-start.26 = (bf16[2,136,256]{2,1,0:T(8,128)(2,1)S(1)}, bf16[2,136,256]{2,1,0:T(8,128)(2,1)S(1)}, u32[]{:S(2)}, u32[]{:S(2)}) collective-permute-start(bf16[2,136,256]{2,1,0:T(8,128)(2,1)S(1)} %pad_maximum_fusion.4.refs_0_), channel_id=1, source_target_pairs={{0,2},{1,3},{2,0},{3,1},{4,6},{5,7},{6,4},{7,5},{8,10},{9,11},{10,... | collective-permute-start | bytes 417800 | tf_op jit(solution)/shard_map/ppermute | solution.py:27
  158.9 4.0 %collective-permute-start.27 = (bf16[2,136,256]{2,1,0:T(8,128)(2,1)S(1)}, bf16[2,136,256]{2,1,0:T(8,128)(2,1)S(1)}, u32[]{:S(2)}, u32[]{:S(2)}) collective-permute-start(bf16[2,136,256]{2,1,0:T(8,128)(2,1)S(1)} %pad_maximum_fusion.4.refs_0_), channel_id=1, source_target_pairs={{0,4},{1,5},{2,6},{3,7},{4,0},{5,1},{6,2},{7,3},{8,12},{9,13},{10,... | collective-permute-start | bytes 417800 | tf_op jit(solution)/shard_map/ppermute | solution.py:27
  162.9 3.0 %collective-permute-start.28 = (bf16[2,136,256]{2,1,0:T(8,128)(2,1)S(1)}, bf16[2,136,256]{2,1,0:T(8,128)(2,1)S(1)}, u32[]{:S(2)}, u32[]{:S(2)}) collective-permute-start(bf16[2,136,256]{2,1,0:T(8,128)(2,1)S(1)} %pad_maximum_fusion.4.refs_0_), channel_id=1, source_target_pairs={{0,6},{1,7},{2,4},{3,5},{4,2},{5,3},{6,0},{7,1},{8,14},{9,15},{10,... | collective-permute-start | bytes 417800 | tf_op jit(solution)/shard_map/ppermute | solution.py:27
  165.9 1.9 collective-permute-start.29
  167.8 3.4 %collective-permute-start.23 = (bf16[4,136,256]{2,1,0:T(8,128)(2,1)S(1)}, bf16[4,136,256]{2,1,0:T(8,128)(2,1)S(1)}, u32[]{:S(2)}, u32[]{:S(2)}) collective-permute-start(bf16[4,136,256]{2,1,0:T(8,128)(2,1)S(1)} %collective-permute-done.22.refs_0_), channel_id=1, source_target_pairs={{0,2},{1,3},{2,0},{3,1},{4,6},{5,7},{6,4},{7,5},{8,10},{9,11},{10,... | collective-permute-start | bytes 835592 | tf_op jit(solution)/shard_map/ppermute | solution.py:27
  171.2 3.2 %collective-permute-start.24 = (bf16[4,136,256]{2,1,0:T(8,128)(2,1)S(1)}, bf16[4,136,256]{2,1,0:T(8,128)(2,1)S(1)}, u32[]{:S(2)}, u32[]{:S(2)}) collective-permute-start(bf16[4,136,256]{2,1,0:T(8,128)(2,1)S(1)} %collective-permute-done.22.refs_0_), channel_id=1, source_target_pairs={{0,4},{1,5},{2,6},{3,7},{4,0},{5,1},{6,2},{7,3},{8,12},{9,13},{10,... | collective-permute-start | bytes 835592 | tf_op jit(solution)/shard_map/ppermute | solution.py:27
  174.5 3.0 %collective-permute-start.25 = (bf16[4,136,256]{2,1,0:T(8,128)(2,1)S(1)}, bf16[4,136,256]{2,1,0:T(8,128)(2,1)S(1)}, u32[]{:S(2)}, u32[]{:S(2)}) collective-permute-start(bf16[4,136,256]{2,1,0:T(8,128)(2,1)S(1)} %collective-permute-done.22.refs_0_), channel_id=1, source_target_pairs={{0,6},{1,7},{2,4},{3,5},{4,2},{5,3},{6,0},{7,1},{8,14},{9,15},{10,... | collective-permute-start | bytes 835592 | tf_op jit(solution)/shard_map/ppermute | solution.py:27
  177.5 3.5 %collective-permute-start.30 = (bf16[2,136,256]{2,1,0:T(8,128)(2,1)S(1)}, bf16[2,136,256]{2,1,0:T(8,128)(2,1)S(1)}, u32[]{:S(2)}, u32[]{:S(2)}) collective-permute-start(bf16[2,136,256]{2,1,0:T(8,128)(2,1)S(1)} %collective-permute-done.21.refs_4_), channel_id=1, source_target_pairs={{0,4},{1,5},{2,6},{3,7},{4,0},{5,1},{6,2},{7,3},{8,12},{9,13},{10,... | collective-permute-start | bytes 417800 | tf_op jit(solution)/shard_map/ppermute | solution.py:27
  180.9 3.0 %collective-permute-start.31 = (bf16[2,136,256]{2,1,0:T(8,128)(2,1)S(1)}, bf16[2,136,256]{2,1,0:T(8,128)(2,1)S(1)}, u32[]{:S(2)}, u32[]{:S(2)}) collective-permute-start(bf16[2,136,256]{2,1,0:T(8,128)(2,1)S(1)} %collective-permute-done.21.refs_4_), channel_id=1, source_target_pairs={{0,6},{1,7},{2,4},{3,5},{4,2},{5,3},{6,0},{7,1},{8,14},{9,15},{10,... | collective-permute-start | bytes 417800 | tf_op jit(solution)/shard_map/ppermute | solution.py:27
  183.9 4.6 %collective-permute-done.30.refs_6_ = bf16[2,136,256]{2,1,0:T(8,128)(2,1)S(1)} collective-permute-done((bf16[2,136,256]{2,1,0:T(8,128)(2,1)S(1)}, bf16[2,136,256]{2,1,0:T(8,128)(2,1)S(1)}, u32[]{:S(2)}, u32[]{:S(2)}) %collective-permute-start.30) | collective-permute-done | bytes 139296 | tf_op jit(solution)/shard_map/ppermute | solution.py:27
  188.6 7.9 %collective-permute-done.31.refs_7_ = bf16[2,136,256]{2,1,0:T(8,128)(2,1)S(1)} collective-permute-done((bf16[2,136,256]{2,1,0:T(8,128)(2,1)S(1)}, bf16[2,136,256]{2,1,0:T(8,128)(2,1)S(1)}, u32[]{:S(2)}, u32[]{:S(2)}) %collective-permute-start.31) | collective-permute-done | bytes 139296 | tf_op jit(solution)/shard_map/ppermute | solution.py:27
  196.5 2.0 mix_early.3
  198.5 2.0 mix_late.3
  200.5 3.7 %collective-permute-start.32 = (f32[2,136,256]{2,1,0:T(8,128)S(1)}, f32[2,136,256]{2,1,0:T(8,128)S(1)}, u32[]{:S(2)}, u32[]{:S(2)}) collective-permute-start(f32[2,136,256]{2,1,0:T(8,128)S(1)} %get-tuple-element.34), channel_id=1, source_target_pairs={{0,1},{1,0},{2,3},{3,2},{4,5},{5,4},{6,7},{7,6},{8,9},{9,8},{10,11... | collective-permute-start | bytes 835592 | tf_op jit(solution)/shard_map/ppermute | solution.py:27
  205.4 5.3 %collective-permute-start.33 = (bf16[136,256]{1,0:T(8,128)(2,1)S(1)}, bf16[136,256]{1,0:T(8,128)(2,1)S(1)}, u32[]{:S(2)}, u32[]{:S(2)}) collective-permute-start(bf16[136,256]{1,0:T(8,128)(2,1)S(1)} %get-tuple-element.36), channel_id=1, source_target_pairs={{0,256},{1,257},{2,258},{3,259},{4,260},{5,261},{6,262},{7,263},{8... | collective-permute-start | bytes 208904 | tf_op jit(solution)/shard_map/ppermute | solution.py:27
  210.6 12.8 %collective-permute-done.33.refs_1_ = bf16[136,256]{1,0:T(8,128)(2,1)S(1)} collective-permute-done((bf16[136,256]{1,0:T(8,128)(2,1)S(1)}, bf16[136,256]{1,0:T(8,128)(2,1)S(1)}, u32[]{:S(2)}, u32[]{:S(2)}) %collective-permute-start.33) | collective-permute-done | bytes 69664 | tf_op jit(solution)/shard_map/ppermute | solution.py:27
  (85 shorter events, 11.8 us)
Async XLA Ops:
  0.6 48.1 %copy-start = (bf16[700,256]{1,0:T(8,128)(2,1)S(1)}, bf16[700,256]{1,0:T(8,128)(2,1)}, u32[]{:S(2)}) copy-start(bf16[700,256]{1,0:T(8,128)(2,1)} %param.20) | copy-start | bytes 1075204
  2.3 25.1 %collective-permute-start.7 = (bf16[4,256,256]{2,1,0:T(8,128)(2,1)S(1)}, bf16[4,256,256]{2,1,0:T(8,128)(2,1)S(1)}, u32[]{:S(2)}, u32[]{:S(2)}) collective-permute-start(bf16[4,256,256]{2,1,0:T(8,128)(2,1)S(1)} %get-tuple-element.41), channel_id=1, source_target_pairs={{0,1},{1,0},{2,3},{3,2},{4,5},{5,4},{6,7},{7,6},{8,9},{9,8},{10,11... | collective-permute-start | bytes 1572872 | tf_op jit(solution)/shard_map/ppermute | solution.py:27
  5.1 1.3 collective-permute-start
  6.4 25.6 %copy-start.15 = (bf16[136,256]{1,0:T(8,128)(2,1)}, bf16[136,256]{1,0:T(8,128)(2,1)S(1)}, u32[]{:S(2)}) copy-start(bf16[136,256]{1,0:T(8,128)(2,1)S(1)} %collective-permute-done) | copy-start | bytes 208900
  6.4 25.6 %collective-permute-start.1 = (bf16[1,136,256]{2,1,0:T(8,128)(2,1)S(1)}, bf16[1,136,256]{2,1,0:T(8,128)(2,1)S(1)}, u32[]{:S(2)}, u32[]{:S(2)}) collective-permute-start(bf16[1,136,256]{2,1,0:T(8,128)(2,1)S(1)} %bitcast.39), channel_id=1, source_target_pairs={{0,32},{1,33},{2,34},{3,35},{4,36},{5,37},{6,38},{7,39},{8,40},{9,... | collective-permute-start | bytes 208904 | tf_op jit(solution)/shard_map/ppermute | solution.py:27
  27.4 13.5 %copy-start.17 = (s32[2,2,700]{2,1,0:T(2,128)S(1)}, s32[2,2,700]{2,1,0:T(2,128)}, u32[]{:S(2)}) copy-start(s32[2,2,700]{2,1,0:T(2,128)} %param.21) | copy-start | bytes 33604
  27.4 27.8 %copy-start.18 = (f32[256]{0:T(256)S(1)}, f32[256]{0:T(256)}, u32[]{:S(2)}) copy-start(f32[256]{0:T(256)} %param.24) | copy-start | bytes 3076
  27.4 27.8 %copy-start.19 = (f32[256]{0:T(256)S(1)}, f32[256]{0:T(256)}, u32[]{:S(2)}) copy-start(f32[256]{0:T(256)} %param.25) | copy-start | bytes 3076
  27.4 27.8 %copy-start.20 = (f32[256]{0:T(256)S(1)}, f32[256]{0:T(256)}, u32[]{:S(2)}) copy-start(f32[256]{0:T(256)} %param.26) | copy-start | bytes 3076
  27.5 27.8 %copy-start.21 = (f32[256]{0:T(256)S(1)}, f32[256]{0:T(256)}, u32[]{:S(2)}) copy-start(f32[256]{0:T(256)} %param.27) | copy-start | bytes 3076
  27.6 52.6 %collective-permute-start.10 = (bf16[4,256,512]{2,1,0:T(8,128)(2,1)S(1)}, bf16[4,256,512]{2,1,0:T(8,128)(2,1)S(1)}, u32[]{:S(2)}, u32[]{:S(2)}) collective-permute-start(bf16[4,256,512]{2,1,0:T(8,128)(2,1)S(1)} %pad_maximum_fusion.refs_8_.refs_4_), channel_id=1, source_target_pairs={{0,192},{1,193},{2,194},{3,195},{4,196},{5,197},{6,198},{7,199},{8... | collective-permute-start | bytes 3145736 | tf_op jit(solution)/shard_map/ppermute | solution.py:27
  32.7 11.4 %collective-permute-start.2 = (bf16[2,136,256]{2,1,0:T(8,128)(2,1)}, bf16[2,136,256]{2,1,0:T(8,128)(2,1)}, u32[]{:S(2)}, u32[]{:S(2)}) collective-permute-start(bf16[2,136,256]{2,1,0:T(8,128)(2,1)} %pad_maximum_fusion.3.refs_0_), channel_id=1, source_target_pairs={{0,16},{1,17},{2,18},{3,19},{4,20},{5,21},{6,22},{7,23},{8,24},{9,... | collective-permute-start | bytes 417800 | tf_op jit(solution)/shard_map/ppermute | solution.py:27
  34.8 48.9 %collective-permute-start.8 = (bf16[4,256,512]{2,1,0:T(8,128)(2,1)S(1)}, bf16[4,256,512]{2,1,0:T(8,128)(2,1)S(1)}, u32[]{:S(2)}, u32[]{:S(2)}) collective-permute-start(bf16[4,256,512]{2,1,0:T(8,128)(2,1)S(1)} %pad_maximum_fusion.refs_8_.refs_4_), channel_id=1, source_target_pairs={{0,64},{1,65},{2,66},{3,67},{4,68},{5,69},{6,70},{7,71},{8,72},{9,... | collective-permute-start | bytes 3145736 | tf_op jit(solution)/shard_map/ppermute | solution.py:27
  38.3 45.5 %collective-permute-start.9 = (bf16[4,256,512]{2,1,0:T(8,128)(2,1)S(1)}, bf16[4,256,512]{2,1,0:T(8,128)(2,1)}, u32[]{:S(2)}, u32[]{:S(2)}) collective-permute-start(bf16[4,256,512]{2,1,0:T(8,128)(2,1)S(1)} %pad_maximum_fusion.refs_8_.refs_4_), channel_id=1, source_target_pairs={{0,128},{1,129},{2,130},{3,131},{4,132},{5,133},{6,134},{7,135},{8... | collective-permute-start | bytes 3145736 | tf_op jit(solution)/shard_map/ppermute | solution.py:27
  40.9 7.9 %collective-permute-start.11 = (bf16[2,136,256]{2,1,0:T(8,128)(2,1)}, bf16[2,136,256]{2,1,0:T(8,128)(2,1)S(1)}, u32[]{:S(2)}, u32[]{:S(2)}) collective-permute-start(bf16[2,136,256]{2,1,0:T(8,128)(2,1)} %pad_maximum_fusion.3.refs_0_), channel_id=1, source_target_pairs={{0,2},{1,3},{2,0},{3,1},{4,6},{5,7},{6,4},{7,5},{8,10},{9,11},{10,... | collective-permute-start | bytes 417800 | tf_op jit(solution)/shard_map/ppermute | solution.py:27
  44.2 8.4 %collective-permute-start.12 = (bf16[2,136,256]{2,1,0:T(8,128)(2,1)}, bf16[2,136,256]{2,1,0:T(8,128)(2,1)S(1)}, u32[]{:S(2)}, u32[]{:S(2)}) collective-permute-start(bf16[2,136,256]{2,1,0:T(8,128)(2,1)} %pad_maximum_fusion.3.refs_0_), channel_id=1, source_target_pairs={{0,4},{1,5},{2,6},{3,7},{4,0},{5,1},{6,2},{7,3},{8,12},{9,13},{10,... | collective-permute-start | bytes 417800 | tf_op jit(solution)/shard_map/ppermute | solution.py:27
  49.6 8.3 %collective-permute-start.13 = (bf16[2,136,256]{2,1,0:T(8,128)(2,1)}, bf16[2,136,256]{2,1,0:T(8,128)(2,1)}, u32[]{:S(2)}, u32[]{:S(2)}) collective-permute-start(bf16[2,136,256]{2,1,0:T(8,128)(2,1)} %pad_maximum_fusion.3.refs_0_), channel_id=1, source_target_pairs={{0,6},{1,7},{2,4},{3,5},{4,2},{5,3},{6,0},{7,1},{8,14},{9,15},{10,... | collective-permute-start | bytes 417800 | tf_op jit(solution)/shard_map/ppermute | solution.py:27
  53.2 8.6 %collective-permute-start.14 = (bf16[2,136,256]{2,1,0:T(8,128)(2,1)}, bf16[2,136,256]{2,1,0:T(8,128)(2,1)}, u32[]{:S(2)}, u32[]{:S(2)}) collective-permute-start(bf16[2,136,256]{2,1,0:T(8,128)(2,1)} %collective-permute-done.2.refs_4_), channel_id=1, source_target_pairs={{0,2},{1,3},{2,0},{3,1},{4,6},{5,7},{6,4},{7,5},{8,10},{9,11},{10,... | collective-permute-start | bytes 417800 | tf_op jit(solution)/shard_map/ppermute | solution.py:27
  57.9 14.8 %collective-permute-start.3 = (bf16[4,136,256]{2,1,0:T(8,128)(2,1)S(1)}, bf16[4,136,256]{2,1,0:T(8,128)(2,1)S(1)}, u32[]{:S(2)}, u32[]{:S(2)}) collective-permute-start(bf16[4,136,256]{2,1,0:T(8,128)(2,1)S(1)} %pad_maximum_fusion.1), channel_id=1, source_target_pairs={{0,8},{1,9},{2,10},{3,11},{4,12},{5,13},{6,14},{7,15},{8,0},{9,1},... | collective-permute-start | bytes 835592 | tf_op jit(solution)/shard_map/ppermute | solution.py:27
  61.8 7.5 %collective-permute-start.15 = (bf16[2,136,256]{2,1,0:T(8,128)(2,1)}, bf16[2,136,256]{2,1,0:T(8,128)(2,1)S(1)}, u32[]{:S(2)}, u32[]{:S(2)}) collective-permute-start(bf16[2,136,256]{2,1,0:T(8,128)(2,1)} %collective-permute-done.2.refs_4_), channel_id=1, source_target_pairs={{0,4},{1,5},{2,6},{3,7},{4,0},{5,1},{6,2},{7,3},{8,12},{9,13},{10,... | collective-permute-start | bytes 417800 | tf_op jit(solution)/shard_map/ppermute | solution.py:27
  69.3 7.5 %collective-permute-start.16 = (bf16[2,136,256]{2,1,0:T(8,128)(2,1)}, bf16[2,136,256]{2,1,0:T(8,128)(2,1)S(1)}, u32[]{:S(2)}, u32[]{:S(2)}) collective-permute-start(bf16[2,136,256]{2,1,0:T(8,128)(2,1)} %collective-permute-done.2.refs_4_), channel_id=1, source_target_pairs={{0,6},{1,7},{2,4},{3,5},{4,2},{5,3},{6,0},{7,1},{8,14},{9,15},{10,... | collective-permute-start | bytes 417800 | tf_op jit(solution)/shard_map/ppermute | solution.py:27
  72.6 15.2 %collective-permute-start.4 = (bf16[4,136,256]{2,1,0:T(8,128)(2,1)S(1)}, bf16[4,136,256]{2,1,0:T(8,128)(2,1)S(1)}, u32[]{:S(2)}, u32[]{:S(2)}) collective-permute-start(bf16[4,136,256]{2,1,0:T(8,128)(2,1)S(1)} %collective-permute-done.3.refs_0_), channel_id=1, source_target_pairs={{0,2},{1,3},{2,0},{3,1},{4,6},{5,7},{6,4},{7,5},{8,10},{9,11},{10,... | collective-permute-start | bytes 835592 | tf_op jit(solution)/shard_map/ppermute | solution.py:27
  76.8 11.1 %collective-permute-start.5 = (bf16[4,136,256]{2,1,0:T(8,128)(2,1)S(1)}, bf16[4,136,256]{2,1,0:T(8,128)(2,1)S(1)}, u32[]{:S(2)}, u32[]{:S(2)}) collective-permute-start(bf16[4,136,256]{2,1,0:T(8,128)(2,1)S(1)} %collective-permute-done.3.refs_0_), channel_id=1, source_target_pairs={{0,4},{1,5},{2,6},{3,7},{4,0},{5,1},{6,2},{7,3},{8,12},{9,13},{10,... | collective-permute-start | bytes 835592 | tf_op jit(solution)/shard_map/ppermute | solution.py:27
  80.2 13.6 %collective-permute-start.6 = (bf16[4,136,256]{2,1,0:T(8,128)(2,1)S(1)}, bf16[4,136,256]{2,1,0:T(8,128)(2,1)S(1)}, u32[]{:S(2)}, u32[]{:S(2)}) collective-permute-start(bf16[4,136,256]{2,1,0:T(8,128)(2,1)S(1)} %collective-permute-done.3.refs_0_), channel_id=1, source_target_pairs={{0,6},{1,7},{2,4},{3,5},{4,2},{5,3},{6,0},{7,1},{8,14},{9,15},{10,... | collective-permute-start | bytes 835592 | tf_op jit(solution)/shard_map/ppermute | solution.py:27
  93.8 25.2 %copy-start.2 = (bf16[64,4,256]{2,1,0:T(4,128)(2,1)S(1)}, bf16[64,4,256]{2,1,0:T(4,128)(2,1)}, u32[]{:S(2)}) copy-start(bf16[64,4,256]{2,1,0:T(4,128)(2,1)} %refs_9_.3) | copy-start | bytes 393220
  93.8 25.2 %copy-start.3 = (bf16[64,4,256]{2,1,0:T(4,128)(2,1)S(1)}, bf16[64,4,256]{2,1,0:T(4,128)(2,1)}, u32[]{:S(2)}) copy-start(bf16[64,4,256]{2,1,0:T(4,128)(2,1)} %refs_8_.3) | copy-start | bytes 393220
  93.8 25.2 %copy-start.5 = (bf16[136,256]{1,0:T(8,128)(2,1)S(1)}, bf16[136,256]{1,0:T(8,128)(2,1)}, u32[]{:S(2)}) copy-start(bf16[136,256]{1,0:T(8,128)(2,1)} %copy-done.4) | copy-start | bytes 208900
  93.8 25.2 %copy-start.10 = (f32[64,2,256]{2,1,0:T(2,128)S(1)}, f32[64,2,256]{2,1,0:T(2,128)}, u32[]{:S(2)}) copy-start(f32[64,2,256]{2,1,0:T(2,128)} %refs_3_.1) | copy-start | bytes 393220
  93.8 25.2 %copy-start.11 = (f32[64,2,256]{2,1,0:T(2,128)S(1)}, f32[64,2,256]{2,1,0:T(2,128)}, u32[]{:S(2)}) copy-start(f32[64,2,256]{2,1,0:T(2,128)} %refs_4_.1) | copy-start | bytes 393220
  93.8 25.2 %copy-start.13 = (s32[64,2]{0,1:T(2,128)S(1)}, s32[64,2]{0,1:T(2,128)}, u32[]{:S(2)}) copy-start(s32[64,2]{0,1:T(2,128)} %param.22) | copy-start | bytes 1540
  93.8 25.2 %copy-start.14 = (s32[64]{0:T(128)S(1)}, s32[64]{0:T(128)}, u32[]{:S(2)}) copy-start(s32[64]{0:T(128)} %param.23) | copy-start | bytes 772
  95.9 5.6 %collective-permute-start.17 = (f32[2,136,256]{2,1,0:T(8,128)S(1)}, f32[2,136,256]{2,1,0:T(8,128)S(1)}, u32[]{:S(2)}, u32[]{:S(2)}) collective-permute-start(f32[2,136,256]{2,1,0:T(8,128)S(1)} %get-tuple-element.26), channel_id=1, source_target_pairs={{0,1},{1,0},{2,3},{3,2},{4,5},{5,4},{6,7},{7,6},{8,9},{9,8},{10,11... | collective-permute-start | bytes 835592 | tf_op jit(solution)/shard_map/ppermute | solution.py:27
  101.6 17.4 %collective-permute-start.18 = (bf16[136,256]{1,0:T(8,128)(2,1)S(1)}, bf16[136,256]{1,0:T(8,128)(2,1)S(1)}, u32[]{:S(2)}, u32[]{:S(2)}) collective-permute-start(bf16[136,256]{1,0:T(8,128)(2,1)S(1)} %get-tuple-element.28), channel_id=1, source_target_pairs={{0,256},{1,257},{2,258},{3,259},{4,260},{5,261},{6,262},{7,263},{8... | collective-permute-start | bytes 208904 | tf_op jit(solution)/shard_map/ppermute | solution.py:27
  120.0 0.7 collective-permute-start.19
  120.6 18.1 %collective-permute-start.20 = (bf16[1,136,256]{2,1,0:T(8,128)(2,1)S(1)}, bf16[1,136,256]{2,1,0:T(8,128)(2,1)S(1)}, u32[]{:S(2)}, u32[]{:S(2)}) collective-permute-start(bf16[1,136,256]{2,1,0:T(8,128)(2,1)S(1)} %bitcast.42), channel_id=1, source_target_pairs={{0,32},{1,33},{2,34},{3,35},{4,36},{5,37},{6,38},{7,39},{8,40},{9,... | collective-permute-start | bytes 208904 | tf_op jit(solution)/shard_map/ppermute | solution.py:27
  138.8 6.7 %collective-permute-start.21 = (bf16[2,136,256]{2,1,0:T(8,128)(2,1)S(1)}, bf16[2,136,256]{2,1,0:T(8,128)(2,1)S(1)}, u32[]{:S(2)}, u32[]{:S(2)}) collective-permute-start(bf16[2,136,256]{2,1,0:T(8,128)(2,1)S(1)} %pad_maximum_fusion.4.refs_0_), channel_id=1, source_target_pairs={{0,16},{1,17},{2,18},{3,19},{4,20},{5,21},{6,22},{7,23},{8,24},{9,... | collective-permute-start | bytes 417800 | tf_op jit(solution)/shard_map/ppermute | solution.py:27
  145.5 22.3 %collective-permute-start.22 = (bf16[4,136,256]{2,1,0:T(8,128)(2,1)S(1)}, bf16[4,136,256]{2,1,0:T(8,128)(2,1)S(1)}, u32[]{:S(2)}, u32[]{:S(2)}) collective-permute-start(bf16[4,136,256]{2,1,0:T(8,128)(2,1)S(1)} %pad_maximum_fusion.2), channel_id=1, source_target_pairs={{0,8},{1,9},{2,10},{3,11},{4,12},{5,13},{6,14},{7,15},{8,0},{9,1},... | collective-permute-start | bytes 835592 | tf_op jit(solution)/shard_map/ppermute | solution.py:27
  156.3 14.9 %collective-permute-start.26 = (bf16[2,136,256]{2,1,0:T(8,128)(2,1)S(1)}, bf16[2,136,256]{2,1,0:T(8,128)(2,1)S(1)}, u32[]{:S(2)}, u32[]{:S(2)}) collective-permute-start(bf16[2,136,256]{2,1,0:T(8,128)(2,1)S(1)} %pad_maximum_fusion.4.refs_0_), channel_id=1, source_target_pairs={{0,2},{1,3},{2,0},{3,1},{4,6},{5,7},{6,4},{7,5},{8,10},{9,11},{10,... | collective-permute-start | bytes 417800 | tf_op jit(solution)/shard_map/ppermute | solution.py:27
  158.9 15.6 %collective-permute-start.27 = (bf16[2,136,256]{2,1,0:T(8,128)(2,1)S(1)}, bf16[2,136,256]{2,1,0:T(8,128)(2,1)S(1)}, u32[]{:S(2)}, u32[]{:S(2)}) collective-permute-start(bf16[2,136,256]{2,1,0:T(8,128)(2,1)S(1)} %pad_maximum_fusion.4.refs_0_), channel_id=1, source_target_pairs={{0,4},{1,5},{2,6},{3,7},{4,0},{5,1},{6,2},{7,3},{8,12},{9,13},{10,... | collective-permute-start | bytes 417800 | tf_op jit(solution)/shard_map/ppermute | solution.py:27
  162.9 14.6 %collective-permute-start.28 = (bf16[2,136,256]{2,1,0:T(8,128)(2,1)S(1)}, bf16[2,136,256]{2,1,0:T(8,128)(2,1)S(1)}, u32[]{:S(2)}, u32[]{:S(2)}) collective-permute-start(bf16[2,136,256]{2,1,0:T(8,128)(2,1)S(1)} %pad_maximum_fusion.4.refs_0_), channel_id=1, source_target_pairs={{0,6},{1,7},{2,4},{3,5},{4,2},{5,3},{6,0},{7,1},{8,14},{9,15},{10,... | collective-permute-start | bytes 417800 | tf_op jit(solution)/shard_map/ppermute | solution.py:27
  165.9 15.1 %collective-permute-start.29 = (bf16[2,136,256]{2,1,0:T(8,128)(2,1)S(1)}, bf16[2,136,256]{2,1,0:T(8,128)(2,1)S(1)}, u32[]{:S(2)}, u32[]{:S(2)}) collective-permute-start(bf16[2,136,256]{2,1,0:T(8,128)(2,1)S(1)} %collective-permute-done.21.refs_4_), channel_id=1, source_target_pairs={{0,2},{1,3},{2,0},{3,1},{4,6},{5,7},{6,4},{7,5},{8,10},{9,11},{10,... | collective-permute-start | bytes 417800 | tf_op jit(solution)/shard_map/ppermute | solution.py:27
  167.8 30.7 %collective-permute-start.23 = (bf16[4,136,256]{2,1,0:T(8,128)(2,1)S(1)}, bf16[4,136,256]{2,1,0:T(8,128)(2,1)S(1)}, u32[]{:S(2)}, u32[]{:S(2)}) collective-permute-start(bf16[4,136,256]{2,1,0:T(8,128)(2,1)S(1)} %collective-permute-done.22.refs_0_), channel_id=1, source_target_pairs={{0,2},{1,3},{2,0},{3,1},{4,6},{5,7},{6,4},{7,5},{8,10},{9,11},{10,... | collective-permute-start | bytes 835592 | tf_op jit(solution)/shard_map/ppermute | solution.py:27
  171.2 27.3 %collective-permute-start.24 = (bf16[4,136,256]{2,1,0:T(8,128)(2,1)S(1)}, bf16[4,136,256]{2,1,0:T(8,128)(2,1)S(1)}, u32[]{:S(2)}, u32[]{:S(2)}) collective-permute-start(bf16[4,136,256]{2,1,0:T(8,128)(2,1)S(1)} %collective-permute-done.22.refs_0_), channel_id=1, source_target_pairs={{0,4},{1,5},{2,6},{3,7},{4,0},{5,1},{6,2},{7,3},{8,12},{9,13},{10,... | collective-permute-start | bytes 835592 | tf_op jit(solution)/shard_map/ppermute | solution.py:27
  174.5 24.0 %collective-permute-start.25 = (bf16[4,136,256]{2,1,0:T(8,128)(2,1)S(1)}, bf16[4,136,256]{2,1,0:T(8,128)(2,1)S(1)}, u32[]{:S(2)}, u32[]{:S(2)}) collective-permute-start(bf16[4,136,256]{2,1,0:T(8,128)(2,1)S(1)} %collective-permute-done.22.refs_0_), channel_id=1, source_target_pairs={{0,6},{1,7},{2,4},{3,5},{4,2},{5,3},{6,0},{7,1},{8,14},{9,15},{10,... | collective-permute-start | bytes 835592 | tf_op jit(solution)/shard_map/ppermute | solution.py:27
  177.5 11.1 %collective-permute-start.30 = (bf16[2,136,256]{2,1,0:T(8,128)(2,1)S(1)}, bf16[2,136,256]{2,1,0:T(8,128)(2,1)S(1)}, u32[]{:S(2)}, u32[]{:S(2)}) collective-permute-start(bf16[2,136,256]{2,1,0:T(8,128)(2,1)S(1)} %collective-permute-done.21.refs_4_), channel_id=1, source_target_pairs={{0,4},{1,5},{2,6},{3,7},{4,0},{5,1},{6,2},{7,3},{8,12},{9,13},{10,... | collective-permute-start | bytes 417800 | tf_op jit(solution)/shard_map/ppermute | solution.py:27
  180.9 15.5 %collective-permute-start.31 = (bf16[2,136,256]{2,1,0:T(8,128)(2,1)S(1)}, bf16[2,136,256]{2,1,0:T(8,128)(2,1)S(1)}, u32[]{:S(2)}, u32[]{:S(2)}) collective-permute-start(bf16[2,136,256]{2,1,0:T(8,128)(2,1)S(1)} %collective-permute-done.21.refs_4_), channel_id=1, source_target_pairs={{0,6},{1,7},{2,4},{3,5},{4,2},{5,3},{6,0},{7,1},{8,14},{9,15},{10,... | collective-permute-start | bytes 417800 | tf_op jit(solution)/shard_map/ppermute | solution.py:27
  200.5 4.8 %collective-permute-start.32 = (f32[2,136,256]{2,1,0:T(8,128)S(1)}, f32[2,136,256]{2,1,0:T(8,128)S(1)}, u32[]{:S(2)}, u32[]{:S(2)}) collective-permute-start(f32[2,136,256]{2,1,0:T(8,128)S(1)} %get-tuple-element.34), channel_id=1, source_target_pairs={{0,1},{1,0},{2,3},{3,2},{4,5},{5,4},{6,7},{7,6},{8,9},{9,8},{10,11... | collective-permute-start | bytes 835592 | tf_op jit(solution)/shard_map/ppermute | solution.py:27
  205.4 18.1 %collective-permute-start.33 = (bf16[136,256]{1,0:T(8,128)(2,1)S(1)}, bf16[136,256]{1,0:T(8,128)(2,1)S(1)}, u32[]{:S(2)}, u32[]{:S(2)}) collective-permute-start(bf16[136,256]{1,0:T(8,128)(2,1)S(1)} %get-tuple-element.36), channel_id=1, source_target_pairs={{0,256},{1,257},{2,258},{3,259},{4,260},{5,261},{6,262},{7,263},{8... | collective-permute-start | bytes 208904 | tf_op jit(solution)/shard_map/ppermute | solution.py:27
  (8 other events, 9.9 us)

commit v4 on v3

--- a/solution.py
+++ b/solution.py
@@ -326,9 +326,14 @@
         if step == 0:
             held, place, lanes = lax.optimization_barrier((held, place, lanes))
         last = [over_b(held, 1)]
-        for pieces in (first, second, last):
-            for k in (1, 2, 3):
-                pieces.append(over_y(pieces[0], k))
+        for pieces, near, far in ((first, 1, 3), (second, 3, 1)):
+            came = {}
+            for k in (near, far):
+                came[k] = over_y(pieces[0], k)
+            came[2] = over_y(came[near], far)
+            pieces += [came[k] for k in (1, 2, 3)]
+        for k in (1, 2, 3):
+            last.append(over_y(last[0], k))
         halves = mix(place, first + second, weights, rows, trials)
         mine, theirs = mix(place, last, weights, rows, trials, halves)
         theirs = over_c(theirs)

time: 226 us -> 218 us (0.965)
  the two profiles are of different devices: /device:TPU:35 before, /device:TPU:33 now
where the time goes in v4:
time: 218 us; the launch traced here: 216 us
  starting transfers between devices  157 us (72%)
  waiting for transfers between devices  41.8 us (19%)
  Pallas kernels  10.5 us (5%)
  local copies, waits for them, and re-layouts  3.83 us (2%)
    ppermute x34, starting transfers between devices, permute(): return lax.ppermute(value, AXES, pairs)  157 us
    ppermute x34, waiting for transfers between devices, permute(): return lax.ppermute(value, AXES, pairs)  41.8 us
    pallas_call x4, Pallas kernels, mix(): pl.pallas_call(functools.partial(mix_kernel, pieces=len(spikes) // 4, row...  8.38 us
  transfers between devices with their start and end apart: 34, of which 15 were waited for; matrix products, arithmetic and copies ran while one was open for 1% of the time, Pallas kernels for 2%

profile of v4, /device:TPU:33, one launch (start us, length us, event | category | flops | bytes accessed | tf_op | source)
XLA Modules:
  0.0 216.4 jit_solution(9186013088856153046)
XLA Ops:
  0.6 1.5 copy.16
  2.3 2.6 %collective-permute-start.7 = (bf16[4,256,256]{2,1,0:T(8,128)(2,1)S(1)}, bf16[4,256,256]{2,1,0:T(8,128)(2,1)S(1)}, u32[]{:S(2)}, u32[]{:S(2)}) collective-permute-start(bf16[4,256,256]{2,1,0:T(8,128)(2,1)S(1)} %get-tuple-element.41), channel_id=1, source_target_pairs={{0,1},{1,0},{2,3},{3,2},{4,5},{5,4},{6,7},{7,6},{8,9},{9,8},{10,11... | collective-permute-start | bytes 1572872 | tf_op jit(solution)/shard_map/ppermute | solution.py:27
  6.4 20.9 %collective-permute-start.1 = (bf16[1,136,256]{2,1,0:T(8,128)(2,1)S(1)}, bf16[1,136,256]{2,1,0:T(8,128)(2,1)S(1)}, u32[]{:S(2)}, u32[]{:S(2)}) collective-permute-start(bf16[1,136,256]{2,1,0:T(8,128)(2,1)S(1)} %bitcast.39), channel_id=1, source_target_pairs={{0,32},{1,33},{2,34},{3,35},{4,36},{5,37},{6,38},{7,39},{8,40},{9,... | collective-permute-start | bytes 208904 | tf_op jit(solution)/shard_map/ppermute | solution.py:27
  27.5 4.4 %collective-permute-start.10 = (bf16[4,256,512]{2,1,0:T(8,128)(2,1)S(1)}, bf16[4,256,512]{2,1,0:T(8,128)(2,1)S(1)}, u32[]{:S(2)}, u32[]{:S(2)}) collective-permute-start(bf16[4,256,512]{2,1,0:T(8,128)(2,1)S(1)} %pad_maximum_fusion.refs_8_.refs_4_), channel_id=1, source_target_pairs={{0,192},{1,193},{2,194},{3,195},{4,196},{5,197},{6,198},{7,199},{8... | collective-permute-start | bytes 3145736 | tf_op jit(solution)/shard_map/ppermute | solution.py:27
  32.7 3.3 %collective-permute-start.2 = (bf16[2,136,256]{2,1,0:T(8,128)(2,1)}, bf16[2,136,256]{2,1,0:T(8,128)(2,1)}, u32[]{:S(2)}, u32[]{:S(2)}) collective-permute-start(bf16[2,136,256]{2,1,0:T(8,128)(2,1)} %pad_maximum_fusion.3.refs_0_), channel_id=1, source_target_pairs={{0,16},{1,17},{2,18},{3,19},{4,20},{5,21},{6,22},{7,23},{8,24},{9,... | collective-permute-start | bytes 417800 | tf_op jit(solution)/shard_map/ppermute | solution.py:27
  36.1 1.9 collective-permute-start.8
  38.0 4.1 %collective-permute-start.9 = (bf16[4,256,512]{2,1,0:T(8,128)(2,1)S(1)}, bf16[4,256,512]{2,1,0:T(8,128)(2,1)}, u32[]{:S(2)}, u32[]{:S(2)}) collective-permute-start(bf16[4,256,512]{2,1,0:T(8,128)(2,1)S(1)} %pad_maximum_fusion.refs_8_.refs_4_), channel_id=1, source_target_pairs={{0,128},{1,129},{2,130},{3,131},{4,132},{5,133},{6,134},{7,135},{8... | collective-permute-start | bytes 3145736 | tf_op jit(solution)/shard_map/ppermute | solution.py:27
  42.2 3.2 %collective-permute-start.11 = (bf16[2,136,256]{2,1,0:T(8,128)(2,1)}, bf16[2,136,256]{2,1,0:T(8,128)(2,1)}, u32[]{:S(2)}, u32[]{:S(2)}) collective-permute-start(bf16[2,136,256]{2,1,0:T(8,128)(2,1)} %pad_maximum_fusion.3.refs_0_), channel_id=1, source_target_pairs={{0,2},{1,3},{2,0},{3,1},{4,6},{5,7},{6,4},{7,5},{8,10},{9,11},{10,... | collective-permute-start | bytes 417800 | tf_op jit(solution)/shard_map/ppermute | solution.py:27
  45.4 3.8 %collective-permute-start.13 = (bf16[2,136,256]{2,1,0:T(8,128)(2,1)}, bf16[2,136,256]{2,1,0:T(8,128)(2,1)S(1)}, u32[]{:S(2)}, u32[]{:S(2)}) collective-permute-start(bf16[2,136,256]{2,1,0:T(8,128)(2,1)} %pad_maximum_fusion.3.refs_0_), channel_id=1, source_target_pairs={{0,6},{1,7},{2,4},{3,5},{4,2},{5,3},{6,0},{7,1},{8,14},{9,15},{10,... | collective-permute-start | bytes 417800 | tf_op jit(solution)/shard_map/ppermute | solution.py:27
  49.4 3.7 %collective-permute-start.15 = (bf16[2,136,256]{2,1,0:T(8,128)(2,1)}, bf16[2,136,256]{2,1,0:T(8,128)(2,1)}, u32[]{:S(2)}, u32[]{:S(2)}) collective-permute-start(bf16[2,136,256]{2,1,0:T(8,128)(2,1)} %collective-permute-done.2.refs_4_), channel_id=1, source_target_pairs={{0,6},{1,7},{2,4},{3,5},{4,2},{5,3},{6,0},{7,1},{8,14},{9,15},{10,... | collective-permute-start | bytes 417800 | tf_op jit(solution)/shard_map/ppermute | solution.py:27
  53.8 1.9 collective-permute-start.14
  57.9 3.9 %collective-permute-start.3 = (bf16[4,136,256]{2,1,0:T(8,128)(2,1)S(1)}, bf16[4,136,256]{2,1,0:T(8,128)(2,1)S(1)}, u32[]{:S(2)}, u32[]{:S(2)}) collective-permute-start(bf16[4,136,256]{2,1,0:T(8,128)(2,1)S(1)} %pad_maximum_fusion.1), channel_id=1, source_target_pairs={{0,8},{1,9},{2,10},{3,11},{4,12},{5,13},{6,14},{7,15},{8,0},{9,1},... | collective-permute-start | bytes 835592 | tf_op jit(solution)/shard_map/ppermute | solution.py:27
  61.8 3.6 %collective-permute-start.12 = (bf16[2,136,256]{2,1,0:T(8,128)(2,1)}, bf16[2,136,256]{2,1,0:T(8,128)(2,1)S(1)}, u32[]{:S(2)}, u32[]{:S(2)}) collective-permute-start(bf16[2,136,256]{2,1,0:T(8,128)(2,1)} %collective-permute-done.11.refs_1_), channel_id=1, source_target_pairs={{0,6},{1,7},{2,4},{3,5},{4,2},{5,3},{6,0},{7,1},{8,14},{9,15},{10,... | collective-permute-start | bytes 417800 | tf_op jit(solution)/shard_map/ppermute | solution.py:27
  65.4 4.0 %collective-permute-done.12.refs_2_ = bf16[2,136,256]{2,1,0:T(8,128)(2,1)S(1)} collective-permute-done((bf16[2,136,256]{2,1,0:T(8,128)(2,1)}, bf16[2,136,256]{2,1,0:T(8,128)(2,1)S(1)}, u32[]{:S(2)}, u32[]{:S(2)}) %collective-permute-start.12) | collective-permute-done | bytes 139296 | tf_op jit(solution)/shard_map/ppermute | solution.py:27
  69.4 2.1 collective-permute-start.16
  71.6 3.1 %collective-permute-start.4 = (bf16[4,136,256]{2,1,0:T(8,128)(2,1)S(1)}, bf16[4,136,256]{2,1,0:T(8,128)(2,1)S(1)}, u32[]{:S(2)}, u32[]{:S(2)}) collective-permute-start(bf16[4,136,256]{2,1,0:T(8,128)(2,1)S(1)} %collective-permute-done.3.refs_0_), channel_id=1, source_target_pairs={{0,2},{1,3},{2,0},{3,1},{4,6},{5,7},{6,4},{7,5},{8,10},{9,11},{10,... | collective-permute-start | bytes 835592 | tf_op jit(solution)/shard_map/ppermute | solution.py:27
  75.8 3.5 %collective-permute-start.5 = (bf16[4,136,256]{2,1,0:T(8,128)(2,1)S(1)}, bf16[4,136,256]{2,1,0:T(8,128)(2,1)S(1)}, u32[]{:S(2)}, u32[]{:S(2)}) collective-permute-start(bf16[4,136,256]{2,1,0:T(8,128)(2,1)S(1)} %collective-permute-done.3.refs_0_), channel_id=1, source_target_pairs={{0,4},{1,5},{2,6},{3,7},{4,0},{5,1},{6,2},{7,3},{8,12},{9,13},{10,... | collective-permute-start | bytes 835592 | tf_op jit(solution)/shard_map/ppermute | solution.py:27
  79.4 2.9 %collective-permute-start.6 = (bf16[4,136,256]{2,1,0:T(8,128)(2,1)S(1)}, bf16[4,136,256]{2,1,0:T(8,128)(2,1)S(1)}, u32[]{:S(2)}, u32[]{:S(2)}) collective-permute-start(bf16[4,136,256]{2,1,0:T(8,128)(2,1)S(1)} %collective-permute-done.3.refs_0_), channel_id=1, source_target_pairs={{0,6},{1,7},{2,4},{3,5},{4,2},{5,3},{6,0},{7,1},{8,14},{9,15},{10,... | collective-permute-start | bytes 835592 | tf_op jit(solution)/shard_map/ppermute | solution.py:27
  83.7 2.3 %mix_early.2 = (f32[2,136,256]{2,1,0:T(8,128)S(1)}, f32[2,136,256]{2,1,0:T(8,128)S(1)}) custom-call(s32[3]{0:T(128)S(1)} %pad_add_fusion.at_ref, bf16[2,136,256]{2,1,0:T(8,128)(2,1)} %pad_maximum_fusion.3.refs_0_, bf16[2,136,256]{2,1,0:T(8,128)(2,1)} %collective-permute-done.11.refs_1_, bf16[2,136,256]{2,1,0:T(8,128)(2,1)S(1)} %collective-permute-done.12.refs_2_, ...), custom_call_target="tpu_custom_call" | custom-call | flops 570425344 | bytes 3768320 | tf_op jit(solution)/shard_map/mix_early/pallas_call | solution.py:231
  86.0 1.6 collective-permute-done.5.refs_2_
  87.6 1.9 collective-permute-done.6.refs_3_
  89.6 2.1 mix_late.2
  91.7 8.8 %collective-permute-start.17 = (f32[2,136,256]{2,1,0:T(8,128)S(1)}, f32[2,136,256]{2,1,0:T(8,128)S(1)}, u32[]{:S(2)}, u32[]{:S(2)}) collective-permute-start(f32[2,136,256]{2,1,0:T(8,128)S(1)} %get-tuple-element.26), channel_id=1, source_target_pairs={{0,1},{1,0},{2,3},{3,2},{4,5},{5,4},{6,7},{7,6},{8,9},{9,8},{10,11... | collective-permute-start | bytes 835592 | tf_op jit(solution)/shard_map/ppermute | solution.py:27
  100.5 1.2 collective-permute-done.17.theirs_ref
  101.7 11.3 %collective-permute-start.18 = (bf16[136,256]{1,0:T(8,128)(2,1)S(1)}, bf16[136,256]{1,0:T(8,128)(2,1)S(1)}, u32[]{:S(2)}, u32[]{:S(2)}) collective-permute-start(bf16[136,256]{1,0:T(8,128)(2,1)S(1)} %get-tuple-element.28), channel_id=1, source_target_pairs={{0,256},{1,257},{2,258},{3,259},{4,260},{5,261},{6,262},{7,263},{8... | collective-permute-start | bytes 208904 | tf_op jit(solution)/shard_map/ppermute | solution.py:27
  113.0 2.7 %collective-permute-done.18.refs_1_ = bf16[136,256]{1,0:T(8,128)(2,1)S(1)} collective-permute-done((bf16[136,256]{1,0:T(8,128)(2,1)S(1)}, bf16[136,256]{1,0:T(8,128)(2,1)S(1)}, u32[]{:S(2)}, u32[]{:S(2)}) %collective-permute-start.18) | collective-permute-done | bytes 69664 | tf_op jit(solution)/shard_map/ppermute | solution.py:27
  117.4 18.6 %collective-permute-start.20 = (bf16[1,136,256]{2,1,0:T(8,128)(2,1)S(1)}, bf16[1,136,256]{2,1,0:T(8,128)(2,1)S(1)}, u32[]{:S(2)}, u32[]{:S(2)}) collective-permute-start(bf16[1,136,256]{2,1,0:T(8,128)(2,1)S(1)} %bitcast.42), channel_id=1, source_target_pairs={{0,32},{1,33},{2,34},{3,35},{4,36},{5,37},{6,38},{7,39},{8,40},{9,... | collective-permute-start | bytes 208904 | tf_op jit(solution)/shard_map/ppermute | solution.py:27
  136.0 4.2 %collective-permute-done.20 = bf16[1,136,256]{2,1,0:T(8,128)(2,1)S(1)} collective-permute-done((bf16[1,136,256]{2,1,0:T(8,128)(2,1)S(1)}, bf16[1,136,256]{2,1,0:T(8,128)(2,1)S(1)}, u32[]{:S(2)}, u32[]{:S(2)}) %collective-permute-start.20) | collective-permute-done | bytes 69664 | tf_op jit(solution)/shard_map/ppermute | solution.py:27
  140.2 1.9 collective-permute-start.21
  142.1 5.5 %collective-permute-done.21.refs_4_ = bf16[2,136,256]{2,1,0:T(8,128)(2,1)S(1)} collective-permute-done((bf16[2,136,256]{2,1,0:T(8,128)(2,1)S(1)}, bf16[2,136,256]{2,1,0:T(8,128)(2,1)S(1)}, u32[]{:S(2)}, u32[]{:S(2)}) %collective-permute-start.21) | collective-permute-done | bytes 139296 | tf_op jit(solution)/shard_map/ppermute | solution.py:27
  147.7 7.0 %collective-permute-start.22 = (bf16[4,136,256]{2,1,0:T(8,128)(2,1)S(1)}, bf16[4,136,256]{2,1,0:T(8,128)(2,1)S(1)}, u32[]{:S(2)}, u32[]{:S(2)}) collective-permute-start(bf16[4,136,256]{2,1,0:T(8,128)(2,1)S(1)} %pad_maximum_fusion.2), channel_id=1, source_target_pairs={{0,8},{1,9},{2,10},{3,11},{4,12},{5,13},{6,14},{7,15},{8,0},{9,1},... | collective-permute-start | bytes 835592 | tf_op jit(solution)/shard_map/ppermute | solution.py:27
  154.7 2.3 %collective-permute-start.26 = (bf16[2,136,256]{2,1,0:T(8,128)(2,1)S(1)}, bf16[2,136,256]{2,1,0:T(8,128)(2,1)S(1)}, u32[]{:S(2)}, u32[]{:S(2)}) collective-permute-start(bf16[2,136,256]{2,1,0:T(8,128)(2,1)S(1)} %pad_maximum_fusion.4.refs_0_), channel_id=1, source_target_pairs={{0,2},{1,3},{2,0},{3,1},{4,6},{5,7},{6,4},{7,5},{8,10},{9,11},{10,... | collective-permute-start | bytes 417800 | tf_op jit(solution)/shard_map/ppermute | solution.py:27
  157.0 3.7 %collective-permute-start.28 = (bf16[2,136,256]{2,1,0:T(8,128)(2,1)S(1)}, bf16[2,136,256]{2,1,0:T(8,128)(2,1)S(1)}, u32[]{:S(2)}, u32[]{:S(2)}) collective-permute-start(bf16[2,136,256]{2,1,0:T(8,128)(2,1)S(1)} %pad_maximum_fusion.4.refs_0_), channel_id=1, source_target_pairs={{0,6},{1,7},{2,4},{3,5},{4,2},{5,3},{6,0},{7,1},{8,14},{9,15},{10,... | collective-permute-start | bytes 417800 | tf_op jit(solution)/shard_map/ppermute | solution.py:27
  160.8 2.7 %collective-permute-start.30 = (bf16[2,136,256]{2,1,0:T(8,128)(2,1)S(1)}, bf16[2,136,256]{2,1,0:T(8,128)(2,1)S(1)}, u32[]{:S(2)}, u32[]{:S(2)}) collective-permute-start(bf16[2,136,256]{2,1,0:T(8,128)(2,1)S(1)} %collective-permute-done.21.refs_4_), channel_id=1, source_target_pairs={{0,6},{1,7},{2,4},{3,5},{4,2},{5,3},{6,0},{7,1},{8,14},{9,15},{10,... | collective-permute-start | bytes 417800 | tf_op jit(solution)/shard_map/ppermute | solution.py:27
  163.5 3.7 %collective-permute-start.27 = (bf16[2,136,256]{2,1,0:T(8,128)(2,1)S(1)}, bf16[2,136,256]{2,1,0:T(8,128)(2,1)S(1)}, u32[]{:S(2)}, u32[]{:S(2)}) collective-permute-start(bf16[2,136,256]{2,1,0:T(8,128)(2,1)S(1)} %collective-permute-done.26.refs_1_), channel_id=1, source_target_pairs={{0,6},{1,7},{2,4},{3,5},{4,2},{5,3},{6,0},{7,1},{8,14},{9,15},{10,... | collective-permute-start | bytes 417800 | tf_op jit(solution)/shard_map/ppermute | solution.py:27
  167.3 1.9 collective-permute-start.23
  169.2 3.9 %collective-permute-start.24 = (bf16[4,136,256]{2,1,0:T(8,128)(2,1)S(1)}, bf16[4,136,256]{2,1,0:T(8,128)(2,1)S(1)}, u32[]{:S(2)}, u32[]{:S(2)}) collective-permute-start(bf16[4,136,256]{2,1,0:T(8,128)(2,1)S(1)} %collective-permute-done.22.refs_0_), channel_id=1, source_target_pairs={{0,4},{1,5},{2,6},{3,7},{4,0},{5,1},{6,2},{7,3},{8,12},{9,13},{10,... | collective-permute-start | bytes 835592 | tf_op jit(solution)/shard_map/ppermute | solution.py:27
  173.2 3.7 %collective-permute-start.25 = (bf16[4,136,256]{2,1,0:T(8,128)(2,1)S(1)}, bf16[4,136,256]{2,1,0:T(8,128)(2,1)S(1)}, u32[]{:S(2)}, u32[]{:S(2)}) collective-permute-start(bf16[4,136,256]{2,1,0:T(8,128)(2,1)S(1)} %collective-permute-done.22.refs_0_), channel_id=1, source_target_pairs={{0,6},{1,7},{2,4},{3,5},{4,2},{5,3},{6,0},{7,1},{8,14},{9,15},{10,... | collective-permute-start | bytes 835592 | tf_op jit(solution)/shard_map/ppermute | solution.py:27
  176.9 1.9 collective-permute-start.29
  178.9 3.4 %collective-permute-start.31 = (bf16[2,136,256]{2,1,0:T(8,128)(2,1)S(1)}, bf16[2,136,256]{2,1,0:T(8,128)(2,1)S(1)}, u32[]{:S(2)}, u32[]{:S(2)}) collective-permute-start(bf16[2,136,256]{2,1,0:T(8,128)(2,1)S(1)} %collective-permute-done.30.refs_7_), channel_id=1, source_target_pairs={{0,2},{1,3},{2,0},{3,1},{4,6},{5,7},{6,4},{7,5},{8,10},{9,11},{10,... | collective-permute-start | bytes 417800 | tf_op jit(solution)/shard_map/ppermute | solution.py:27
  182.2 2.6 %collective-permute-done.29.refs_5_ = bf16[2,136,256]{2,1,0:T(8,128)(2,1)S(1)} collective-permute-done((bf16[2,136,256]{2,1,0:T(8,128)(2,1)S(1)}, bf16[2,136,256]{2,1,0:T(8,128)(2,1)S(1)}, u32[]{:S(2)}, u32[]{:S(2)}) %collective-permute-start.29) | collective-permute-done | bytes 139296 | tf_op jit(solution)/shard_map/ppermute | solution.py:27
  184.8 3.0 %collective-permute-done.31.refs_6_ = bf16[2,136,256]{2,1,0:T(8,128)(2,1)S(1)} collective-permute-done((bf16[2,136,256]{2,1,0:T(8,128)(2,1)S(1)}, bf16[2,136,256]{2,1,0:T(8,128)(2,1)S(1)}, u32[]{:S(2)}, u32[]{:S(2)}) %collective-permute-start.31) | collective-permute-done | bytes 139296 | tf_op jit(solution)/shard_map/ppermute | solution.py:27
  187.8 2.0 mix_early.3
  189.8 2.0 mix_late.3
  191.8 4.4 %collective-permute-start.32 = (f32[2,136,256]{2,1,0:T(8,128)S(1)}, f32[2,136,256]{2,1,0:T(8,128)S(1)}, u32[]{:S(2)}, u32[]{:S(2)}) collective-permute-start(f32[2,136,256]{2,1,0:T(8,128)S(1)} %get-tuple-element.34), channel_id=1, source_target_pairs={{0,1},{1,0},{2,3},{3,2},{4,5},{5,4},{6,7},{7,6},{8,9},{9,8},{10,11... | collective-permute-start | bytes 835592 | tf_op jit(solution)/shard_map/ppermute | solution.py:27
  196.2 1.2 collective-permute-done.32.theirs_ref
  197.4 6.8 %collective-permute-start.33 = (bf16[136,256]{1,0:T(8,128)(2,1)S(1)}, bf16[136,256]{1,0:T(8,128)(2,1)S(1)}, u32[]{:S(2)}, u32[]{:S(2)}) collective-permute-start(bf16[136,256]{1,0:T(8,128)(2,1)S(1)} %get-tuple-element.36), channel_id=1, source_target_pairs={{0,256},{1,257},{2,258},{3,259},{4,260},{5,261},{6,262},{7,263},{8... | collective-permute-start | bytes 208904 | tf_op jit(solution)/shard_map/ppermute | solution.py:27
  204.3 11.2 %collective-permute-done.33.refs_1_ = bf16[136,256]{1,0:T(8,128)(2,1)S(1)} collective-permute-done((bf16[136,256]{1,0:T(8,128)(2,1)S(1)}, bf16[136,256]{1,0:T(8,128)(2,1)S(1)}, u32[]{:S(2)}, u32[]{:S(2)}) %collective-permute-start.33) | collective-permute-done | bytes 69664 | tf_op jit(solution)/shard_map/ppermute | solution.py:27
  (81 shorter events, 10.6 us)
Async XLA Ops:
  0.6 48.6 %copy-start = (bf16[700,256]{1,0:T(8,128)(2,1)S(1)}, bf16[700,256]{1,0:T(8,128)(2,1)}, u32[]{:S(2)}) copy-start(bf16[700,256]{1,0:T(8,128)(2,1)} %param.20) | copy-start | bytes 1075204
  2.3 25.1 %collective-permute-start.7 = (bf16[4,256,256]{2,1,0:T(8,128)(2,1)S(1)}, bf16[4,256,256]{2,1,0:T(8,128)(2,1)S(1)}, u32[]{:S(2)}, u32[]{:S(2)}) collective-permute-start(bf16[4,256,256]{2,1,0:T(8,128)(2,1)S(1)} %get-tuple-element.41), channel_id=1, source_target_pairs={{0,1},{1,0},{2,3},{3,2},{4,5},{5,4},{6,7},{7,6},{8,9},{9,8},{10,11... | collective-permute-start | bytes 1572872 | tf_op jit(solution)/shard_map/ppermute | solution.py:27
  5.1 1.3 collective-permute-start
  6.4 25.6 %copy-start.13 = (bf16[136,256]{1,0:T(8,128)(2,1)}, bf16[136,256]{1,0:T(8,128)(2,1)S(1)}, u32[]{:S(2)}) copy-start(bf16[136,256]{1,0:T(8,128)(2,1)S(1)} %collective-permute-done) | copy-start | bytes 208900
  6.4 25.6 %collective-permute-start.1 = (bf16[1,136,256]{2,1,0:T(8,128)(2,1)S(1)}, bf16[1,136,256]{2,1,0:T(8,128)(2,1)S(1)}, u32[]{:S(2)}, u32[]{:S(2)}) collective-permute-start(bf16[1,136,256]{2,1,0:T(8,128)(2,1)S(1)} %bitcast.39), channel_id=1, source_target_pairs={{0,32},{1,33},{2,34},{3,35},{4,36},{5,37},{6,38},{7,39},{8,40},{9,... | collective-permute-start | bytes 208904 | tf_op jit(solution)/shard_map/ppermute | solution.py:27
  27.4 14.8 %copy-start.15 = (s32[2,2,700]{2,1,0:T(2,128)S(1)}, s32[2,2,700]{2,1,0:T(2,128)}, u32[]{:S(2)}) copy-start(s32[2,2,700]{2,1,0:T(2,128)} %param.21) | copy-start | bytes 33604
  27.4 28.4 %copy-start.16 = (f32[256]{0:T(256)S(1)}, f32[256]{0:T(256)}, u32[]{:S(2)}) copy-start(f32[256]{0:T(256)} %param.24) | copy-start | bytes 3076
  27.4 28.4 %copy-start.17 = (f32[256]{0:T(256)S(1)}, f32[256]{0:T(256)}, u32[]{:S(2)}) copy-start(f32[256]{0:T(256)} %param.25) | copy-start | bytes 3076
  27.4 28.4 %copy-start.18 = (f32[256]{0:T(256)S(1)}, f32[256]{0:T(256)}, u32[]{:S(2)}) copy-start(f32[256]{0:T(256)} %param.26) | copy-start | bytes 3076
  27.4 28.4 %copy-start.19 = (f32[256]{0:T(256)S(1)}, f32[256]{0:T(256)}, u32[]{:S(2)}) copy-start(f32[256]{0:T(256)} %param.27) | copy-start | bytes 3076
  27.5 51.8 %collective-permute-start.10 = (bf16[4,256,512]{2,1,0:T(8,128)(2,1)S(1)}, bf16[4,256,512]{2,1,0:T(8,128)(2,1)S(1)}, u32[]{:S(2)}, u32[]{:S(2)}) collective-permute-start(bf16[4,256,512]{2,1,0:T(8,128)(2,1)S(1)} %pad_maximum_fusion.refs_8_.refs_4_), channel_id=1, source_target_pairs={{0,192},{1,193},{2,194},{3,195},{4,196},{5,197},{6,198},{7,199},{8... | collective-permute-start | bytes 3145736 | tf_op jit(solution)/shard_map/ppermute | solution.py:27
  32.7 12.7 %collective-permute-start.2 = (bf16[2,136,256]{2,1,0:T(8,128)(2,1)}, bf16[2,136,256]{2,1,0:T(8,128)(2,1)}, u32[]{:S(2)}, u32[]{:S(2)}) collective-permute-start(bf16[2,136,256]{2,1,0:T(8,128)(2,1)} %pad_maximum_fusion.3.refs_0_), channel_id=1, source_target_pairs={{0,16},{1,17},{2,18},{3,19},{4,20},{5,21},{6,22},{7,23},{8,24},{9,... | collective-permute-start | bytes 417800 | tf_op jit(solution)/shard_map/ppermute | solution.py:27
  36.1 46.2 %collective-permute-start.8 = (bf16[4,256,512]{2,1,0:T(8,128)(2,1)S(1)}, bf16[4,256,512]{2,1,0:T(8,128)(2,1)S(1)}, u32[]{:S(2)}, u32[]{:S(2)}) collective-permute-start(bf16[4,256,512]{2,1,0:T(8,128)(2,1)S(1)} %pad_maximum_fusion.refs_8_.refs_4_), channel_id=1, source_target_pairs={{0,64},{1,65},{2,66},{3,67},{4,68},{5,69},{6,70},{7,71},{8,72},{9,... | collective-permute-start | bytes 3145736 | tf_op jit(solution)/shard_map/ppermute | solution.py:27
  38.0 44.8 %collective-permute-start.9 = (bf16[4,256,512]{2,1,0:T(8,128)(2,1)S(1)}, bf16[4,256,512]{2,1,0:T(8,128)(2,1)}, u32[]{:S(2)}, u32[]{:S(2)}) collective-permute-start(bf16[4,256,512]{2,1,0:T(8,128)(2,1)S(1)} %pad_maximum_fusion.refs_8_.refs_4_), channel_id=1, source_target_pairs={{0,128},{1,129},{2,130},{3,131},{4,132},{5,133},{6,134},{7,135},{8... | collective-permute-start | bytes 3145736 | tf_op jit(solution)/shard_map/ppermute | solution.py:27
  42.2 7.2 %collective-permute-start.11 = (bf16[2,136,256]{2,1,0:T(8,128)(2,1)}, bf16[2,136,256]{2,1,0:T(8,128)(2,1)}, u32[]{:S(2)}, u32[]{:S(2)}) collective-permute-start(bf16[2,136,256]{2,1,0:T(8,128)(2,1)} %pad_maximum_fusion.3.refs_0_), channel_id=1, source_target_pairs={{0,2},{1,3},{2,0},{3,1},{4,6},{5,7},{6,4},{7,5},{8,10},{9,11},{10,... | collective-permute-start | bytes 417800 | tf_op jit(solution)/shard_map/ppermute | solution.py:27
  45.4 7.7 %collective-permute-start.13 = (bf16[2,136,256]{2,1,0:T(8,128)(2,1)}, bf16[2,136,256]{2,1,0:T(8,128)(2,1)S(1)}, u32[]{:S(2)}, u32[]{:S(2)}) collective-permute-start(bf16[2,136,256]{2,1,0:T(8,128)(2,1)} %pad_maximum_fusion.3.refs_0_), channel_id=1, source_target_pairs={{0,6},{1,7},{2,4},{3,5},{4,2},{5,3},{6,0},{7,1},{8,14},{9,15},{10,... | collective-permute-start | bytes 417800 | tf_op jit(solution)/shard_map/ppermute | solution.py:27
  49.4 8.5 %collective-permute-start.15 = (bf16[2,136,256]{2,1,0:T(8,128)(2,1)}, bf16[2,136,256]{2,1,0:T(8,128)(2,1)}, u32[]{:S(2)}, u32[]{:S(2)}) collective-permute-start(bf16[2,136,256]{2,1,0:T(8,128)(2,1)} %collective-permute-done.2.refs_4_), channel_id=1, source_target_pairs={{0,6},{1,7},{2,4},{3,5},{4,2},{5,3},{6,0},{7,1},{8,14},{9,15},{10,... | collective-permute-start | bytes 417800 | tf_op jit(solution)/shard_map/ppermute | solution.py:27
  53.8 8.0 %collective-permute-start.14 = (bf16[2,136,256]{2,1,0:T(8,128)(2,1)}, bf16[2,136,256]{2,1,0:T(8,128)(2,1)}, u32[]{:S(2)}, u32[]{:S(2)}) collective-permute-start(bf16[2,136,256]{2,1,0:T(8,128)(2,1)} %collective-permute-done.2.refs_4_), channel_id=1, source_target_pairs={{0,2},{1,3},{2,0},{3,1},{4,6},{5,7},{6,4},{7,5},{8,10},{9,11},{10,... | collective-permute-start | bytes 417800 | tf_op jit(solution)/shard_map/ppermute | solution.py:27
  57.9 13.7 %collective-permute-start.3 = (bf16[4,136,256]{2,1,0:T(8,128)(2,1)S(1)}, bf16[4,136,256]{2,1,0:T(8,128)(2,1)S(1)}, u32[]{:S(2)}, u32[]{:S(2)}) collective-permute-start(bf16[4,136,256]{2,1,0:T(8,128)(2,1)S(1)} %pad_maximum_fusion.1), channel_id=1, source_target_pairs={{0,8},{1,9},{2,10},{3,11},{4,12},{5,13},{6,14},{7,15},{8,0},{9,1},... | collective-permute-start | bytes 835592 | tf_op jit(solution)/shard_map/ppermute | solution.py:27
  61.8 7.6 %collective-permute-start.12 = (bf16[2,136,256]{2,1,0:T(8,128)(2,1)}, bf16[2,136,256]{2,1,0:T(8,128)(2,1)S(1)}, u32[]{:S(2)}, u32[]{:S(2)}) collective-permute-start(bf16[2,136,256]{2,1,0:T(8,128)(2,1)} %collective-permute-done.11.refs_1_), channel_id=1, source_target_pairs={{0,6},{1,7},{2,4},{3,5},{4,2},{5,3},{6,0},{7,1},{8,14},{9,15},{10,... | collective-permute-start | bytes 417800 | tf_op jit(solution)/shard_map/ppermute | solution.py:27
  69.4 6.4 %collective-permute-start.16 = (bf16[2,136,256]{2,1,0:T(8,128)(2,1)}, bf16[2,136,256]{2,1,0:T(8,128)(2,1)S(1)}, u32[]{:S(2)}, u32[]{:S(2)}) collective-permute-start(bf16[2,136,256]{2,1,0:T(8,128)(2,1)} %collective-permute-done.15.refs_7_), channel_id=1, source_target_pairs={{0,2},{1,3},{2,0},{3,1},{4,6},{5,7},{6,4},{7,5},{8,10},{9,11},{10,... | collective-permute-start | bytes 417800 | tf_op jit(solution)/shard_map/ppermute | solution.py:27
  71.6 14.4 %collective-permute-start.4 = (bf16[4,136,256]{2,1,0:T(8,128)(2,1)S(1)}, bf16[4,136,256]{2,1,0:T(8,128)(2,1)S(1)}, u32[]{:S(2)}, u32[]{:S(2)}) collective-permute-start(bf16[4,136,256]{2,1,0:T(8,128)(2,1)S(1)} %collective-permute-done.3.refs_0_), channel_id=1, source_target_pairs={{0,2},{1,3},{2,0},{3,1},{4,6},{5,7},{6,4},{7,5},{8,10},{9,11},{10,... | collective-permute-start | bytes 835592 | tf_op jit(solution)/shard_map/ppermute | solution.py:27
  75.8 11.8 %collective-permute-start.5 = (bf16[4,136,256]{2,1,0:T(8,128)(2,1)S(1)}, bf16[4,136,256]{2,1,0:T(8,128)(2,1)S(1)}, u32[]{:S(2)}, u32[]{:S(2)}) collective-permute-start(bf16[4,136,256]{2,1,0:T(8,128)(2,1)S(1)} %collective-permute-done.3.refs_0_), channel_id=1, source_target_pairs={{0,4},{1,5},{2,6},{3,7},{4,0},{5,1},{6,2},{7,3},{8,12},{9,13},{10,... | collective-permute-start | bytes 835592 | tf_op jit(solution)/shard_map/ppermute | solution.py:27
  79.4 10.2 %collective-permute-start.6 = (bf16[4,136,256]{2,1,0:T(8,128)(2,1)S(1)}, bf16[4,136,256]{2,1,0:T(8,128)(2,1)S(1)}, u32[]{:S(2)}, u32[]{:S(2)}) collective-permute-start(bf16[4,136,256]{2,1,0:T(8,128)(2,1)S(1)} %collective-permute-done.3.refs_0_), channel_id=1, source_target_pairs={{0,6},{1,7},{2,4},{3,5},{4,2},{5,3},{6,0},{7,1},{8,14},{9,15},{10,... | collective-permute-start | bytes 835592 | tf_op jit(solution)/shard_map/ppermute | solution.py:27
  89.5 26.2 %copy-start.2 = (bf16[64,4,256]{2,1,0:T(4,128)(2,1)S(1)}, bf16[64,4,256]{2,1,0:T(4,128)(2,1)}, u32[]{:S(2)}) copy-start(bf16[64,4,256]{2,1,0:T(4,128)(2,1)} %refs_9_.3) | copy-start | bytes 393220
  89.5 26.2 %copy-start.3 = (bf16[64,4,256]{2,1,0:T(4,128)(2,1)S(1)}, bf16[64,4,256]{2,1,0:T(4,128)(2,1)}, u32[]{:S(2)}) copy-start(bf16[64,4,256]{2,1,0:T(4,128)(2,1)} %refs_8_.3) | copy-start | bytes 393220
  89.5 26.2 %copy-start.5 = (bf16[136,256]{1,0:T(8,128)(2,1)S(1)}, bf16[136,256]{1,0:T(8,128)(2,1)}, u32[]{:S(2)}) copy-start(bf16[136,256]{1,0:T(8,128)(2,1)} %copy-done.4) | copy-start | bytes 208900
  89.5 26.2 %copy-start.8 = (f32[64,2,256]{2,1,0:T(2,128)S(1)}, f32[64,2,256]{2,1,0:T(2,128)}, u32[]{:S(2)}) copy-start(f32[64,2,256]{2,1,0:T(2,128)} %refs_3_.1) | copy-start | bytes 393220
  89.5 26.2 %copy-start.9 = (f32[64,2,256]{2,1,0:T(2,128)S(1)}, f32[64,2,256]{2,1,0:T(2,128)}, u32[]{:S(2)}) copy-start(f32[64,2,256]{2,1,0:T(2,128)} %refs_4_.1) | copy-start | bytes 393220
  89.6 26.2 %copy-start.11 = (s32[64,2]{0,1:T(2,128)S(1)}, s32[64,2]{0,1:T(2,128)}, u32[]{:S(2)}) copy-start(s32[64,2]{0,1:T(2,128)} %param.22) | copy-start | bytes 1540
  89.6 26.2 %copy-start.12 = (s32[64]{0:T(128)S(1)}, s32[64]{0:T(128)}, u32[]{:S(2)}) copy-start(s32[64]{0:T(128)} %param.23) | copy-start | bytes 772
  91.7 10.0 %collective-permute-start.17 = (f32[2,136,256]{2,1,0:T(8,128)S(1)}, f32[2,136,256]{2,1,0:T(8,128)S(1)}, u32[]{:S(2)}, u32[]{:S(2)}) collective-permute-start(f32[2,136,256]{2,1,0:T(8,128)S(1)} %get-tuple-element.26), channel_id=1, source_target_pairs={{0,1},{1,0},{2,3},{3,2},{4,5},{5,4},{6,7},{7,6},{8,9},{9,8},{10,11... | collective-permute-start | bytes 835592 | tf_op jit(solution)/shard_map/ppermute | solution.py:27
  101.7 14.1 %collective-permute-start.18 = (bf16[136,256]{1,0:T(8,128)(2,1)S(1)}, bf16[136,256]{1,0:T(8,128)(2,1)S(1)}, u32[]{:S(2)}, u32[]{:S(2)}) collective-permute-start(bf16[136,256]{1,0:T(8,128)(2,1)S(1)} %get-tuple-element.28), channel_id=1, source_target_pairs={{0,256},{1,257},{2,258},{3,259},{4,260},{5,261},{6,262},{7,263},{8... | collective-permute-start | bytes 208904 | tf_op jit(solution)/shard_map/ppermute | solution.py:27
  116.7 0.7 collective-permute-start.19
  117.4 22.8 %collective-permute-start.20 = (bf16[1,136,256]{2,1,0:T(8,128)(2,1)S(1)}, bf16[1,136,256]{2,1,0:T(8,128)(2,1)S(1)}, u32[]{:S(2)}, u32[]{:S(2)}) collective-permute-start(bf16[1,136,256]{2,1,0:T(8,128)(2,1)S(1)} %bitcast.42), channel_id=1, source_target_pairs={{0,32},{1,33},{2,34},{3,35},{4,36},{5,37},{6,38},{7,39},{8,40},{9,... | collective-permute-start | bytes 208904 | tf_op jit(solution)/shard_map/ppermute | solution.py:27
  140.2 7.4 %collective-permute-start.21 = (bf16[2,136,256]{2,1,0:T(8,128)(2,1)S(1)}, bf16[2,136,256]{2,1,0:T(8,128)(2,1)S(1)}, u32[]{:S(2)}, u32[]{:S(2)}) collective-permute-start(bf16[2,136,256]{2,1,0:T(8,128)(2,1)S(1)} %pad_maximum_fusion.4.refs_0_), channel_id=1, source_target_pairs={{0,16},{1,17},{2,18},{3,19},{4,20},{5,21},{6,22},{7,23},{8,24},{9,... | collective-permute-start | bytes 417800 | tf_op jit(solution)/shard_map/ppermute | solution.py:27
  147.7 19.6 %collective-permute-start.22 = (bf16[4,136,256]{2,1,0:T(8,128)(2,1)S(1)}, bf16[4,136,256]{2,1,0:T(8,128)(2,1)S(1)}, u32[]{:S(2)}, u32[]{:S(2)}) collective-permute-start(bf16[4,136,256]{2,1,0:T(8,128)(2,1)S(1)} %pad_maximum_fusion.2), channel_id=1, source_target_pairs={{0,8},{1,9},{2,10},{3,11},{4,12},{5,13},{6,14},{7,15},{8,0},{9,1},... | collective-permute-start | bytes 835592 | tf_op jit(solution)/shard_map/ppermute | solution.py:27
  154.7 8.8 %collective-permute-start.26 = (bf16[2,136,256]{2,1,0:T(8,128)(2,1)S(1)}, bf16[2,136,256]{2,1,0:T(8,128)(2,1)S(1)}, u32[]{:S(2)}, u32[]{:S(2)}) collective-permute-start(bf16[2,136,256]{2,1,0:T(8,128)(2,1)S(1)} %pad_maximum_fusion.4.refs_0_), channel_id=1, source_target_pairs={{0,2},{1,3},{2,0},{3,1},{4,6},{5,7},{6,4},{7,5},{8,10},{9,11},{10,... | collective-permute-start | bytes 417800 | tf_op jit(solution)/shard_map/ppermute | solution.py:27
  157.0 16.1 %collective-permute-start.28 = (bf16[2,136,256]{2,1,0:T(8,128)(2,1)S(1)}, bf16[2,136,256]{2,1,0:T(8,128)(2,1)S(1)}, u32[]{:S(2)}, u32[]{:S(2)}) collective-permute-start(bf16[2,136,256]{2,1,0:T(8,128)(2,1)S(1)} %pad_maximum_fusion.4.refs_0_), channel_id=1, source_target_pairs={{0,6},{1,7},{2,4},{3,5},{4,2},{5,3},{6,0},{7,1},{8,14},{9,15},{10,... | collective-permute-start | bytes 417800 | tf_op jit(solution)/shard_map/ppermute | solution.py:27
  160.8 16.2 %collective-permute-start.30 = (bf16[2,136,256]{2,1,0:T(8,128)(2,1)S(1)}, bf16[2,136,256]{2,1,0:T(8,128)(2,1)S(1)}, u32[]{:S(2)}, u32[]{:S(2)}) collective-permute-start(bf16[2,136,256]{2,1,0:T(8,128)(2,1)S(1)} %collective-permute-done.21.refs_4_), channel_id=1, source_target_pairs={{0,6},{1,7},{2,4},{3,5},{4,2},{5,3},{6,0},{7,1},{8,14},{9,15},{10,... | collective-permute-start | bytes 417800 | tf_op jit(solution)/shard_map/ppermute | solution.py:27
  163.5 15.3 %collective-permute-start.27 = (bf16[2,136,256]{2,1,0:T(8,128)(2,1)S(1)}, bf16[2,136,256]{2,1,0:T(8,128)(2,1)S(1)}, u32[]{:S(2)}, u32[]{:S(2)}) collective-permute-start(bf16[2,136,256]{2,1,0:T(8,128)(2,1)S(1)} %collective-permute-done.26.refs_1_), channel_id=1, source_target_pairs={{0,6},{1,7},{2,4},{3,5},{4,2},{5,3},{6,0},{7,1},{8,14},{9,15},{10,... | collective-permute-start | bytes 417800 | tf_op jit(solution)/shard_map/ppermute | solution.py:27
  167.3 22.5 %collective-permute-start.23 = (bf16[4,136,256]{2,1,0:T(8,128)(2,1)S(1)}, bf16[4,136,256]{2,1,0:T(8,128)(2,1)S(1)}, u32[]{:S(2)}, u32[]{:S(2)}) collective-permute-start(bf16[4,136,256]{2,1,0:T(8,128)(2,1)S(1)} %collective-permute-done.22.refs_0_), channel_id=1, source_target_pairs={{0,2},{1,3},{2,0},{3,1},{4,6},{5,7},{6,4},{7,5},{8,10},{9,11},{10,... | collective-permute-start | bytes 835592 | tf_op jit(solution)/shard_map/ppermute | solution.py:27
  169.2 20.6 %collective-permute-start.24 = (bf16[4,136,256]{2,1,0:T(8,128)(2,1)S(1)}, bf16[4,136,256]{2,1,0:T(8,128)(2,1)S(1)}, u32[]{:S(2)}, u32[]{:S(2)}) collective-permute-start(bf16[4,136,256]{2,1,0:T(8,128)(2,1)S(1)} %collective-permute-done.22.refs_0_), channel_id=1, source_target_pairs={{0,4},{1,5},{2,6},{3,7},{4,0},{5,1},{6,2},{7,3},{8,12},{9,13},{10,... | collective-permute-start | bytes 835592 | tf_op jit(solution)/shard_map/ppermute | solution.py:27
  173.2 16.6 %collective-permute-start.25 = (bf16[4,136,256]{2,1,0:T(8,128)(2,1)S(1)}, bf16[4,136,256]{2,1,0:T(8,128)(2,1)S(1)}, u32[]{:S(2)}, u32[]{:S(2)}) collective-permute-start(bf16[4,136,256]{2,1,0:T(8,128)(2,1)S(1)} %collective-permute-done.22.refs_0_), channel_id=1, source_target_pairs={{0,6},{1,7},{2,4},{3,5},{4,2},{5,3},{6,0},{7,1},{8,14},{9,15},{10,... | collective-permute-start | bytes 835592 | tf_op jit(solution)/shard_map/ppermute | solution.py:27
  176.9 7.9 %collective-permute-start.29 = (bf16[2,136,256]{2,1,0:T(8,128)(2,1)S(1)}, bf16[2,136,256]{2,1,0:T(8,128)(2,1)S(1)}, u32[]{:S(2)}, u32[]{:S(2)}) collective-permute-start(bf16[2,136,256]{2,1,0:T(8,128)(2,1)S(1)} %collective-permute-done.21.refs_4_), channel_id=1, source_target_pairs={{0,2},{1,3},{2,0},{3,1},{4,6},{5,7},{6,4},{7,5},{8,10},{9,11},{10,... | collective-permute-start | bytes 417800 | tf_op jit(solution)/shard_map/ppermute | solution.py:27
  178.9 8.9 %collective-permute-start.31 = (bf16[2,136,256]{2,1,0:T(8,128)(2,1)S(1)}, bf16[2,136,256]{2,1,0:T(8,128)(2,1)S(1)}, u32[]{:S(2)}, u32[]{:S(2)}) collective-permute-start(bf16[2,136,256]{2,1,0:T(8,128)(2,1)S(1)} %collective-permute-done.30.refs_7_), channel_id=1, source_target_pairs={{0,2},{1,3},{2,0},{3,1},{4,6},{5,7},{6,4},{7,5},{8,10},{9,11},{10,... | collective-permute-start | bytes 417800 | tf_op jit(solution)/shard_map/ppermute | solution.py:27
  191.8 5.5 %collective-permute-start.32 = (f32[2,136,256]{2,1,0:T(8,128)S(1)}, f32[2,136,256]{2,1,0:T(8,128)S(1)}, u32[]{:S(2)}, u32[]{:S(2)}) collective-permute-start(f32[2,136,256]{2,1,0:T(8,128)S(1)} %get-tuple-element.34), channel_id=1, source_target_pairs={{0,1},{1,0},{2,3},{3,2},{4,5},{5,4},{6,7},{7,6},{8,9},{9,8},{10,11... | collective-permute-start | bytes 835592 | tf_op jit(solution)/shard_map/ppermute | solution.py:27
  197.4 18.1 %collective-permute-start.33 = (bf16[136,256]{1,0:T(8,128)(2,1)S(1)}, bf16[136,256]{1,0:T(8,128)(2,1)S(1)}, u32[]{:S(2)}, u32[]{:S(2)}) collective-permute-start(bf16[136,256]{1,0:T(8,128)(2,1)S(1)} %get-tuple-element.36), channel_id=1, source_target_pairs={{0,256},{1,257},{2,258},{3,259},{4,260},{5,261},{6,262},{7,263},{8... | collective-permute-start | bytes 208904 | tf_op jit(solution)/shard_map/ppermute | solution.py:27
  (6 other events, 8.3 us)

commit v5 on v3

--- a/solution.py
+++ b/solution.py
@@ -183,29 +183,25 @@
     )(keep, came, packed, v, a, lanes, ids, count, factor_u, factor_v)
 
 
-def mix_kernel(at_ref, *refs, pieces, rows, trials, late):
-    spikes, weights = refs[: 4 * pieces], refs[4 * pieces : 4 * pieces + 4]
+def mix_kernel(at_ref, *refs, pairs, rows, trials, late):
+    spikes, weights = refs[:8], refs[8:12]
     mine_ref, theirs_ref = refs[-2:]
     before = refs[-4:-2]
     flip, shift, y = at_ref[0], at_ref[1], at_ref[2]
     tall, block = spikes[0].shape[1:]
-    depth = spikes[0].shape[0] // 2
     extra = None
     for ref in spikes:
-        for pair in range(depth):
-            tail = ref[2 * pair : 2 * pair + 2, rows:, :].astype(jnp.float32)
-            extra = tail if extra is None else extra + tail
+        tail = ref[:, rows:, :].astype(jnp.float32)
+        extra = tail if extra is None else extra + tail
     part = extra[:, :trials] + extra[:, trials : 2 * trials] + extra[:, 2 * trials : 3 * trials]
 
     def run(there):
         total = None
         for q in range(4):
-            for high in range(2):
-                ref = spikes[q + 4 * high] if pieces == 2 else spikes[q]
-                chunk = ref[...] if pieces == 2 else ref[2 * high : 2 * high + 2]
+            for i, pair in enumerate(pairs):
                 piece = jnp.dot(
-                    chunk.reshape(2 * tall, block),
-                    weights[there ^ (2 * high + int(late))][y ^ q],
+                    spikes[q + 4 * i][...].reshape(2 * tall, block),
+                    weights[there ^ pair][y ^ q],
                     preferred_element_type=jnp.float32,
                 )
                 total = piece if total is None else total + piece
@@ -223,14 +219,14 @@
         pl.when(shift == there)(functools.partial(run, there))
 
 
-def mix(at, spikes, weights, rows, trials, before=()):
+def mix(at, spikes, weights, rows, trials, pairs, before=()):
     _, tall, block = spikes[0].shape
     out = jax.ShapeDtypeStruct((2, tall, block), jnp.float32)
     whole = pl.BlockSpec(memory_space=pltpu.VMEM)
     inputs = len(spikes) * spikes[0].size + 2 * weights[0].size
     return pl.pallas_call(
         functools.partial(
-            mix_kernel, pieces=len(spikes) // 4, rows=rows, trials=trials, late=len(before) > 0
+            mix_kernel, pairs=pairs, rows=rows, trials=trials, late=len(before) > 0
         ),
         out_shape=(out, out),
         in_specs=[pl.BlockSpec(memory_space=pltpu.SMEM)]
@@ -320,17 +316,23 @@
     for step in range(STEPS):
         held = to_owner(packed)[None]
         other = over_a(held)
-        first = [jnp.concatenate([held, other], axis=0)]
-        second = [over_b(first[0], 2)]
-        held = jnp.concatenate([first[0], second[0]], axis=0)
+        pairs = {0: jnp.concatenate([held, other], axis=0)}
+        pairs[2] = over_b(pairs[0], 2)
+        pairs[1] = over_b(pairs[0], 1)
         if step == 0:
-            held, place, lanes = lax.optimization_barrier((held, place, lanes))
-        last = [over_b(held, 1)]
-        for pieces in (first, second, last):
-            for k in (1, 2, 3):
-                pieces.append(over_y(pieces[0], k))
-        halves = mix(place, first + second, weights, rows, trials)
-        mine, theirs = mix(place, last, weights, rows, trials, halves)
+            pairs[2], place, lanes = lax.optimization_barrier((pairs[2], place, lanes))
+        pairs[3] = over_b(pairs[2], 1)
+        spread = {}
+        for j in range(4):
+            near, far = (3, 1) if j >= 2 else (1, 3)
+            came = {0: pairs[j]}
+            for k in (near, far):
+                came[k] = over_y(pairs[j], k)
+            came[2] = over_y(came[near], far)
+            spread[j] = [came[k] for k in range(4)]
+        early, late = spread[0] + spread[1], spread[2] + spread[3]
+        halves = mix(place, early, weights, rows, trials, (0, 1))
+        mine, theirs = mix(place, late, weights, rows, trials, (2, 3), halves)
         theirs = over_c(theirs)
         keep, give = fold(mine, theirs, rows, trials)
         came = over_zh(give)

time: 226 us -> 224 us (level)
  the two profiles are of different devices: /device:TPU:35 before, /device:TPU:18 now
where the time goes in v5:
time: 224 us; the launch traced here: 222 us
  starting transfers between devices  169 us (75%)
  waiting for transfers between devices  37.8 us (17%)
  Pallas kernels  10.7 us (5%)
  local copies, waits for them, and re-layouts  2.32 us (1%)
    ppermute x42, starting transfers between devices, permute(): return lax.ppermute(value, AXES, pairs)  169 us
    ppermute x42, waiting for transfers between devices, permute(): return lax.ppermute(value, AXES, pairs)  37.8 us
    pallas_call x4, Pallas kernels, mix(): pl.pallas_call(functools.partial(mix_kernel, pairs=pairs, rows=rows, tria...  8.55 us
  transfers between devices with their start and end apart: 42, of which 15 were waited for; matrix products, arithmetic and copies ran while one was open for 0% of the time, Pallas kernels for 2%

profile of v5, /device:TPU:18, one launch (start us, length us, event | category | flops | bytes accessed | tf_op | source)
XLA Modules:
  0.0 222.4 jit_solution(12553003338299893527)
XLA Ops:
  2.3 1.9 collective-permute-start.10
  5.8 24.2 %collective-permute-start.1 = (bf16[1,136,256]{2,1,0:T(8,128)(2,1)S(1)}, bf16[1,136,256]{2,1,0:T(8,128)(2,1)S(1)}, u32[]{:S(2)}, u32[]{:S(2)}) collective-permute-start(bf16[1,136,256]{2,1,0:T(8,128)(2,1)S(1)} %bitcast.39), channel_id=1, source_target_pairs={{0,32},{1,33},{2,34},{3,35},{4,36},{5,37},{6,38},{7,39},{8,40},{9,... | collective-permute-start | bytes 208904 | tf_op jit(solution)/shard_map/ppermute | solution.py:27
  30.1 2.4 %collective-permute-start.11 = (bf16[4,256,512]{2,1,0:T(8,128)(2,1)S(1)}, bf16[4,256,512]{2,1,0:T(8,128)(2,1)S(1)}, u32[]{:S(2)}, u32[]{:S(2)}) collective-permute-start(bf16[4,256,512]{2,1,0:T(8,128)(2,1)S(1)} %pad_maximum_fusion.refs_8_), channel_id=1, source_target_pairs={{0,64},{1,65},{2,66},{3,67},{4,68},{5,69},{6,70},{7,71},{8,72},{9,... | collective-permute-start | bytes 3145736 | tf_op jit(solution)/shard_map/ppermute | solution.py:27
  32.6 4.3 %collective-permute-start.12 = (bf16[4,256,512]{2,1,0:T(8,128)(2,1)S(1)}, bf16[4,256,512]{2,1,0:T(8,128)(2,1)S(1)}, u32[]{:S(2)}, u32[]{:S(2)}) collective-permute-start(bf16[4,256,512]{2,1,0:T(8,128)(2,1)S(1)} %pad_maximum_fusion.refs_8_), channel_id=1, source_target_pairs={{0,128},{1,129},{2,130},{3,131},{4,132},{5,133},{6,134},{7,135},{8... | collective-permute-start | bytes 3145736 | tf_op jit(solution)/shard_map/ppermute | solution.py:27
  39.5 2.4 %collective-permute-start.13 = (bf16[4,256,512]{2,1,0:T(8,128)(2,1)S(1)}, bf16[4,256,512]{2,1,0:T(8,128)(2,1)}, u32[]{:S(2)}, u32[]{:S(2)}) collective-permute-start(bf16[4,256,512]{2,1,0:T(8,128)(2,1)S(1)} %pad_maximum_fusion.refs_8_), channel_id=1, source_target_pairs={{0,192},{1,193},{2,194},{3,195},{4,196},{5,197},{6,198},{7,199},{8... | collective-permute-start | bytes 3145736 | tf_op jit(solution)/shard_map/ppermute | solution.py:27
  42.0 3.7 %collective-permute-start.17 = (bf16[2,136,256]{2,1,0:T(8,128)(2,1)}, bf16[2,136,256]{2,1,0:T(8,128)(2,1)}, u32[]{:S(2)}, u32[]{:S(2)}) collective-permute-start(bf16[2,136,256]{2,1,0:T(8,128)(2,1)} %pad_maximum_fusion.1.refs_0_), channel_id=1, source_target_pairs={{0,8},{1,9},{2,10},{3,11},{4,12},{5,13},{6,14},{7,15},{8,0},{9,1},... | collective-permute-start | bytes 417800 | tf_op jit(solution)/shard_map/ppermute | solution.py:27
  47.4 3.2 %collective-permute-start.14 = (bf16[2,136,256]{2,1,0:T(8,128)(2,1)}, bf16[2,136,256]{2,1,0:T(8,128)(2,1)}, u32[]{:S(2)}, u32[]{:S(2)}) collective-permute-start(bf16[2,136,256]{2,1,0:T(8,128)(2,1)} %pad_maximum_fusion.1.refs_0_), channel_id=1, source_target_pairs={{0,2},{1,3},{2,0},{3,1},{4,6},{5,7},{6,4},{7,5},{8,10},{9,11},{10,... | collective-permute-start | bytes 417800 | tf_op jit(solution)/shard_map/ppermute | solution.py:27
  50.6 2.0 collective-permute-start.16
  52.7 2.0 collective-permute-done.14.refs_1_
  54.7 3.2 %collective-permute-start.18 = (bf16[2,136,256]{2,1,0:T(8,128)(2,1)}, bf16[2,136,256]{2,1,0:T(8,128)(2,1)}, u32[]{:S(2)}, u32[]{:S(2)}) collective-permute-start(bf16[2,136,256]{2,1,0:T(8,128)(2,1)} %collective-permute-done.17.refs_4_), channel_id=1, source_target_pairs={{0,2},{1,3},{2,0},{3,1},{4,6},{5,7},{6,4},{7,5},{8,10},{9,11},{10,... | collective-permute-start | bytes 417800 | tf_op jit(solution)/shard_map/ppermute | solution.py:27
  57.9 2.2 collective-permute-start.20
  61.9 2.4 %collective-permute-start.15 = (bf16[2,136,256]{2,1,0:T(8,128)(2,1)}, bf16[2,136,256]{2,1,0:T(8,128)(2,1)}, u32[]{:S(2)}, u32[]{:S(2)}) collective-permute-start(bf16[2,136,256]{2,1,0:T(8,128)(2,1)} %collective-permute-done.14.refs_1_), channel_id=1, source_target_pairs={{0,6},{1,7},{2,4},{3,5},{4,2},{5,3},{6,0},{7,1},{8,14},{9,15},{10,... | collective-permute-start | bytes 417800 | tf_op jit(solution)/shard_map/ppermute | solution.py:27
  65.9 2.5 %collective-permute-start.6 = (bf16[2,136,256]{2,1,0:T(8,128)(2,1)}, bf16[2,136,256]{2,1,0:T(8,128)(2,1)S(1)}, u32[]{:S(2)}, u32[]{:S(2)}) collective-permute-start(bf16[2,136,256]{2,1,0:T(8,128)(2,1)} %collective-permute-done.2.refs_0_), channel_id=1, source_target_pairs={{0,8},{1,9},{2,10},{3,11},{4,12},{5,13},{6,14},{7,15},{8,0},{9,1},... | collective-permute-start | bytes 417800 | tf_op jit(solution)/shard_map/ppermute | solution.py:27
  69.2 2.4 %collective-permute-start.4 = (bf16[2,136,256]{2,1,0:T(8,128)(2,1)}, bf16[2,136,256]{2,1,0:T(8,128)(2,1)S(1)}, u32[]{:S(2)}, u32[]{:S(2)}) collective-permute-start(bf16[2,136,256]{2,1,0:T(8,128)(2,1)} %collective-permute-done.2.refs_0_), channel_id=1, source_target_pairs={{0,6},{1,7},{2,4},{3,5},{4,2},{5,3},{6,0},{7,1},{8,14},{9,15},{10,... | collective-permute-start | bytes 417800 | tf_op jit(solution)/shard_map/ppermute | solution.py:27
  73.1 2.1 collective-permute-start.19
  76.8 3.3 %collective-permute-start.8 = (bf16[2,136,256]{2,1,0:T(8,128)(2,1)S(1)}, bf16[2,136,256]{2,1,0:T(8,128)(2,1)S(1)}, u32[]{:S(2)}, u32[]{:S(2)}) collective-permute-start(bf16[2,136,256]{2,1,0:T(8,128)(2,1)S(1)} %collective-permute-done.6.refs_4_), channel_id=1, source_target_pairs={{0,6},{1,7},{2,4},{3,5},{4,2},{5,3},{6,0},{7,1},{8,14},{9,15},{10,... | collective-permute-start | bytes 417800 | tf_op jit(solution)/shard_map/ppermute | solution.py:27
  80.6 7.1 %collective-permute-start.3 = (bf16[2,136,256]{2,1,0:T(8,128)(2,1)}, bf16[2,136,256]{2,1,0:T(8,128)(2,1)S(1)}, u32[]{:S(2)}, u32[]{:S(2)}) collective-permute-start(bf16[2,136,256]{2,1,0:T(8,128)(2,1)} %collective-permute-done.2.refs_0_), channel_id=1, source_target_pairs={{0,2},{1,3},{2,0},{3,1},{4,6},{5,7},{6,4},{7,5},{8,10},{9,11},{10,... | collective-permute-start | bytes 417800 | tf_op jit(solution)/shard_map/ppermute | solution.py:27
  87.8 4.0 %collective-permute-start.7 = (bf16[2,136,256]{2,1,0:T(8,128)(2,1)S(1)}, bf16[2,136,256]{2,1,0:T(8,128)(2,1)S(1)}, u32[]{:S(2)}, u32[]{:S(2)}) collective-permute-start(bf16[2,136,256]{2,1,0:T(8,128)(2,1)S(1)} %collective-permute-done.6.refs_4_), channel_id=1, source_target_pairs={{0,2},{1,3},{2,0},{3,1},{4,6},{5,7},{6,4},{7,5},{8,10},{9,11},{10,... | collective-permute-start | bytes 417800 | tf_op jit(solution)/shard_map/ppermute | solution.py:27
  91.7 1.9 collective-permute-start.5
  93.7 3.9 %collective-permute-start.9 = (bf16[2,136,256]{2,1,0:T(8,128)(2,1)S(1)}, bf16[2,136,256]{2,1,0:T(8,128)(2,1)S(1)}, u32[]{:S(2)}, u32[]{:S(2)}) collective-permute-start(bf16[2,136,256]{2,1,0:T(8,128)(2,1)S(1)} %collective-permute-done.8.refs_7_), channel_id=1, source_target_pairs={{0,2},{1,3},{2,0},{3,1},{4,6},{5,7},{6,4},{7,5},{8,10},{9,11},{10,... | collective-permute-start | bytes 417800 | tf_op jit(solution)/shard_map/ppermute | solution.py:27
  97.6 2.4 %mix_early.2 = (f32[2,136,256]{2,1,0:T(8,128)S(1)}, f32[2,136,256]{2,1,0:T(8,128)S(1)}) custom-call(s32[3]{0:T(128)S(1)} %pad_add_fusion.at_ref, bf16[2,136,256]{2,1,0:T(8,128)(2,1)} %pad_maximum_fusion.1.refs_0_, bf16[2,136,256]{2,1,0:T(8,128)(2,1)} %collective-permute-done.14.refs_1_, bf16[2,136,256]{2,1,0:T(8,128)(2,1)} %collective-permute-done.15.refs_2_, ...), custom_call_target="tpu_custom_call" | custom-call | flops 570425344 | bytes 3768320 | tf_op jit(solution)/shard_map/mix_early/pallas_call | solution.py:227
  100.7 2.2 mix_late.2
  102.8 1.9 collective-permute-start.21
  106.3 8.4 %collective-permute-start.22 = (bf16[136,256]{1,0:T(8,128)(2,1)S(1)}, bf16[136,256]{1,0:T(8,128)(2,1)S(1)}, u32[]{:S(2)}, u32[]{:S(2)}) collective-permute-start(bf16[136,256]{1,0:T(8,128)(2,1)S(1)} %get-tuple-element.28), channel_id=1, source_target_pairs={{0,256},{1,257},{2,258},{3,259},{4,260},{5,261},{6,262},{7,263},{8... | collective-permute-start | bytes 208904 | tf_op jit(solution)/shard_map/ppermute | solution.py:27
  114.7 6.6 %collective-permute-done.22.refs_1_ = bf16[136,256]{1,0:T(8,128)(2,1)S(1)} collective-permute-done((bf16[136,256]{1,0:T(8,128)(2,1)S(1)}, bf16[136,256]{1,0:T(8,128)(2,1)S(1)}, u32[]{:S(2)}, u32[]{:S(2)}) %collective-permute-start.22) | collective-permute-done | bytes 69664 | tf_op jit(solution)/shard_map/ppermute | solution.py:27
  123.0 18.5 %collective-permute-start.24 = (bf16[1,136,256]{2,1,0:T(8,128)(2,1)S(1)}, bf16[1,136,256]{2,1,0:T(8,128)(2,1)S(1)}, u32[]{:S(2)}, u32[]{:S(2)}) collective-permute-start(bf16[1,136,256]{2,1,0:T(8,128)(2,1)S(1)} %bitcast.41), channel_id=1, source_target_pairs={{0,32},{1,33},{2,34},{3,35},{4,36},{5,37},{6,38},{7,39},{8,40},{9,... | collective-permute-start | bytes 208904 | tf_op jit(solution)/shard_map/ppermute | solution.py:27
  141.4 3.1 %collective-permute-done.24 = bf16[1,136,256]{2,1,0:T(8,128)(2,1)S(1)} collective-permute-done((bf16[1,136,256]{2,1,0:T(8,128)(2,1)S(1)}, bf16[1,136,256]{2,1,0:T(8,128)(2,1)S(1)}, u32[]{:S(2)}, u32[]{:S(2)}) %collective-permute-start.24) | collective-permute-done | bytes 69664 | tf_op jit(solution)/shard_map/ppermute | solution.py:27
  144.5 5.8 %collective-permute-start.25 = (bf16[2,136,256]{2,1,0:T(8,128)(2,1)S(1)}, bf16[2,136,256]{2,1,0:T(8,128)(2,1)S(1)}, u32[]{:S(2)}, u32[]{:S(2)}) collective-permute-start(bf16[2,136,256]{2,1,0:T(8,128)(2,1)S(1)} %pad_maximum_fusion.2.refs_0_), channel_id=1, source_target_pairs={{0,16},{1,17},{2,18},{3,19},{4,20},{5,21},{6,22},{7,23},{8,24},{9,... | collective-permute-start | bytes 417800 | tf_op jit(solution)/shard_map/ppermute | solution.py:27
  150.3 1.9 collective-permute-start.36
  152.2 1.9 collective-permute-start.33
  154.2 2.5 %collective-permute-start.35 = (bf16[2,136,256]{2,1,0:T(8,128)(2,1)S(1)}, bf16[2,136,256]{2,1,0:T(8,128)(2,1)S(1)}, u32[]{:S(2)}, u32[]{:S(2)}) collective-permute-start(bf16[2,136,256]{2,1,0:T(8,128)(2,1)S(1)} %pad_maximum_fusion.2.refs_0_), channel_id=1, source_target_pairs={{0,6},{1,7},{2,4},{3,5},{4,2},{5,3},{6,0},{7,1},{8,14},{9,15},{10,... | collective-permute-start | bytes 417800 | tf_op jit(solution)/shard_map/ppermute | solution.py:27
  156.7 3.4 %collective-permute-start.29 = (bf16[2,136,256]{2,1,0:T(8,128)(2,1)S(1)}, bf16[2,136,256]{2,1,0:T(8,128)(2,1)S(1)}, u32[]{:S(2)}, u32[]{:S(2)}) collective-permute-start(bf16[2,136,256]{2,1,0:T(8,128)(2,1)S(1)} %collective-permute-done.25.refs_0_), channel_id=1, source_target_pairs={{0,8},{1,9},{2,10},{3,11},{4,12},{5,13},{6,14},{7,15},{8,0},{9,1},... | collective-permute-start | bytes 417800 | tf_op jit(solution)/shard_map/ppermute | solution.py:27
  160.0 3.9 %collective-permute-start.37 = (bf16[2,136,256]{2,1,0:T(8,128)(2,1)S(1)}, bf16[2,136,256]{2,1,0:T(8,128)(2,1)S(1)}, u32[]{:S(2)}, u32[]{:S(2)}) collective-permute-start(bf16[2,136,256]{2,1,0:T(8,128)(2,1)S(1)} %collective-permute-done.36.refs_4_), channel_id=1, source_target_pairs={{0,2},{1,3},{2,0},{3,1},{4,6},{5,7},{6,4},{7,5},{8,10},{9,11},{10,... | collective-permute-start | bytes 417800 | tf_op jit(solution)/shard_map/ppermute | solution.py:27
  164.0 4.5 %collective-permute-start.34 = (bf16[2,136,256]{2,1,0:T(8,128)(2,1)S(1)}, bf16[2,136,256]{2,1,0:T(8,128)(2,1)S(1)}, u32[]{:S(2)}, u32[]{:S(2)}) collective-permute-start(bf16[2,136,256]{2,1,0:T(8,128)(2,1)S(1)} %collective-permute-done.33.refs_1_), channel_id=1, source_target_pairs={{0,6},{1,7},{2,4},{3,5},{4,2},{5,3},{6,0},{7,1},{8,14},{9,15},{10,... | collective-permute-start | bytes 417800 | tf_op jit(solution)/shard_map/ppermute | solution.py:27
  168.5 1.9 collective-permute-start.39
  170.5 3.9 %collective-permute-start.27 = (bf16[2,136,256]{2,1,0:T(8,128)(2,1)S(1)}, bf16[2,136,256]{2,1,0:T(8,128)(2,1)S(1)}, u32[]{:S(2)}, u32[]{:S(2)}) collective-permute-start(bf16[2,136,256]{2,1,0:T(8,128)(2,1)S(1)} %collective-permute-done.25.refs_0_), channel_id=1, source_target_pairs={{0,6},{1,7},{2,4},{3,5},{4,2},{5,3},{6,0},{7,1},{8,14},{9,15},{10,... | collective-permute-start | bytes 417800 | tf_op jit(solution)/shard_map/ppermute | solution.py:27
  174.4 1.9 collective-permute-start.31
  176.3 3.9 %collective-permute-start.38 = (bf16[2,136,256]{2,1,0:T(8,128)(2,1)S(1)}, bf16[2,136,256]{2,1,0:T(8,128)(2,1)S(1)}, u32[]{:S(2)}, u32[]{:S(2)}) collective-permute-start(bf16[2,136,256]{2,1,0:T(8,128)(2,1)S(1)} %collective-permute-done.37.refs_5_), channel_id=1, source_target_pairs={{0,6},{1,7},{2,4},{3,5},{4,2},{5,3},{6,0},{7,1},{8,14},{9,15},{10,... | collective-permute-start | bytes 417800 | tf_op jit(solution)/shard_map/ppermute | solution.py:27
  180.3 4.9 %collective-permute-start.26 = (bf16[2,136,256]{2,1,0:T(8,128)(2,1)S(1)}, bf16[2,136,256]{2,1,0:T(8,128)(2,1)S(1)}, u32[]{:S(2)}, u32[]{:S(2)}) collective-permute-start(bf16[2,136,256]{2,1,0:T(8,128)(2,1)S(1)} %collective-permute-done.25.refs_0_), channel_id=1, source_target_pairs={{0,2},{1,3},{2,0},{3,1},{4,6},{5,7},{6,4},{7,5},{8,10},{9,11},{10,... | collective-permute-start | bytes 417800 | tf_op jit(solution)/shard_map/ppermute | solution.py:27
  185.2 1.9 collective-permute-start.30
  187.2 3.9 %collective-permute-start.28 = (bf16[2,136,256]{2,1,0:T(8,128)(2,1)S(1)}, bf16[2,136,256]{2,1,0:T(8,128)(2,1)S(1)}, u32[]{:S(2)}, u32[]{:S(2)}) collective-permute-start(bf16[2,136,256]{2,1,0:T(8,128)(2,1)S(1)} %collective-permute-done.27.refs_3_), channel_id=1, source_target_pairs={{0,2},{1,3},{2,0},{3,1},{4,6},{5,7},{6,4},{7,5},{8,10},{9,11},{10,... | collective-permute-start | bytes 417800 | tf_op jit(solution)/shard_map/ppermute | solution.py:27
  191.1 1.9 collective-permute-start.32
  193.1 2.0 mix_early.3
  195.1 3.0 %collective-permute-done.32.refs_6_ = bf16[2,136,256]{2,1,0:T(8,128)(2,1)S(1)} collective-permute-done((bf16[2,136,256]{2,1,0:T(8,128)(2,1)S(1)}, bf16[2,136,256]{2,1,0:T(8,128)(2,1)S(1)}, u32[]{:S(2)}, u32[]{:S(2)}) %collective-permute-start.32) | collective-permute-done | bytes 139296 | tf_op jit(solution)/shard_map/ppermute | solution.py:27
  198.1 2.0 mix_late.3
  200.1 1.9 collective-permute-start.40
  203.6 7.6 %collective-permute-start.41 = (bf16[136,256]{1,0:T(8,128)(2,1)S(1)}, bf16[136,256]{1,0:T(8,128)(2,1)S(1)}, u32[]{:S(2)}, u32[]{:S(2)}) collective-permute-start(bf16[136,256]{1,0:T(8,128)(2,1)S(1)} %get-tuple-element.36), channel_id=1, source_target_pairs={{0,256},{1,257},{2,258},{3,259},{4,260},{5,261},{6,262},{7,263},{8... | collective-permute-start | bytes 208904 | tf_op jit(solution)/shard_map/ppermute | solution.py:27
  211.2 10.3 %collective-permute-done.41.refs_1_ = bf16[136,256]{1,0:T(8,128)(2,1)S(1)} collective-permute-done((bf16[136,256]{1,0:T(8,128)(2,1)S(1)}, bf16[136,256]{1,0:T(8,128)(2,1)S(1)}, u32[]{:S(2)}, u32[]{:S(2)}) %collective-permute-start.41) | collective-permute-done | bytes 69664 | tf_op jit(solution)/shard_map/ppermute | solution.py:27
  (87 shorter events, 21.5 us)
Async XLA Ops:
  0.6 63.6 %copy-start = (bf16[700,256]{1,0:T(8,128)(2,1)S(1)}, bf16[700,256]{1,0:T(8,128)(2,1)}, u32[]{:S(2)}) copy-start(bf16[700,256]{1,0:T(8,128)(2,1)} %param.20) | copy-start | bytes 1075204
  2.3 27.7 %collective-permute-start.10 = (bf16[4,256,256]{2,1,0:T(8,128)(2,1)S(1)}, bf16[4,256,256]{2,1,0:T(8,128)(2,1)S(1)}, u32[]{:S(2)}, u32[]{:S(2)}) collective-permute-start(bf16[4,256,256]{2,1,0:T(8,128)(2,1)S(1)} %get-tuple-element.41), channel_id=1, source_target_pairs={{0,1},{1,0},{2,3},{3,2},{4,5},{5,4},{6,7},{7,6},{8,9},{9,8},{10,11... | collective-permute-start | bytes 1572872 | tf_op jit(solution)/shard_map/ppermute | solution.py:27
  4.5 1.3 collective-permute-start
  5.8 31.1 %collective-permute-start.1 = (bf16[1,136,256]{2,1,0:T(8,128)(2,1)S(1)}, bf16[1,136,256]{2,1,0:T(8,128)(2,1)S(1)}, u32[]{:S(2)}, u32[]{:S(2)}) collective-permute-start(bf16[1,136,256]{2,1,0:T(8,128)(2,1)S(1)} %bitcast.39), channel_id=1, source_target_pairs={{0,32},{1,33},{2,34},{3,35},{4,36},{5,37},{6,38},{7,39},{8,40},{9,... | collective-permute-start | bytes 208904 | tf_op jit(solution)/shard_map/ppermute | solution.py:27
  30.0 27.9 %copy-start.11 = (s32[2,2,700]{2,1,0:T(2,128)S(1)}, s32[2,2,700]{2,1,0:T(2,128)}, u32[]{:S(2)}) copy-start(s32[2,2,700]{2,1,0:T(2,128)} %param.21) | copy-start | bytes 33604
  30.0 34.4 %copy-start.12 = (f32[256]{0:T(256)S(1)}, f32[256]{0:T(256)}, u32[]{:S(2)}) copy-start(f32[256]{0:T(256)} %param.24) | copy-start | bytes 3076
  30.0 34.4 %copy-start.13 = (f32[256]{0:T(256)S(1)}, f32[256]{0:T(256)}, u32[]{:S(2)}) copy-start(f32[256]{0:T(256)} %param.25) | copy-start | bytes 3076
  30.0 34.4 %copy-start.14 = (f32[256]{0:T(256)S(1)}, f32[256]{0:T(256)}, u32[]{:S(2)}) copy-start(f32[256]{0:T(256)} %param.26) | copy-start | bytes 3076
  30.0 34.4 %copy-start.15 = (f32[256]{0:T(256)S(1)}, f32[256]{0:T(256)}, u32[]{:S(2)}) copy-start(f32[256]{0:T(256)} %param.27) | copy-start | bytes 3076
  30.1 61.6 %collective-permute-start.11 = (bf16[4,256,512]{2,1,0:T(8,128)(2,1)S(1)}, bf16[4,256,512]{2,1,0:T(8,128)(2,1)S(1)}, u32[]{:S(2)}, u32[]{:S(2)}) collective-permute-start(bf16[4,256,512]{2,1,0:T(8,128)(2,1)S(1)} %pad_maximum_fusion.refs_8_), channel_id=1, source_target_pairs={{0,64},{1,65},{2,66},{3,67},{4,68},{5,69},{6,70},{7,71},{8,72},{9,... | collective-permute-start | bytes 3145736 | tf_op jit(solution)/shard_map/ppermute | solution.py:27
  32.6 61.1 %collective-permute-start.12 = (bf16[4,256,512]{2,1,0:T(8,128)(2,1)S(1)}, bf16[4,256,512]{2,1,0:T(8,128)(2,1)S(1)}, u32[]{:S(2)}, u32[]{:S(2)}) collective-permute-start(bf16[4,256,512]{2,1,0:T(8,128)(2,1)S(1)} %pad_maximum_fusion.refs_8_), channel_id=1, source_target_pairs={{0,128},{1,129},{2,130},{3,131},{4,132},{5,133},{6,134},{7,135},{8... | collective-permute-start | bytes 3145736 | tf_op jit(solution)/shard_map/ppermute | solution.py:27
  37.6 9.8 %collective-permute-start.2 = (bf16[2,136,256]{2,1,0:T(8,128)(2,1)}, bf16[2,136,256]{2,1,0:T(8,128)(2,1)}, u32[]{:S(2)}, u32[]{:S(2)}) collective-permute-start(bf16[2,136,256]{2,1,0:T(8,128)(2,1)} %pad_maximum_fusion.1.refs_0_), channel_id=1, source_target_pairs={{0,16},{1,17},{2,18},{3,19},{4,20},{5,21},{6,22},{7,23},{8,24},{9,... | collective-permute-start | bytes 417800 | tf_op jit(solution)/shard_map/ppermute | solution.py:27
  39.5 58.1 %collective-permute-start.13 = (bf16[4,256,512]{2,1,0:T(8,128)(2,1)S(1)}, bf16[4,256,512]{2,1,0:T(8,128)(2,1)}, u32[]{:S(2)}, u32[]{:S(2)}) collective-permute-start(bf16[4,256,512]{2,1,0:T(8,128)(2,1)S(1)} %pad_maximum_fusion.refs_8_), channel_id=1, source_target_pairs={{0,192},{1,193},{2,194},{3,195},{4,196},{5,197},{6,198},{7,199},{8... | collective-permute-start | bytes 3145736 | tf_op jit(solution)/shard_map/ppermute | solution.py:27
  42.0 8.6 %collective-permute-start.17 = (bf16[2,136,256]{2,1,0:T(8,128)(2,1)}, bf16[2,136,256]{2,1,0:T(8,128)(2,1)}, u32[]{:S(2)}, u32[]{:S(2)}) collective-permute-start(bf16[2,136,256]{2,1,0:T(8,128)(2,1)} %pad_maximum_fusion.1.refs_0_), channel_id=1, source_target_pairs={{0,8},{1,9},{2,10},{3,11},{4,12},{5,13},{6,14},{7,15},{8,0},{9,1},... | collective-permute-start | bytes 417800 | tf_op jit(solution)/shard_map/ppermute | solution.py:27
  47.4 7.3 %collective-permute-start.14 = (bf16[2,136,256]{2,1,0:T(8,128)(2,1)}, bf16[2,136,256]{2,1,0:T(8,128)(2,1)}, u32[]{:S(2)}, u32[]{:S(2)}) collective-permute-start(bf16[2,136,256]{2,1,0:T(8,128)(2,1)} %pad_maximum_fusion.1.refs_0_), channel_id=1, source_target_pairs={{0,2},{1,3},{2,0},{3,1},{4,6},{5,7},{6,4},{7,5},{8,10},{9,11},{10,... | collective-permute-start | bytes 417800 | tf_op jit(solution)/shard_map/ppermute | solution.py:27
  50.6 7.3 %collective-permute-start.16 = (bf16[2,136,256]{2,1,0:T(8,128)(2,1)}, bf16[2,136,256]{2,1,0:T(8,128)(2,1)}, u32[]{:S(2)}, u32[]{:S(2)}) collective-permute-start(bf16[2,136,256]{2,1,0:T(8,128)(2,1)} %pad_maximum_fusion.1.refs_0_), channel_id=1, source_target_pairs={{0,6},{1,7},{2,4},{3,5},{4,2},{5,3},{6,0},{7,1},{8,14},{9,15},{10,... | collective-permute-start | bytes 417800 | tf_op jit(solution)/shard_map/ppermute | solution.py:27
  54.7 7.3 %collective-permute-start.18 = (bf16[2,136,256]{2,1,0:T(8,128)(2,1)}, bf16[2,136,256]{2,1,0:T(8,128)(2,1)}, u32[]{:S(2)}, u32[]{:S(2)}) collective-permute-start(bf16[2,136,256]{2,1,0:T(8,128)(2,1)} %collective-permute-done.17.refs_4_), channel_id=1, source_target_pairs={{0,2},{1,3},{2,0},{3,1},{4,6},{5,7},{6,4},{7,5},{8,10},{9,11},{10,... | collective-permute-start | bytes 417800 | tf_op jit(solution)/shard_map/ppermute | solution.py:27
  57.9 8.0 %collective-permute-start.20 = (bf16[2,136,256]{2,1,0:T(8,128)(2,1)}, bf16[2,136,256]{2,1,0:T(8,128)(2,1)}, u32[]{:S(2)}, u32[]{:S(2)}) collective-permute-start(bf16[2,136,256]{2,1,0:T(8,128)(2,1)} %collective-permute-done.17.refs_4_), channel_id=1, source_target_pairs={{0,6},{1,7},{2,4},{3,5},{4,2},{5,3},{6,0},{7,1},{8,14},{9,15},{10,... | collective-permute-start | bytes 417800 | tf_op jit(solution)/shard_map/ppermute | solution.py:27
  61.9 7.3 %collective-permute-start.15 = (bf16[2,136,256]{2,1,0:T(8,128)(2,1)}, bf16[2,136,256]{2,1,0:T(8,128)(2,1)}, u32[]{:S(2)}, u32[]{:S(2)}) collective-permute-start(bf16[2,136,256]{2,1,0:T(8,128)(2,1)} %collective-permute-done.14.refs_1_), channel_id=1, source_target_pairs={{0,6},{1,7},{2,4},{3,5},{4,2},{5,3},{6,0},{7,1},{8,14},{9,15},{10,... | collective-permute-start | bytes 417800 | tf_op jit(solution)/shard_map/ppermute | solution.py:27
  65.9 7.1 %collective-permute-start.6 = (bf16[2,136,256]{2,1,0:T(8,128)(2,1)}, bf16[2,136,256]{2,1,0:T(8,128)(2,1)S(1)}, u32[]{:S(2)}, u32[]{:S(2)}) collective-permute-start(bf16[2,136,256]{2,1,0:T(8,128)(2,1)} %collective-permute-done.2.refs_0_), channel_id=1, source_target_pairs={{0,8},{1,9},{2,10},{3,11},{4,12},{5,13},{6,14},{7,15},{8,0},{9,1},... | collective-permute-start | bytes 417800 | tf_op jit(solution)/shard_map/ppermute | solution.py:27
  69.2 7.6 %collective-permute-start.4 = (bf16[2,136,256]{2,1,0:T(8,128)(2,1)}, bf16[2,136,256]{2,1,0:T(8,128)(2,1)S(1)}, u32[]{:S(2)}, u32[]{:S(2)}) collective-permute-start(bf16[2,136,256]{2,1,0:T(8,128)(2,1)} %collective-permute-done.2.refs_0_), channel_id=1, source_target_pairs={{0,6},{1,7},{2,4},{3,5},{4,2},{5,3},{6,0},{7,1},{8,14},{9,15},{10,... | collective-permute-start | bytes 417800 | tf_op jit(solution)/shard_map/ppermute | solution.py:27
  73.1 7.6 %collective-permute-start.19 = (bf16[2,136,256]{2,1,0:T(8,128)(2,1)}, bf16[2,136,256]{2,1,0:T(8,128)(2,1)S(1)}, u32[]{:S(2)}, u32[]{:S(2)}) collective-permute-start(bf16[2,136,256]{2,1,0:T(8,128)(2,1)} %collective-permute-done.18.refs_5_), channel_id=1, source_target_pairs={{0,6},{1,7},{2,4},{3,5},{4,2},{5,3},{6,0},{7,1},{8,14},{9,15},{10,... | collective-permute-start | bytes 417800 | tf_op jit(solution)/shard_map/ppermute | solution.py:27
  76.8 10.9 %collective-permute-start.8 = (bf16[2,136,256]{2,1,0:T(8,128)(2,1)S(1)}, bf16[2,136,256]{2,1,0:T(8,128)(2,1)S(1)}, u32[]{:S(2)}, u32[]{:S(2)}) collective-permute-start(bf16[2,136,256]{2,1,0:T(8,128)(2,1)S(1)} %collective-permute-done.6.refs_4_), channel_id=1, source_target_pairs={{0,6},{1,7},{2,4},{3,5},{4,2},{5,3},{6,0},{7,1},{8,14},{9,15},{10,... | collective-permute-start | bytes 417800 | tf_op jit(solution)/shard_map/ppermute | solution.py:27
  80.6 19.4 %collective-permute-start.3 = (bf16[2,136,256]{2,1,0:T(8,128)(2,1)}, bf16[2,136,256]{2,1,0:T(8,128)(2,1)S(1)}, u32[]{:S(2)}, u32[]{:S(2)}) collective-permute-start(bf16[2,136,256]{2,1,0:T(8,128)(2,1)} %collective-permute-done.2.refs_0_), channel_id=1, source_target_pairs={{0,2},{1,3},{2,0},{3,1},{4,6},{5,7},{6,4},{7,5},{8,10},{9,11},{10,... | collective-permute-start | bytes 417800 | tf_op jit(solution)/shard_map/ppermute | solution.py:27
  87.8 12.3 %collective-permute-start.7 = (bf16[2,136,256]{2,1,0:T(8,128)(2,1)S(1)}, bf16[2,136,256]{2,1,0:T(8,128)(2,1)S(1)}, u32[]{:S(2)}, u32[]{:S(2)}) collective-permute-start(bf16[2,136,256]{2,1,0:T(8,128)(2,1)S(1)} %collective-permute-done.6.refs_4_), channel_id=1, source_target_pairs={{0,2},{1,3},{2,0},{3,1},{4,6},{5,7},{6,4},{7,5},{8,10},{9,11},{10,... | collective-permute-start | bytes 417800 | tf_op jit(solution)/shard_map/ppermute | solution.py:27
  91.7 8.3 %collective-permute-start.5 = (bf16[2,136,256]{2,1,0:T(8,128)(2,1)S(1)}, bf16[2,136,256]{2,1,0:T(8,128)(2,1)S(1)}, u32[]{:S(2)}, u32[]{:S(2)}) collective-permute-start(bf16[2,136,256]{2,1,0:T(8,128)(2,1)S(1)} %collective-permute-done.4.refs_3_), channel_id=1, source_target_pairs={{0,2},{1,3},{2,0},{3,1},{4,6},{5,7},{6,4},{7,5},{8,10},{9,11},{10,... | collective-permute-start | bytes 417800 | tf_op jit(solution)/shard_map/ppermute | solution.py:27
  93.7 6.9 %collective-permute-start.9 = (bf16[2,136,256]{2,1,0:T(8,128)(2,1)S(1)}, bf16[2,136,256]{2,1,0:T(8,128)(2,1)S(1)}, u32[]{:S(2)}, u32[]{:S(2)}) collective-permute-start(bf16[2,136,256]{2,1,0:T(8,128)(2,1)S(1)} %collective-permute-done.8.refs_7_), channel_id=1, source_target_pairs={{0,2},{1,3},{2,0},{3,1},{4,6},{5,7},{6,4},{7,5},{8,10},{9,11},{10,... | collective-permute-start | bytes 417800 | tf_op jit(solution)/shard_map/ppermute | solution.py:27
  102.8 3.5 %collective-permute-start.21 = (f32[2,136,256]{2,1,0:T(8,128)S(1)}, f32[2,136,256]{2,1,0:T(8,128)S(1)}, u32[]{:S(2)}, u32[]{:S(2)}) collective-permute-start(f32[2,136,256]{2,1,0:T(8,128)S(1)} %get-tuple-element.26), channel_id=1, source_target_pairs={{0,1},{1,0},{2,3},{3,2},{4,5},{5,4},{6,7},{7,6},{8,9},{9,8},{10,11... | collective-permute-start | bytes 835592 | tf_op jit(solution)/shard_map/ppermute | solution.py:27
  106.3 15.0 %collective-permute-start.22 = (bf16[136,256]{1,0:T(8,128)(2,1)S(1)}, bf16[136,256]{1,0:T(8,128)(2,1)S(1)}, u32[]{:S(2)}, u32[]{:S(2)}) collective-permute-start(bf16[136,256]{1,0:T(8,128)(2,1)S(1)} %get-tuple-element.28), channel_id=1, source_target_pairs={{0,256},{1,257},{2,258},{3,259},{4,260},{5,261},{6,262},{7,263},{8... | collective-permute-start | bytes 208904 | tf_op jit(solution)/shard_map/ppermute | solution.py:27
  122.3 0.7 collective-permute-start.23
  123.0 21.6 %collective-permute-start.24 = (bf16[1,136,256]{2,1,0:T(8,128)(2,1)S(1)}, bf16[1,136,256]{2,1,0:T(8,128)(2,1)S(1)}, u32[]{:S(2)}, u32[]{:S(2)}) collective-permute-start(bf16[1,136,256]{2,1,0:T(8,128)(2,1)S(1)} %bitcast.41), channel_id=1, source_target_pairs={{0,32},{1,33},{2,34},{3,35},{4,36},{5,37},{6,38},{7,39},{8,40},{9,... | collective-permute-start | bytes 208904 | tf_op jit(solution)/shard_map/ppermute | solution.py:27
  144.5 12.1 %collective-permute-start.25 = (bf16[2,136,256]{2,1,0:T(8,128)(2,1)S(1)}, bf16[2,136,256]{2,1,0:T(8,128)(2,1)S(1)}, u32[]{:S(2)}, u32[]{:S(2)}) collective-permute-start(bf16[2,136,256]{2,1,0:T(8,128)(2,1)S(1)} %pad_maximum_fusion.2.refs_0_), channel_id=1, source_target_pairs={{0,16},{1,17},{2,18},{3,19},{4,20},{5,21},{6,22},{7,23},{8,24},{9,... | collective-permute-start | bytes 417800 | tf_op jit(solution)/shard_map/ppermute | solution.py:27
  150.3 9.7 %collective-permute-start.36 = (bf16[2,136,256]{2,1,0:T(8,128)(2,1)S(1)}, bf16[2,136,256]{2,1,0:T(8,128)(2,1)S(1)}, u32[]{:S(2)}, u32[]{:S(2)}) collective-permute-start(bf16[2,136,256]{2,1,0:T(8,128)(2,1)S(1)} %pad_maximum_fusion.2.refs_0_), channel_id=1, source_target_pairs={{0,8},{1,9},{2,10},{3,11},{4,12},{5,13},{6,14},{7,15},{8,0},{9,1},... | collective-permute-start | bytes 417800 | tf_op jit(solution)/shard_map/ppermute | solution.py:27
  152.2 11.7 %collective-permute-start.33 = (bf16[2,136,256]{2,1,0:T(8,128)(2,1)S(1)}, bf16[2,136,256]{2,1,0:T(8,128)(2,1)S(1)}, u32[]{:S(2)}, u32[]{:S(2)}) collective-permute-start(bf16[2,136,256]{2,1,0:T(8,128)(2,1)S(1)} %pad_maximum_fusion.2.refs_0_), channel_id=1, source_target_pairs={{0,2},{1,3},{2,0},{3,1},{4,6},{5,7},{6,4},{7,5},{8,10},{9,11},{10,... | collective-permute-start | bytes 417800 | tf_op jit(solution)/shard_map/ppermute | solution.py:27
  154.2 16.3 %collective-permute-start.35 = (bf16[2,136,256]{2,1,0:T(8,128)(2,1)S(1)}, bf16[2,136,256]{2,1,0:T(8,128)(2,1)S(1)}, u32[]{:S(2)}, u32[]{:S(2)}) collective-permute-start(bf16[2,136,256]{2,1,0:T(8,128)(2,1)S(1)} %pad_maximum_fusion.2.refs_0_), channel_id=1, source_target_pairs={{0,6},{1,7},{2,4},{3,5},{4,2},{5,3},{6,0},{7,1},{8,14},{9,15},{10,... | collective-permute-start | bytes 417800 | tf_op jit(solution)/shard_map/ppermute | solution.py:27
  156.7 17.7 %collective-permute-start.29 = (bf16[2,136,256]{2,1,0:T(8,128)(2,1)S(1)}, bf16[2,136,256]{2,1,0:T(8,128)(2,1)S(1)}, u32[]{:S(2)}, u32[]{:S(2)}) collective-permute-start(bf16[2,136,256]{2,1,0:T(8,128)(2,1)S(1)} %collective-permute-done.25.refs_0_), channel_id=1, source_target_pairs={{0,8},{1,9},{2,10},{3,11},{4,12},{5,13},{6,14},{7,15},{8,0},{9,1},... | collective-permute-start | bytes 417800 | tf_op jit(solution)/shard_map/ppermute | solution.py:27
  160.0 16.3 %collective-permute-start.37 = (bf16[2,136,256]{2,1,0:T(8,128)(2,1)S(1)}, bf16[2,136,256]{2,1,0:T(8,128)(2,1)S(1)}, u32[]{:S(2)}, u32[]{:S(2)}) collective-permute-start(bf16[2,136,256]{2,1,0:T(8,128)(2,1)S(1)} %collective-permute-done.36.refs_4_), channel_id=1, source_target_pairs={{0,2},{1,3},{2,0},{3,1},{4,6},{5,7},{6,4},{7,5},{8,10},{9,11},{10,... | collective-permute-start | bytes 417800 | tf_op jit(solution)/shard_map/ppermute | solution.py:27
  164.0 16.3 %collective-permute-start.34 = (bf16[2,136,256]{2,1,0:T(8,128)(2,1)S(1)}, bf16[2,136,256]{2,1,0:T(8,128)(2,1)S(1)}, u32[]{:S(2)}, u32[]{:S(2)}) collective-permute-start(bf16[2,136,256]{2,1,0:T(8,128)(2,1)S(1)} %collective-permute-done.33.refs_1_), channel_id=1, source_target_pairs={{0,6},{1,7},{2,4},{3,5},{4,2},{5,3},{6,0},{7,1},{8,14},{9,15},{10,... | collective-permute-start | bytes 417800 | tf_op jit(solution)/shard_map/ppermute | solution.py:27
  168.5 16.7 %collective-permute-start.39 = (bf16[2,136,256]{2,1,0:T(8,128)(2,1)S(1)}, bf16[2,136,256]{2,1,0:T(8,128)(2,1)S(1)}, u32[]{:S(2)}, u32[]{:S(2)}) collective-permute-start(bf16[2,136,256]{2,1,0:T(8,128)(2,1)S(1)} %collective-permute-done.36.refs_4_), channel_id=1, source_target_pairs={{0,6},{1,7},{2,4},{3,5},{4,2},{5,3},{6,0},{7,1},{8,14},{9,15},{10,... | collective-permute-start | bytes 417800 | tf_op jit(solution)/shard_map/ppermute | solution.py:27
  170.5 16.7 %collective-permute-start.27 = (bf16[2,136,256]{2,1,0:T(8,128)(2,1)S(1)}, bf16[2,136,256]{2,1,0:T(8,128)(2,1)S(1)}, u32[]{:S(2)}, u32[]{:S(2)}) collective-permute-start(bf16[2,136,256]{2,1,0:T(8,128)(2,1)S(1)} %collective-permute-done.25.refs_0_), channel_id=1, source_target_pairs={{0,6},{1,7},{2,4},{3,5},{4,2},{5,3},{6,0},{7,1},{8,14},{9,15},{10,... | collective-permute-start | bytes 417800 | tf_op jit(solution)/shard_map/ppermute | solution.py:27
  174.4 16.7 %collective-permute-start.31 = (bf16[2,136,256]{2,1,0:T(8,128)(2,1)S(1)}, bf16[2,136,256]{2,1,0:T(8,128)(2,1)S(1)}, u32[]{:S(2)}, u32[]{:S(2)}) collective-permute-start(bf16[2,136,256]{2,1,0:T(8,128)(2,1)S(1)} %collective-permute-done.29.refs_4_), channel_id=1, source_target_pairs={{0,6},{1,7},{2,4},{3,5},{4,2},{5,3},{6,0},{7,1},{8,14},{9,15},{10,... | collective-permute-start | bytes 417800 | tf_op jit(solution)/shard_map/ppermute | solution.py:27
  176.3 16.7 %collective-permute-start.38 = (bf16[2,136,256]{2,1,0:T(8,128)(2,1)S(1)}, bf16[2,136,256]{2,1,0:T(8,128)(2,1)S(1)}, u32[]{:S(2)}, u32[]{:S(2)}) collective-permute-start(bf16[2,136,256]{2,1,0:T(8,128)(2,1)S(1)} %collective-permute-done.37.refs_5_), channel_id=1, source_target_pairs={{0,6},{1,7},{2,4},{3,5},{4,2},{5,3},{6,0},{7,1},{8,14},{9,15},{10,... | collective-permute-start | bytes 417800 | tf_op jit(solution)/shard_map/ppermute | solution.py:27
  180.3 14.8 %collective-permute-start.26 = (bf16[2,136,256]{2,1,0:T(8,128)(2,1)S(1)}, bf16[2,136,256]{2,1,0:T(8,128)(2,1)S(1)}, u32[]{:S(2)}, u32[]{:S(2)}) collective-permute-start(bf16[2,136,256]{2,1,0:T(8,128)(2,1)S(1)} %collective-permute-done.25.refs_0_), channel_id=1, source_target_pairs={{0,2},{1,3},{2,0},{3,1},{4,6},{5,7},{6,4},{7,5},{8,10},{9,11},{10,... | collective-permute-start | bytes 417800 | tf_op jit(solution)/shard_map/ppermute | solution.py:27
  185.2 9.8 %collective-permute-start.30 = (bf16[2,136,256]{2,1,0:T(8,128)(2,1)S(1)}, bf16[2,136,256]{2,1,0:T(8,128)(2,1)S(1)}, u32[]{:S(2)}, u32[]{:S(2)}) collective-permute-start(bf16[2,136,256]{2,1,0:T(8,128)(2,1)S(1)} %collective-permute-done.29.refs_4_), channel_id=1, source_target_pairs={{0,2},{1,3},{2,0},{3,1},{4,6},{5,7},{6,4},{7,5},{8,10},{9,11},{10,... | collective-permute-start | bytes 417800 | tf_op jit(solution)/shard_map/ppermute | solution.py:27
  187.2 7.9 %collective-permute-start.28 = (bf16[2,136,256]{2,1,0:T(8,128)(2,1)S(1)}, bf16[2,136,256]{2,1,0:T(8,128)(2,1)S(1)}, u32[]{:S(2)}, u32[]{:S(2)}) collective-permute-start(bf16[2,136,256]{2,1,0:T(8,128)(2,1)S(1)} %collective-permute-done.27.refs_3_), channel_id=1, source_target_pairs={{0,2},{1,3},{2,0},{3,1},{4,6},{5,7},{6,4},{7,5},{8,10},{9,11},{10,... | collective-permute-start | bytes 417800 | tf_op jit(solution)/shard_map/ppermute | solution.py:27
  191.1 6.9 %collective-permute-start.32 = (bf16[2,136,256]{2,1,0:T(8,128)(2,1)S(1)}, bf16[2,136,256]{2,1,0:T(8,128)(2,1)S(1)}, u32[]{:S(2)}, u32[]{:S(2)}) collective-permute-start(bf16[2,136,256]{2,1,0:T(8,128)(2,1)S(1)} %collective-permute-done.31.refs_7_), channel_id=1, source_target_pairs={{0,2},{1,3},{2,0},{3,1},{4,6},{5,7},{6,4},{7,5},{8,10},{9,11},{10,... | collective-permute-start | bytes 417800 | tf_op jit(solution)/shard_map/ppermute | solution.py:27
  200.1 3.5 %collective-permute-start.40 = (f32[2,136,256]{2,1,0:T(8,128)S(1)}, f32[2,136,256]{2,1,0:T(8,128)S(1)}, u32[]{:S(2)}, u32[]{:S(2)}) collective-permute-start(f32[2,136,256]{2,1,0:T(8,128)S(1)} %get-tuple-element.34), channel_id=1, source_target_pairs={{0,1},{1,0},{2,3},{3,2},{4,5},{5,4},{6,7},{7,6},{8,9},{9,8},{10,11... | collective-permute-start | bytes 835592 | tf_op jit(solution)/shard_map/ppermute | solution.py:27
  203.6 18.0 %collective-permute-start.41 = (bf16[136,256]{1,0:T(8,128)(2,1)S(1)}, bf16[136,256]{1,0:T(8,128)(2,1)S(1)}, u32[]{:S(2)}, u32[]{:S(2)}) collective-permute-start(bf16[136,256]{1,0:T(8,128)(2,1)S(1)} %get-tuple-element.36), channel_id=1, source_target_pairs={{0,256},{1,257},{2,258},{3,259},{4,260},{5,261},{6,262},{7,263},{8... | collective-permute-start | bytes 208904 | tf_op jit(solution)/shard_map/ppermute | solution.py:27
  (10 other events, 149.4 us)

commit v6 on v3

--- a/solution.py
+++ b/solution.py
@@ -326,10 +326,14 @@
         if step == 0:
             held, place, lanes = lax.optimization_barrier((held, place, lanes))
         last = [over_b(held, 1)]
-        for pieces in (first, second, last):
-            for k in (1, 2, 3):
-                pieces.append(over_y(pieces[0], k))
-        halves = mix(place, first + second, weights, rows, trials)
+        early, came = [held], {}
+        for k in (3, 1):
+            came[k] = over_y(held, k)
+        came[2] = over_y(came[3], 1)
+        early += [came[k] for k in (1, 2, 3)]
+        for k in (1, 2, 3):
+            last.append(over_y(last[0], k))
+        halves = mix(place, early, weights, rows, trials)
         mine, theirs = mix(place, last, weights, rows, trials, halves)
         theirs = over_c(theirs)
         keep, give = fold(mine, theirs, rows, trials)

time: 226 us -> 205 us (0.907)
  the two profiles are of different devices: /device:TPU:35 before, /device:TPU:69 now
where the time goes in v6:
time: 205 us; the launch traced here: 204 us
  starting transfers between devices  124 us (60%)
  waiting for transfers between devices  64.1 us (31%)
  Pallas kernels  10.2 us (5%)
  local copies, waits for them, and re-layouts  2.32 us (1%)
    ppermute x28, starting transfers between devices, permute(): return lax.ppermute(value, AXES, pairs)  124 us
    ppermute x28, waiting for transfers between devices, permute(): return lax.ppermute(value, AXES, pairs)  64.1 us
    pallas_call x4, Pallas kernels, mix(): pl.pallas_call(functools.partial(mix_kernel, pieces=len(spikes) // 4, row...  8.09 us
  transfers between devices with their start and end apart: 28, of which 14 were waited for; matrix products, arithmetic and copies ran while one was open for 1% of the time, Pallas kernels for 2%

profile of v6, /device:TPU:69, one launch (start us, length us, event | category | flops | bytes accessed | tf_op | source)
XLA Modules:
  0.0 204.3 jit_solution(11719542127766646839)
XLA Ops:
  0.6 1.5 copy.16
  2.3 2.6 %collective-permute-start.7 = (bf16[4,256,256]{2,1,0:T(8,128)(2,1)S(1)}, bf16[4,256,256]{2,1,0:T(8,128)(2,1)S(1)}, u32[]{:S(2)}, u32[]{:S(2)}) collective-permute-start(bf16[4,256,256]{2,1,0:T(8,128)(2,1)S(1)} %get-tuple-element.41), channel_id=1, source_target_pairs={{0,1},{1,0},{2,3},{3,2},{4,5},{5,4},{6,7},{7,6},{8,9},{9,8},{10,11... | collective-permute-start | bytes 1572872 | tf_op jit(solution)/shard_map/ppermute | solution.py:27
  6.5 18.9 %collective-permute-start.1 = (bf16[1,136,256]{2,1,0:T(8,128)(2,1)S(1)}, bf16[1,136,256]{2,1,0:T(8,128)(2,1)S(1)}, u32[]{:S(2)}, u32[]{:S(2)}) collective-permute-start(bf16[1,136,256]{2,1,0:T(8,128)(2,1)S(1)} %bitcast.39), channel_id=1, source_target_pairs={{0,32},{1,33},{2,34},{3,35},{4,36},{5,37},{6,38},{7,39},{8,40},{9,... | collective-permute-start | bytes 208904 | tf_op jit(solution)/shard_map/ppermute | solution.py:27
  25.5 2.2 %collective-permute-start.10 = (bf16[4,256,512]{2,1,0:T(8,128)(2,1)S(1)}, bf16[4,256,512]{2,1,0:T(8,128)(2,1)S(1)}, u32[]{:S(2)}, u32[]{:S(2)}) collective-permute-start(bf16[4,256,512]{2,1,0:T(8,128)(2,1)S(1)} %pad_maximum_fusion.refs_4_), channel_id=1, source_target_pairs={{0,192},{1,193},{2,194},{3,195},{4,196},{5,197},{6,198},{7,199},{8... | collective-permute-start | bytes 3145736 | tf_op jit(solution)/shard_map/ppermute | solution.py:27
  27.8 0.7 pad_maximum_fusion.3
  28.4 8.8 %collective-permute-start.2 = (bf16[2,136,256]{2,1,0:T(8,128)(2,1)}, bf16[2,136,256]{2,1,0:T(8,128)(2,1)}, u32[]{:S(2)}, u32[]{:S(2)}) collective-permute-start(bf16[2,136,256]{2,1,0:T(8,128)(2,1)} %pad_maximum_fusion.3), channel_id=1, source_target_pairs={{0,16},{1,17},{2,18},{3,19},{4,20},{5,21},{6,22},{7,23},{8,24},{9,... | collective-permute-start | bytes 417800 | tf_op jit(solution)/shard_map/ppermute | solution.py:27
  37.2 2.8 %collective-permute-start.8 = (bf16[4,256,512]{2,1,0:T(8,128)(2,1)S(1)}, bf16[4,256,512]{2,1,0:T(8,128)(2,1)S(1)}, u32[]{:S(2)}, u32[]{:S(2)}) collective-permute-start(bf16[4,256,512]{2,1,0:T(8,128)(2,1)S(1)} %pad_maximum_fusion.refs_4_), channel_id=1, source_target_pairs={{0,64},{1,65},{2,66},{3,67},{4,68},{5,69},{6,70},{7,71},{8,72},{9,... | collective-permute-start | bytes 3145736 | tf_op jit(solution)/shard_map/ppermute | solution.py:27
  40.0 2.4 %collective-permute-start.9 = (bf16[4,256,512]{2,1,0:T(8,128)(2,1)S(1)}, bf16[4,256,512]{2,1,0:T(8,128)(2,1)}, u32[]{:S(2)}, u32[]{:S(2)}) collective-permute-start(bf16[4,256,512]{2,1,0:T(8,128)(2,1)S(1)} %pad_maximum_fusion.refs_4_), channel_id=1, source_target_pairs={{0,128},{1,129},{2,130},{3,131},{4,132},{5,133},{6,134},{7,135},{8... | collective-permute-start | bytes 3145736 | tf_op jit(solution)/shard_map/ppermute | solution.py:27
  42.8 1.0 pad_maximum_fusion.1.refs_0_
  43.8 4.6 %collective-permute-start.12 = (bf16[4,136,256]{2,1,0:T(8,128)(2,1)S(1)}, bf16[4,136,256]{2,1,0:T(8,128)(2,1)S(1)}, u32[]{:S(2)}, u32[]{:S(2)}) collective-permute-start(bf16[4,136,256]{2,1,0:T(8,128)(2,1)S(1)} %pad_maximum_fusion.1.refs_0_), channel_id=1, source_target_pairs={{0,6},{1,7},{2,4},{3,5},{4,2},{5,3},{6,0},{7,1},{8,14},{9,15},{10,... | collective-permute-start | bytes 835592 | tf_op jit(solution)/shard_map/ppermute | solution.py:27
  48.4 1.9 collective-permute-start.11
  50.4 3.6 %collective-permute-done.12.refs_3_ = bf16[4,136,256]{2,1,0:T(8,128)(2,1)S(1)} collective-permute-done((bf16[4,136,256]{2,1,0:T(8,128)(2,1)S(1)}, bf16[4,136,256]{2,1,0:T(8,128)(2,1)S(1)}, u32[]{:S(2)}, u32[]{:S(2)}) %collective-permute-start.12) | collective-permute-done | bytes 278560 | tf_op jit(solution)/shard_map/ppermute | solution.py:27
  53.9 1.9 collective-permute-start.3
  55.9 1.1 collective-permute-done.11.refs_1_
  57.0 2.1 %collective-permute-start.13 = (bf16[4,136,256]{2,1,0:T(8,128)(2,1)S(1)}, bf16[4,136,256]{2,1,0:T(8,128)(2,1)S(1)}, u32[]{:S(2)}, u32[]{:S(2)}) collective-permute-start(bf16[4,136,256]{2,1,0:T(8,128)(2,1)S(1)} %collective-permute-done.12.refs_3_), channel_id=1, source_target_pairs={{0,2},{1,3},{2,0},{3,1},{4,6},{5,7},{6,4},{7,5},{8,10},{9,11},{10,... | collective-permute-start | bytes 835592 | tf_op jit(solution)/shard_map/ppermute | solution.py:27
  59.0 2.9 %collective-permute-done.3.refs_0_ = bf16[4,136,256]{2,1,0:T(8,128)(2,1)S(1)} collective-permute-done((bf16[4,136,256]{2,1,0:T(8,128)(2,1)S(1)}, bf16[4,136,256]{2,1,0:T(8,128)(2,1)S(1)}, u32[]{:S(2)}, u32[]{:S(2)}) %collective-permute-start.3) | collective-permute-done | bytes 278560 | tf_op jit(solution)/shard_map/ppermute | solution.py:27
  61.9 1.9 collective-permute-start.4
  63.8 0.8 collective-permute-done.13.refs_2_
  64.6 4.9 %collective-permute-start.5 = (bf16[4,136,256]{2,1,0:T(8,128)(2,1)S(1)}, bf16[4,136,256]{2,1,0:T(8,128)(2,1)S(1)}, u32[]{:S(2)}, u32[]{:S(2)}) collective-permute-start(bf16[4,136,256]{2,1,0:T(8,128)(2,1)S(1)} %collective-permute-done.3.refs_0_), channel_id=1, source_target_pairs={{0,4},{1,5},{2,6},{3,7},{4,0},{5,1},{6,2},{7,3},{8,12},{9,13},{10,... | collective-permute-start | bytes 835592 | tf_op jit(solution)/shard_map/ppermute | solution.py:27
  69.5 2.0 collective-permute-start.6
  71.6 14.1 %collective-permute-done.9.refs_6_ = bf16[4,256,512]{2,1,0:T(8,128)(2,1)} collective-permute-done((bf16[4,256,512]{2,1,0:T(8,128)(2,1)S(1)}, bf16[4,256,512]{2,1,0:T(8,128)(2,1)}, u32[]{:S(2)}, u32[]{:S(2)}) %collective-permute-start.9) | collective-permute-done | bytes 1048608 | tf_op jit(solution)/shard_map/ppermute | solution.py:27
  85.6 2.0 mix_early.2
  87.7 2.1 %mix_late.2 = (f32[2,136,256]{2,1,0:T(8,128)S(1)}, f32[2,136,256]{2,1,0:T(8,128)S(1)}) custom-call(s32[3]{0:T(128)S(1)} %pad_add_fusion.at_ref, bf16[4,136,256]{2,1,0:T(8,128)(2,1)S(1)} %collective-permute-done.3.refs_0_, bf16[4,136,256]{2,1,0:T(8,128)(2,1)S(1)} %collective-permute-done.4.refs_1_, bf16[4,136,256]{2,1,0:T(8,128)(2,1)S(1)} %collective-permute-done.5.refs_2_, ...), custom_call_target="tpu_custom_call" | custom-call | flops 570425344 | bytes 3768320 | tf_op jit(solution)/shard_map/mix_late/pallas_call | solution.py:231
  89.8 3.5 %collective-permute-start.14 = (f32[2,136,256]{2,1,0:T(8,128)S(1)}, f32[2,136,256]{2,1,0:T(8,128)S(1)}, u32[]{:S(2)}, u32[]{:S(2)}) collective-permute-start(f32[2,136,256]{2,1,0:T(8,128)S(1)} %get-tuple-element.26), channel_id=1, source_target_pairs={{0,1},{1,0},{2,3},{3,2},{4,5},{5,4},{6,7},{7,6},{8,9},{9,8},{10,11... | collective-permute-start | bytes 835592 | tf_op jit(solution)/shard_map/ppermute | solution.py:27
  93.4 1.2 collective-permute-done.14.theirs_ref
  94.6 5.8 %collective-permute-start.15 = (bf16[136,256]{1,0:T(8,128)(2,1)S(1)}, bf16[136,256]{1,0:T(8,128)(2,1)S(1)}, u32[]{:S(2)}, u32[]{:S(2)}) collective-permute-start(bf16[136,256]{1,0:T(8,128)(2,1)S(1)} %get-tuple-element.28), channel_id=1, source_target_pairs={{0,256},{1,257},{2,258},{3,259},{4,260},{5,261},{6,262},{7,263},{8... | collective-permute-start | bytes 208904 | tf_op jit(solution)/shard_map/ppermute | solution.py:27
  100.4 9.7 %collective-permute-done.15.refs_1_ = bf16[136,256]{1,0:T(8,128)(2,1)S(1)} collective-permute-done((bf16[136,256]{1,0:T(8,128)(2,1)S(1)}, bf16[136,256]{1,0:T(8,128)(2,1)S(1)}, u32[]{:S(2)}, u32[]{:S(2)}) %collective-permute-start.15) | collective-permute-done | bytes 69664 | tf_op jit(solution)/shard_map/ppermute | solution.py:27
  110.2 0.9 update.2
  111.8 13.4 %collective-permute-start.17 = (bf16[1,136,256]{2,1,0:T(8,128)(2,1)S(1)}, bf16[1,136,256]{2,1,0:T(8,128)(2,1)S(1)}, u32[]{:S(2)}, u32[]{:S(2)}) collective-permute-start(bf16[1,136,256]{2,1,0:T(8,128)(2,1)S(1)} %bitcast.42), channel_id=1, source_target_pairs={{0,32},{1,33},{2,34},{3,35},{4,36},{5,37},{6,38},{7,39},{8,40},{9,... | collective-permute-start | bytes 208904 | tf_op jit(solution)/shard_map/ppermute | solution.py:27
  125.2 1.9 collective-permute-done.17
  127.1 1.9 collective-permute-start.18
  129.0 4.8 %collective-permute-done.18 = bf16[2,136,256]{2,1,0:T(8,128)(2,1)S(1)} collective-permute-done((bf16[2,136,256]{2,1,0:T(8,128)(2,1)S(1)}, bf16[2,136,256]{2,1,0:T(8,128)(2,1)S(1)}, u32[]{:S(2)}, u32[]{:S(2)}) %collective-permute-start.18) | collective-permute-done | bytes 139296 | tf_op jit(solution)/shard_map/ppermute | solution.py:27
  133.8 7.8 %collective-permute-start.24 = (bf16[4,136,256]{2,1,0:T(8,128)(2,1)S(1)}, bf16[4,136,256]{2,1,0:T(8,128)(2,1)S(1)}, u32[]{:S(2)}, u32[]{:S(2)}) collective-permute-start(bf16[4,136,256]{2,1,0:T(8,128)(2,1)S(1)} %pad_maximum_fusion.2.refs_0_), channel_id=1, source_target_pairs={{0,6},{1,7},{2,4},{3,5},{4,2},{5,3},{6,0},{7,1},{8,14},{9,15},{10,... | collective-permute-start | bytes 835592 | tf_op jit(solution)/shard_map/ppermute | solution.py:27
  141.6 7.0 %collective-permute-start.19 = (bf16[4,136,256]{2,1,0:T(8,128)(2,1)S(1)}, bf16[4,136,256]{2,1,0:T(8,128)(2,1)S(1)}, u32[]{:S(2)}, u32[]{:S(2)}) collective-permute-start(bf16[4,136,256]{2,1,0:T(8,128)(2,1)S(1)} %pad_maximum_fusion.2.refs_0_), channel_id=1, source_target_pairs={{0,8},{1,9},{2,10},{3,11},{4,12},{5,13},{6,14},{7,15},{8,0},{9,1},... | collective-permute-start | bytes 835592 | tf_op jit(solution)/shard_map/ppermute | solution.py:27
  148.7 1.9 collective-permute-start.23
  150.6 3.4 %collective-permute-start.25 = (bf16[4,136,256]{2,1,0:T(8,128)(2,1)S(1)}, bf16[4,136,256]{2,1,0:T(8,128)(2,1)S(1)}, u32[]{:S(2)}, u32[]{:S(2)}) collective-permute-start(bf16[4,136,256]{2,1,0:T(8,128)(2,1)S(1)} %collective-permute-done.24.refs_3_), channel_id=1, source_target_pairs={{0,2},{1,3},{2,0},{3,1},{4,6},{5,7},{6,4},{7,5},{8,10},{9,11},{10,... | collective-permute-start | bytes 835592 | tf_op jit(solution)/shard_map/ppermute | solution.py:27
  154.3 1.9 collective-permute-start.20
  156.2 5.3 %collective-permute-start.21 = (bf16[4,136,256]{2,1,0:T(8,128)(2,1)S(1)}, bf16[4,136,256]{2,1,0:T(8,128)(2,1)S(1)}, u32[]{:S(2)}, u32[]{:S(2)}) collective-permute-start(bf16[4,136,256]{2,1,0:T(8,128)(2,1)S(1)} %collective-permute-done.19.refs_0_), channel_id=1, source_target_pairs={{0,4},{1,5},{2,6},{3,7},{4,0},{5,1},{6,2},{7,3},{8,12},{9,13},{10,... | collective-permute-start | bytes 835592 | tf_op jit(solution)/shard_map/ppermute | solution.py:27
  161.5 2.4 %collective-permute-start.22 = (bf16[4,136,256]{2,1,0:T(8,128)(2,1)S(1)}, bf16[4,136,256]{2,1,0:T(8,128)(2,1)S(1)}, u32[]{:S(2)}, u32[]{:S(2)}) collective-permute-start(bf16[4,136,256]{2,1,0:T(8,128)(2,1)S(1)} %collective-permute-done.19.refs_0_), channel_id=1, source_target_pairs={{0,6},{1,7},{2,4},{3,5},{4,2},{5,3},{6,0},{7,1},{8,14},{9,15},{10,... | collective-permute-start | bytes 835592 | tf_op jit(solution)/shard_map/ppermute | solution.py:27
  163.9 2.0 mix_early.3
  165.9 3.1 %collective-permute-done.20.refs_1_ = bf16[4,136,256]{2,1,0:T(8,128)(2,1)S(1)} collective-permute-done((bf16[4,136,256]{2,1,0:T(8,128)(2,1)S(1)}, bf16[4,136,256]{2,1,0:T(8,128)(2,1)S(1)}, u32[]{:S(2)}, u32[]{:S(2)}) %collective-permute-start.20) | collective-permute-done | bytes 278560 | tf_op jit(solution)/shard_map/ppermute | solution.py:27
  169.0 7.9 %collective-permute-done.21.refs_2_ = bf16[4,136,256]{2,1,0:T(8,128)(2,1)S(1)} collective-permute-done((bf16[4,136,256]{2,1,0:T(8,128)(2,1)S(1)}, bf16[4,136,256]{2,1,0:T(8,128)(2,1)S(1)}, u32[]{:S(2)}, u32[]{:S(2)}) %collective-permute-start.21) | collective-permute-done | bytes 278560 | tf_op jit(solution)/shard_map/ppermute | solution.py:27
  177.0 2.0 mix_late.3
  179.0 4.6 %collective-permute-start.26 = (f32[2,136,256]{2,1,0:T(8,128)S(1)}, f32[2,136,256]{2,1,0:T(8,128)S(1)}, u32[]{:S(2)}, u32[]{:S(2)}) collective-permute-start(f32[2,136,256]{2,1,0:T(8,128)S(1)} %get-tuple-element.34), channel_id=1, source_target_pairs={{0,1},{1,0},{2,3},{3,2},{4,5},{5,4},{6,7},{7,6},{8,9},{9,8},{10,11... | collective-permute-start | bytes 835592 | tf_op jit(solution)/shard_map/ppermute | solution.py:27
  183.5 1.2 collective-permute-done.26.theirs_ref
  184.8 7.2 %collective-permute-start.27 = (bf16[136,256]{1,0:T(8,128)(2,1)S(1)}, bf16[136,256]{1,0:T(8,128)(2,1)S(1)}, u32[]{:S(2)}, u32[]{:S(2)}) collective-permute-start(bf16[136,256]{1,0:T(8,128)(2,1)S(1)} %get-tuple-element.36), channel_id=1, source_target_pairs={{0,256},{1,257},{2,258},{3,259},{4,260},{5,261},{6,262},{7,263},{8... | collective-permute-start | bytes 208904 | tf_op jit(solution)/shard_map/ppermute | solution.py:27
  191.9 11.6 %collective-permute-done.27.refs_1_ = bf16[136,256]{1,0:T(8,128)(2,1)S(1)} collective-permute-done((bf16[136,256]{1,0:T(8,128)(2,1)S(1)}, bf16[136,256]{1,0:T(8,128)(2,1)S(1)}, u32[]{:S(2)}, u32[]{:S(2)}) %collective-permute-start.27) | collective-permute-done | bytes 69664 | tf_op jit(solution)/shard_map/ppermute | solution.py:27
  203.5 0.9 update.3
  (65 shorter events, 3.2 us)
Async XLA Ops:
  0.6 41.8 %copy-start = (bf16[700,256]{1,0:T(8,128)(2,1)S(1)}, bf16[700,256]{1,0:T(8,128)(2,1)}, u32[]{:S(2)}) copy-start(bf16[700,256]{1,0:T(8,128)(2,1)} %param.20) | copy-start | bytes 1075204
  2.2 2.7 %copy-start.1 = (bf16[64,4,256]{2,1,0:T(4,128)(2,1)S(1)}, bf16[64,4,256]{2,1,0:T(4,128)(2,1)}, u32[]{:S(2)}) copy-start(bf16[64,4,256]{2,1,0:T(4,128)(2,1)} %refs_9_.3) | copy-start | bytes 393220
  2.2 2.7 %copy-start.8 = (bf16[64,2,256]{2,1,0:T(2,128)(2,1)S(1)}, bf16[64,2,256]{2,1,0:T(2,128)(2,1)}, u32[]{:S(2)}) copy-start(bf16[64,2,256]{2,1,0:T(2,128)(2,1)} %spikes_ref.1) | copy-start | bytes 196612
  2.2 4.2 %copy-start.13 = (s32[2,2,700]{2,1,0:T(2,128)S(1)}, s32[2,2,700]{2,1,0:T(2,128)}, u32[]{:S(2)}) copy-start(s32[2,2,700]{2,1,0:T(2,128)} %param.21) | copy-start | bytes 33604
  2.3 23.1 %collective-permute-start.7 = (bf16[4,256,256]{2,1,0:T(8,128)(2,1)S(1)}, bf16[4,256,256]{2,1,0:T(8,128)(2,1)S(1)}, u32[]{:S(2)}, u32[]{:S(2)}) collective-permute-start(bf16[4,256,256]{2,1,0:T(8,128)(2,1)S(1)} %get-tuple-element.41), channel_id=1, source_target_pairs={{0,1},{1,0},{2,3},{3,2},{4,5},{5,4},{6,7},{7,6},{8,9},{9,8},{10,11... | collective-permute-start | bytes 1572872 | tf_op jit(solution)/shard_map/ppermute | solution.py:27
  5.2 1.3 collective-permute-start
  5.8 0.6 copy-start.4
  6.5 21.2 %copy-start.11 = (bf16[136,256]{1,0:T(8,128)(2,1)}, bf16[136,256]{1,0:T(8,128)(2,1)S(1)}, u32[]{:S(2)}) copy-start(bf16[136,256]{1,0:T(8,128)(2,1)S(1)} %collective-permute-done) | copy-start | bytes 208900
  6.5 21.2 %collective-permute-start.1 = (bf16[1,136,256]{2,1,0:T(8,128)(2,1)S(1)}, bf16[1,136,256]{2,1,0:T(8,128)(2,1)S(1)}, u32[]{:S(2)}, u32[]{:S(2)}) collective-permute-start(bf16[1,136,256]{2,1,0:T(8,128)(2,1)S(1)} %bitcast.39), channel_id=1, source_target_pairs={{0,32},{1,33},{2,34},{3,35},{4,36},{5,37},{6,38},{7,39},{8,40},{9,... | collective-permute-start | bytes 208904 | tf_op jit(solution)/shard_map/ppermute | solution.py:27
  25.4 17.2 %copy-start.14 = (f32[256]{0:T(256)S(1)}, f32[256]{0:T(256)}, u32[]{:S(2)}) copy-start(f32[256]{0:T(256)} %param.24) | copy-start | bytes 3076
  25.4 17.2 %copy-start.15 = (f32[256]{0:T(256)S(1)}, f32[256]{0:T(256)}, u32[]{:S(2)}) copy-start(f32[256]{0:T(256)} %param.25) | copy-start | bytes 3076
  25.4 17.2 %copy-start.16 = (f32[256]{0:T(256)S(1)}, f32[256]{0:T(256)}, u32[]{:S(2)}) copy-start(f32[256]{0:T(256)} %param.26) | copy-start | bytes 3076
  25.4 17.2 %copy-start.17 = (f32[256]{0:T(256)S(1)}, f32[256]{0:T(256)}, u32[]{:S(2)}) copy-start(f32[256]{0:T(256)} %param.27) | copy-start | bytes 3076
  25.5 43.9 %collective-permute-start.10 = (bf16[4,256,512]{2,1,0:T(8,128)(2,1)S(1)}, bf16[4,256,512]{2,1,0:T(8,128)(2,1)S(1)}, u32[]{:S(2)}, u32[]{:S(2)}) collective-permute-start(bf16[4,256,512]{2,1,0:T(8,128)(2,1)S(1)} %pad_maximum_fusion.refs_4_), channel_id=1, source_target_pairs={{0,192},{1,193},{2,194},{3,195},{4,196},{5,197},{6,198},{7,199},{8... | collective-permute-start | bytes 3145736 | tf_op jit(solution)/shard_map/ppermute | solution.py:27
  27.7 0.7 copy-start.12
  28.4 14.4 %collective-permute-start.2 = (bf16[2,136,256]{2,1,0:T(8,128)(2,1)}, bf16[2,136,256]{2,1,0:T(8,128)(2,1)}, u32[]{:S(2)}, u32[]{:S(2)}) collective-permute-start(bf16[2,136,256]{2,1,0:T(8,128)(2,1)} %pad_maximum_fusion.3), channel_id=1, source_target_pairs={{0,16},{1,17},{2,18},{3,19},{4,20},{5,21},{6,22},{7,23},{8,24},{9,... | collective-permute-start | bytes 417800 | tf_op jit(solution)/shard_map/ppermute | solution.py:27
  37.2 34.3 %collective-permute-start.8 = (bf16[4,256,512]{2,1,0:T(8,128)(2,1)S(1)}, bf16[4,256,512]{2,1,0:T(8,128)(2,1)S(1)}, u32[]{:S(2)}, u32[]{:S(2)}) collective-permute-start(bf16[4,256,512]{2,1,0:T(8,128)(2,1)S(1)} %pad_maximum_fusion.refs_4_), channel_id=1, source_target_pairs={{0,64},{1,65},{2,66},{3,67},{4,68},{5,69},{6,70},{7,71},{8,72},{9,... | collective-permute-start | bytes 3145736 | tf_op jit(solution)/shard_map/ppermute | solution.py:27
  40.0 45.6 %collective-permute-start.9 = (bf16[4,256,512]{2,1,0:T(8,128)(2,1)S(1)}, bf16[4,256,512]{2,1,0:T(8,128)(2,1)}, u32[]{:S(2)}, u32[]{:S(2)}) collective-permute-start(bf16[4,256,512]{2,1,0:T(8,128)(2,1)S(1)} %pad_maximum_fusion.refs_4_), channel_id=1, source_target_pairs={{0,128},{1,129},{2,130},{3,131},{4,132},{5,133},{6,134},{7,135},{8... | collective-permute-start | bytes 3145736 | tf_op jit(solution)/shard_map/ppermute | solution.py:27
  43.8 10.1 %collective-permute-start.12 = (bf16[4,136,256]{2,1,0:T(8,128)(2,1)S(1)}, bf16[4,136,256]{2,1,0:T(8,128)(2,1)S(1)}, u32[]{:S(2)}, u32[]{:S(2)}) collective-permute-start(bf16[4,136,256]{2,1,0:T(8,128)(2,1)S(1)} %pad_maximum_fusion.1.refs_0_), channel_id=1, source_target_pairs={{0,6},{1,7},{2,4},{3,5},{4,2},{5,3},{6,0},{7,1},{8,14},{9,15},{10,... | collective-permute-start | bytes 835592 | tf_op jit(solution)/shard_map/ppermute | solution.py:27
  48.4 8.5 %collective-permute-start.11 = (bf16[4,136,256]{2,1,0:T(8,128)(2,1)S(1)}, bf16[4,136,256]{2,1,0:T(8,128)(2,1)S(1)}, u32[]{:S(2)}, u32[]{:S(2)}) collective-permute-start(bf16[4,136,256]{2,1,0:T(8,128)(2,1)S(1)} %pad_maximum_fusion.1.refs_0_), channel_id=1, source_target_pairs={{0,2},{1,3},{2,0},{3,1},{4,6},{5,7},{6,4},{7,5},{8,10},{9,11},{10,... | collective-permute-start | bytes 835592 | tf_op jit(solution)/shard_map/ppermute | solution.py:27
  53.9 8.0 %collective-permute-start.3 = (bf16[4,136,256]{2,1,0:T(8,128)(2,1)S(1)}, bf16[4,136,256]{2,1,0:T(8,128)(2,1)S(1)}, u32[]{:S(2)}, u32[]{:S(2)}) collective-permute-start(bf16[4,136,256]{2,1,0:T(8,128)(2,1)S(1)} %pad_maximum_fusion.1.refs_0_), channel_id=1, source_target_pairs={{0,8},{1,9},{2,10},{3,11},{4,12},{5,13},{6,14},{7,15},{8,0},{9,1},... | collective-permute-start | bytes 835592 | tf_op jit(solution)/shard_map/ppermute | solution.py:27
  57.0 7.7 %collective-permute-start.13 = (bf16[4,136,256]{2,1,0:T(8,128)(2,1)S(1)}, bf16[4,136,256]{2,1,0:T(8,128)(2,1)S(1)}, u32[]{:S(2)}, u32[]{:S(2)}) collective-permute-start(bf16[4,136,256]{2,1,0:T(8,128)(2,1)S(1)} %collective-permute-done.12.refs_3_), channel_id=1, source_target_pairs={{0,2},{1,3},{2,0},{3,1},{4,6},{5,7},{6,4},{7,5},{8,10},{9,11},{10,... | collective-permute-start | bytes 835592 | tf_op jit(solution)/shard_map/ppermute | solution.py:27
  61.9 25.7 %collective-permute-start.4 = (bf16[4,136,256]{2,1,0:T(8,128)(2,1)S(1)}, bf16[4,136,256]{2,1,0:T(8,128)(2,1)S(1)}, u32[]{:S(2)}, u32[]{:S(2)}) collective-permute-start(bf16[4,136,256]{2,1,0:T(8,128)(2,1)S(1)} %collective-permute-done.3.refs_0_), channel_id=1, source_target_pairs={{0,2},{1,3},{2,0},{3,1},{4,6},{5,7},{6,4},{7,5},{8,10},{9,11},{10,... | collective-permute-start | bytes 835592 | tf_op jit(solution)/shard_map/ppermute | solution.py:27
  64.6 23.0 %collective-permute-start.5 = (bf16[4,136,256]{2,1,0:T(8,128)(2,1)S(1)}, bf16[4,136,256]{2,1,0:T(8,128)(2,1)S(1)}, u32[]{:S(2)}, u32[]{:S(2)}) collective-permute-start(bf16[4,136,256]{2,1,0:T(8,128)(2,1)S(1)} %collective-permute-done.3.refs_0_), channel_id=1, source_target_pairs={{0,4},{1,5},{2,6},{3,7},{4,0},{5,1},{6,2},{7,3},{8,12},{9,13},{10,... | collective-permute-start | bytes 835592 | tf_op jit(solution)/shard_map/ppermute | solution.py:27
  69.5 18.1 %collective-permute-start.6 = (bf16[4,136,256]{2,1,0:T(8,128)(2,1)S(1)}, bf16[4,136,256]{2,1,0:T(8,128)(2,1)S(1)}, u32[]{:S(2)}, u32[]{:S(2)}) collective-permute-start(bf16[4,136,256]{2,1,0:T(8,128)(2,1)S(1)} %collective-permute-done.3.refs_0_), channel_id=1, source_target_pairs={{0,6},{1,7},{2,4},{3,5},{4,2},{5,3},{6,0},{7,1},{8,14},{9,15},{10,... | collective-permute-start | bytes 835592 | tf_op jit(solution)/shard_map/ppermute | solution.py:27
  87.6 22.5 %copy-start.2 = (bf16[64,4,256]{2,1,0:T(4,128)(2,1)S(1)}, bf16[64,4,256]{2,1,0:T(4,128)(2,1)}, u32[]{:S(2)}) copy-start(bf16[64,4,256]{2,1,0:T(4,128)(2,1)} %refs_9_.3) | copy-start | bytes 393220
  87.6 22.5 %copy-start.3 = (bf16[64,4,256]{2,1,0:T(4,128)(2,1)S(1)}, bf16[64,4,256]{2,1,0:T(4,128)(2,1)}, u32[]{:S(2)}) copy-start(bf16[64,4,256]{2,1,0:T(4,128)(2,1)} %refs_8_.3) | copy-start | bytes 393220
  87.7 22.5 %copy-start.5 = (bf16[136,256]{1,0:T(8,128)(2,1)S(1)}, bf16[136,256]{1,0:T(8,128)(2,1)}, u32[]{:S(2)}) copy-start(bf16[136,256]{1,0:T(8,128)(2,1)} %copy-done.4) | copy-start | bytes 208900
  87.7 22.5 %copy-start.6 = (f32[64,2,256]{2,1,0:T(2,128)S(1)}, f32[64,2,256]{2,1,0:T(2,128)}, u32[]{:S(2)}) copy-start(f32[64,2,256]{2,1,0:T(2,128)} %refs_3_.1) | copy-start | bytes 393220
  87.7 22.5 %copy-start.7 = (f32[64,2,256]{2,1,0:T(2,128)S(1)}, f32[64,2,256]{2,1,0:T(2,128)}, u32[]{:S(2)}) copy-start(f32[64,2,256]{2,1,0:T(2,128)} %refs_4_.1) | copy-start | bytes 393220
  87.7 22.5 %copy-start.9 = (s32[64,2]{0,1:T(2,128)S(1)}, s32[64,2]{0,1:T(2,128)}, u32[]{:S(2)}) copy-start(s32[64,2]{0,1:T(2,128)} %param.22) | copy-start | bytes 1540
  87.7 22.5 %copy-start.10 = (s32[64]{0:T(128)S(1)}, s32[64]{0:T(128)}, u32[]{:S(2)}) copy-start(s32[64]{0:T(128)} %param.23) | copy-start | bytes 772
  89.8 4.7 %collective-permute-start.14 = (f32[2,136,256]{2,1,0:T(8,128)S(1)}, f32[2,136,256]{2,1,0:T(8,128)S(1)}, u32[]{:S(2)}, u32[]{:S(2)}) collective-permute-start(f32[2,136,256]{2,1,0:T(8,128)S(1)} %get-tuple-element.26), channel_id=1, source_target_pairs={{0,1},{1,0},{2,3},{3,2},{4,5},{5,4},{6,7},{7,6},{8,9},{9,8},{10,11... | collective-permute-start | bytes 835592 | tf_op jit(solution)/shard_map/ppermute | solution.py:27
  94.6 15.6 %collective-permute-start.15 = (bf16[136,256]{1,0:T(8,128)(2,1)S(1)}, bf16[136,256]{1,0:T(8,128)(2,1)S(1)}, u32[]{:S(2)}, u32[]{:S(2)}) collective-permute-start(bf16[136,256]{1,0:T(8,128)(2,1)S(1)} %get-tuple-element.28), channel_id=1, source_target_pairs={{0,256},{1,257},{2,258},{3,259},{4,260},{5,261},{6,262},{7,263},{8... | collective-permute-start | bytes 208904 | tf_op jit(solution)/shard_map/ppermute | solution.py:27
  111.1 0.7 collective-permute-start.16
  111.8 15.3 %collective-permute-start.17 = (bf16[1,136,256]{2,1,0:T(8,128)(2,1)S(1)}, bf16[1,136,256]{2,1,0:T(8,128)(2,1)S(1)}, u32[]{:S(2)}, u32[]{:S(2)}) collective-permute-start(bf16[1,136,256]{2,1,0:T(8,128)(2,1)S(1)} %bitcast.42), channel_id=1, source_target_pairs={{0,32},{1,33},{2,34},{3,35},{4,36},{5,37},{6,38},{7,39},{8,40},{9,... | collective-permute-start | bytes 208904 | tf_op jit(solution)/shard_map/ppermute | solution.py:27
  127.1 6.7 %collective-permute-start.18 = (bf16[2,136,256]{2,1,0:T(8,128)(2,1)S(1)}, bf16[2,136,256]{2,1,0:T(8,128)(2,1)S(1)}, u32[]{:S(2)}, u32[]{:S(2)}) collective-permute-start(bf16[2,136,256]{2,1,0:T(8,128)(2,1)S(1)} %pad_maximum_fusion.4), channel_id=1, source_target_pairs={{0,16},{1,17},{2,18},{3,19},{4,20},{5,21},{6,22},{7,23},{8,24},{9,... | collective-permute-start | bytes 417800 | tf_op jit(solution)/shard_map/ppermute | solution.py:27
  133.8 16.8 %collective-permute-start.24 = (bf16[4,136,256]{2,1,0:T(8,128)(2,1)S(1)}, bf16[4,136,256]{2,1,0:T(8,128)(2,1)S(1)}, u32[]{:S(2)}, u32[]{:S(2)}) collective-permute-start(bf16[4,136,256]{2,1,0:T(8,128)(2,1)S(1)} %pad_maximum_fusion.2.refs_0_), channel_id=1, source_target_pairs={{0,6},{1,7},{2,4},{3,5},{4,2},{5,3},{6,0},{7,1},{8,14},{9,15},{10,... | collective-permute-start | bytes 835592 | tf_op jit(solution)/shard_map/ppermute | solution.py:27
  141.6 12.7 %collective-permute-start.19 = (bf16[4,136,256]{2,1,0:T(8,128)(2,1)S(1)}, bf16[4,136,256]{2,1,0:T(8,128)(2,1)S(1)}, u32[]{:S(2)}, u32[]{:S(2)}) collective-permute-start(bf16[4,136,256]{2,1,0:T(8,128)(2,1)S(1)} %pad_maximum_fusion.2.refs_0_), channel_id=1, source_target_pairs={{0,8},{1,9},{2,10},{3,11},{4,12},{5,13},{6,14},{7,15},{8,0},{9,1},... | collective-permute-start | bytes 835592 | tf_op jit(solution)/shard_map/ppermute | solution.py:27
  148.7 15.2 %collective-permute-start.23 = (bf16[4,136,256]{2,1,0:T(8,128)(2,1)S(1)}, bf16[4,136,256]{2,1,0:T(8,128)(2,1)S(1)}, u32[]{:S(2)}, u32[]{:S(2)}) collective-permute-start(bf16[4,136,256]{2,1,0:T(8,128)(2,1)S(1)} %pad_maximum_fusion.2.refs_0_), channel_id=1, source_target_pairs={{0,2},{1,3},{2,0},{3,1},{4,6},{5,7},{6,4},{7,5},{8,10},{9,11},{10,... | collective-permute-start | bytes 835592 | tf_op jit(solution)/shard_map/ppermute | solution.py:27
  150.6 13.3 %collective-permute-start.25 = (bf16[4,136,256]{2,1,0:T(8,128)(2,1)S(1)}, bf16[4,136,256]{2,1,0:T(8,128)(2,1)S(1)}, u32[]{:S(2)}, u32[]{:S(2)}) collective-permute-start(bf16[4,136,256]{2,1,0:T(8,128)(2,1)S(1)} %collective-permute-done.24.refs_3_), channel_id=1, source_target_pairs={{0,2},{1,3},{2,0},{3,1},{4,6},{5,7},{6,4},{7,5},{8,10},{9,11},{10,... | collective-permute-start | bytes 835592 | tf_op jit(solution)/shard_map/ppermute | solution.py:27
  154.3 14.7 %collective-permute-start.20 = (bf16[4,136,256]{2,1,0:T(8,128)(2,1)S(1)}, bf16[4,136,256]{2,1,0:T(8,128)(2,1)S(1)}, u32[]{:S(2)}, u32[]{:S(2)}) collective-permute-start(bf16[4,136,256]{2,1,0:T(8,128)(2,1)S(1)} %collective-permute-done.19.refs_0_), channel_id=1, source_target_pairs={{0,2},{1,3},{2,0},{3,1},{4,6},{5,7},{6,4},{7,5},{8,10},{9,11},{10,... | collective-permute-start | bytes 835592 | tf_op jit(solution)/shard_map/ppermute | solution.py:27
  156.2 20.7 %collective-permute-start.21 = (bf16[4,136,256]{2,1,0:T(8,128)(2,1)S(1)}, bf16[4,136,256]{2,1,0:T(8,128)(2,1)S(1)}, u32[]{:S(2)}, u32[]{:S(2)}) collective-permute-start(bf16[4,136,256]{2,1,0:T(8,128)(2,1)S(1)} %collective-permute-done.19.refs_0_), channel_id=1, source_target_pairs={{0,4},{1,5},{2,6},{3,7},{4,0},{5,1},{6,2},{7,3},{8,12},{9,13},{10,... | collective-permute-start | bytes 835592 | tf_op jit(solution)/shard_map/ppermute | solution.py:27
  161.5 15.5 %collective-permute-start.22 = (bf16[4,136,256]{2,1,0:T(8,128)(2,1)S(1)}, bf16[4,136,256]{2,1,0:T(8,128)(2,1)S(1)}, u32[]{:S(2)}, u32[]{:S(2)}) collective-permute-start(bf16[4,136,256]{2,1,0:T(8,128)(2,1)S(1)} %collective-permute-done.19.refs_0_), channel_id=1, source_target_pairs={{0,6},{1,7},{2,4},{3,5},{4,2},{5,3},{6,0},{7,1},{8,14},{9,15},{10,... | collective-permute-start | bytes 835592 | tf_op jit(solution)/shard_map/ppermute | solution.py:27
  179.0 5.7 %collective-permute-start.26 = (f32[2,136,256]{2,1,0:T(8,128)S(1)}, f32[2,136,256]{2,1,0:T(8,128)S(1)}, u32[]{:S(2)}, u32[]{:S(2)}) collective-permute-start(f32[2,136,256]{2,1,0:T(8,128)S(1)} %get-tuple-element.34), channel_id=1, source_target_pairs={{0,1},{1,0},{2,3},{3,2},{4,5},{5,4},{6,7},{7,6},{8,9},{9,8},{10,11... | collective-permute-start | bytes 835592 | tf_op jit(solution)/shard_map/ppermute | solution.py:27
  184.8 18.7 %collective-permute-start.27 = (bf16[136,256]{1,0:T(8,128)(2,1)S(1)}, bf16[136,256]{1,0:T(8,128)(2,1)S(1)}, u32[]{:S(2)}, u32[]{:S(2)}) collective-permute-start(bf16[136,256]{1,0:T(8,128)(2,1)S(1)} %get-tuple-element.36), channel_id=1, source_target_pairs={{0,256},{1,257},{2,258},{3,259},{4,260},{5,261},{6,262},{7,263},{8... | collective-permute-start | bytes 208904 | tf_op jit(solution)/shard_map/ppermute | solution.py:27
